TPU v7x, 256 devices: a whole 4x4x8 slice. The times are simulated.
256 devices in a mesh: member: 2 (over core), tile: 128 (over x, z, y).
Axes of the slice: x: 4, y: 4, z: 8, core: 2. Of those that a mesh axis runs over, the one named last changes fastest.
Arguments:
- parent_state: float32 [4, 81, 1024, 128], P('member', None, 'tile'), may hold values from -6 to 6
- nest_state: float32 [4, 81, 32768], P('member', None, 'tile'), may hold values from -6 to 6
- terrain: int32 [1024, 128], P('tile'), may hold values from 0 to 3000
- shift_x: int32 [4], replicated, may hold values from -16 to 16
- boundary_index: int32 [4, 16384], P(None, 'tile'), may hold values from 0 to 131071, as said below
- reloc_dest: int32 [4, 32768], P(None, 'tile'), may hold values from 0 to 32767, as said below
Outputs:
- parent_out: float32 [4, 81, 1024, 128], P('member', None, 'tile')
- nest_out: float32 [4, 81, 32768], P('member', None, 'tile')
- nest_mean: float32 [81, 32768], P(None, 'tile')
- nest_variance: float32 [81, 32768], P(None, 'tile')
Inputs may be any that keep to these rules, and one draw needn't show every extreme that they name: `boundary_index`: for each step and nest tile t, entries t * 128 to t * 128 + 127 come in 64 runs of 2; each run lies on one parent tile (rows of 8), different runs of one tile on different parent tiles, and the cells within one run differ. `reloc_dest`: for each step a permutation of the 32768 nest columns. The columns of one tile go in runs of 4 (slots g * 4 to g * 4 + 3) each wholly to one tile, into that tile's run g; the runs of one tile go to 64 different tiles, so exactly 4 or no columns pass from one tile to another.
All inputs are finite; a program needn't handle non-finite values.
Results may differ from a plain program's by a relative error of at most 0.00047.
Values may be sent and summed in bfloat16 or wider, within the bound.
No kernel may reach another device: no remote copies, remote signals or barrier semaphores. Data moves between devices by JAX's collectives and lax.ppermute only.
A program may use at most 64 MiB of HBM per device.

v0:
```python
import functools

import jax
import jax.numpy as jnp
import numpy as np
from jax import lax
from jax.experimental import pallas as pl
from jax.experimental.pallas import tpu as pltpu
from jax.sharding import PartitionSpec as P

F32 = jnp.float32
BF16 = jnp.bfloat16
LEV = 81
STEPS = 4
NT = 128
ROWS = 8
W = 128
LPAD = 96
RING = 16
BSTR = LPAD * RING
L_DEST = 81
L_REQ = 88
HORIZ = 0.15
VERT = 0.1
DRAG = 0.1
RELAX = 0.5
IMPL = 0.8
VMEM_LIMIT = 48 * 1024 * 1024


def solve_matrix():
    n = np.full(LEV, 2.0)
    n[0] = n[-1] = 1.0
    a = np.diag(1.0 + IMPL * n)
    a -= IMPL * (np.eye(LEV, k=1) + np.eye(LEV, k=-1))
    return np.linalg.inv(a)


def padded_transpose(m):
    out = np.zeros((W, W))
    out[:LEV, :LEV] = m.T
    return out


def split3(m):
    m = np.asarray(m, np.float64)
    parts = []
    for _ in range(3):
        part = m.astype(jnp.bfloat16)
        parts.append(part)
        m = m - part.astype(np.float64)
    return parts


def constants():
    s = solve_matrix()
    power = [np.linalg.matrix_power(s, k) for k in range(STEPS + 1)]
    keep = 1.0 - RELAX
    interior = padded_transpose(power[STEPS])
    bound = padded_transpose(power[STEPS] * keep**STEPS)
    q_mix = np.stack([bound, interior]).astype(np.float32)
    stack = np.concatenate(
        [
            padded_transpose(power[STEPS - k] * RELAX * keep ** (STEPS - 1 - k))
            for k in range(STEPS)
        ]
    )
    e_mix = np.concatenate(split3(stack), axis=1)
    return q_mix, e_mix


def call(body, out_shape, in_specs=None, scratch=(), name=None, flops=0, nbytes=0):
    kwargs = {} if in_specs is None else {"in_specs": in_specs}
    return pl.pallas_call(
        body,
        out_shape=out_shape,
        scratch_shapes=list(scratch),
        compiler_params=pltpu.CompilerParams(vmem_limit_bytes=VMEM_LIMIT),
        cost_estimate=pl.CostEstimate(
            flops=flops, bytes_accessed=nbytes, transcendentals=0
        ),
        name=name,
        **kwargs,
    )


VM = pl.BlockSpec(memory_space=pltpu.VMEM)
SM = pl.BlockSpec(memory_space=pltpu.SMEM)


def send_kernel(shift_ref, nest_ref, bidx_ref, dest_ref, msg_ref, pad_ref):
    zeros = jnp.zeros((W - LEV + 1, 2 * W), F32)
    for b in range(2):
        pad_ref[b, LEV - 1 :, :] = zeros
        pad_ref[b, :LEV, :] = nest_ref[b]
        pad_ref[b, L_DEST : L_DEST + STEPS, :] = dest_ref[...].astype(F32)
        for half in range(2):
            block = pad_ref[b, :, half * W : (half + 1) * W]
            start = b * 2 * W + half * W
            msg_ref[start : start + W, :] = block.T
    lane = lax.broadcasted_iota(jnp.int32, (NT, W), 1)
    tile = lax.broadcasted_iota(jnp.int32, (NT, W), 0)
    for s in range(STEPS):
        idx = bidx_ref[s : s + 1, :]
        owner = jnp.right_shift(idx, 10)
        row = jnp.bitwise_and(jnp.right_shift(idx, 7), ROWS - 1)
        col = jnp.bitwise_and(jnp.bitwise_and(idx, W - 1) + shift_ref[s], W - 1)
        cell = (row * W + col + 1).astype(F32)
        mine = tile == owner
        picked = jnp.where(mine, jnp.broadcast_to(cell, (NT, W)), 0.0)
        even = jnp.bitwise_and(lane, 1) == 0
        first = jnp.sum(jnp.where(even, picked, 0.0), axis=1, keepdims=True) - 1.0
        second = jnp.sum(jnp.where(even, 0.0, picked), axis=1, keepdims=True) - 1.0
        rows = msg_ref[pl.ds(s, NT, stride=4), :]
        rows = jnp.where(lane == L_REQ, first, rows)
        rows = jnp.where(lane == L_REQ + 1, second, rows)
        msg_ref[pl.ds(s, NT, stride=4), :] = rows


def halo_kernel(parent_ref, terrain_ref, down_ref, up_ref):
    damping = DRAG * terrain_ref[...].astype(F32) / 3000.0
    down_ref[: 2 * LEV, :, :] = parent_ref[:, 4:, :]
    up_ref[: 2 * LEV, :, :] = parent_ref[:, :4, :]
    down_ref[2 * LEV, :, :] = damping[4:, :]
    up_ref[2 * LEV, :, :] = damping[:4, :]


def ring_step(read, write, level_stride, coef, own_only=False):
    row = lax.broadcasted_iota(jnp.int32, (ROWS, W), 0)
    last = row == ROWS - 1
    head = row == 0
    c0, c1, h1, v1 = coef
    chunk = 9

    def body(step, carry):
        for member in range(2):
            for k in range(chunk):
                level = step * chunk + k
                base = member * level_stride
                below = base + jnp.maximum(level - 1, 0)
                above = base + jnp.minimum(level + 1, LEV - 1)
                x0, x1 = read(base + level)
                d0, d1 = read(below)
                u0, u1 = read(above)
                f0 = pltpu.roll(x0, ROWS - 1, 0)
                f1 = pltpu.roll(x1, ROWS - 1, 0)
                g0 = pltpu.roll(x0, 1, 0)
                g1 = pltpu.roll(x1, 1, 0)
                near0 = jnp.where(last, f1, f0) + jnp.where(head, g1, g0)
                near0 = near0 + (pltpu.roll(x0, 1, 1) + pltpu.roll(x0, W - 1, 1))
                y0 = c0 * x0 + HORIZ * near0 + VERT * (d0 + u0)
                if own_only:
                    write(member, level, y0, None)
                    continue
                near1 = jnp.where(last, f0, f1) + jnp.where(head, g0, g1)
                near1 = near1 + (pltpu.roll(x1, 1, 1) + pltpu.roll(x1, W - 1, 1))
                y1 = c1 * x1 + h1 * near1 + v1 * (d1 + u1)
                write(member, level, y0, y1)
        return carry

    lax.fori_loop(0, LEV // chunk, body, 0)


def parent_kernel(
    tile_ref, parent_ref, next_ref, prev_ref, terrain_ref, cells_ref, ring_ref, a_ref, b_ref
):
    tile = tile_ref[0]
    damping = DRAG * terrain_ref[...].astype(F32) / 3000.0
    pads = jnp.zeros(((LPAD - LEV) * RING, W), F32)
    for ref in (a_ref, b_ref):
        for member in range(2):
            top = member * BSTR + LEV * RING
            ref[top : top + (LPAD - LEV) * RING, :] = pads
    for s in range(STEPS):
        for member in range(2):
            cells_ref[s, member * W + LPAD : (member + 1) * W, :] = jnp.zeros(
                (W - LPAD, ROWS * W), BF16
            )

    def fill(level, carry):
        for member in range(2):
            src = member * LEV + level
            base = pl.multiple_of(member * BSTR + level * RING, RING)
            a_ref[pl.ds(base, ROWS), :] = parent_ref[src]
            a_ref[pl.ds(base + 8, 4), :] = next_ref[src]
            a_ref[pl.ds(base + 12, 4), :] = prev_ref[src]
        return carry

    lax.fori_loop(0, LEV, fill, 0)
    b_ref[0:4, :] = next_ref[2 * LEV]
    b_ref[4:8, :] = prev_ref[2 * LEV]
    row = lax.broadcasted_iota(jnp.int32, (ROWS, W), 0)
    south = jnp.where(tile < NT - 1, 1.0, 0.0).astype(F32)
    north = jnp.where(tile > 0, 1.0, 0.0).astype(F32)
    valid = jnp.where(row < 4, south, north)
    stay = 1.0 - 4.0 * HORIZ - 2.0 * VERT
    coef = (stay - damping, (stay - b_ref[0:8, :]) * valid, HORIZ * valid, VERT * valid)

    def emit(s, ref):
        for member in range(2):
            for y in range(ROWS):
                rows = ref[pl.ds(member * BSTR + y, LPAD, stride=RING), :]
                cells_ref[s, member * W : member * W + LPAD, y * W : (y + 1) * W] = (
                    rows.astype(BF16)
                )

    emit(0, a_ref)
    src, dst = a_ref, b_ref
    for s in range(1, STEPS):

        def read(index, src=src):
            base = pl.multiple_of(index * RING, RING)
            return src[pl.ds(base, ROWS), :], src[pl.ds(base + ROWS, ROWS), :]

        def write(member, level, y0, y1, dst=dst):
            base = pl.multiple_of((member * LPAD + level) * RING, RING)
            dst[pl.ds(base, ROWS), :] = y0
            dst[pl.ds(base + ROWS, ROWS), :] = y1

        ring_step(read, write, LPAD, coef)
        emit(s, dst)
        src, dst = dst, src

    def drain(level, carry):
        for member in range(2):
            base = pl.multiple_of((member * LPAD + level) * RING, RING)
            ring_ref[member * LEV + level] = src[pl.ds(base, RING), :]
        return carry

    lax.fori_loop(0, LEV, drain, 0)


def last_parent_kernel(ring_ref, terrain_ref, out_ref):
    damping = DRAG * terrain_ref[...].astype(F32) / 3000.0
    stay = 1.0 - 4.0 * HORIZ - 2.0 * VERT

    def read(index):
        return ring_ref[index, 0:ROWS, :], ring_ref[index, ROWS:RING, :]

    def write(member, level, y0, y1):
        out_ref[member * LEV + level] = y0

    ring_step(read, write, LEV, (stay - damping, None, None, None), own_only=True)


def gather_kernel(got_ref, cells_ref, out_ref, scr_ref):
    lane = lax.broadcasted_iota(jnp.int32, (NT, ROWS * W), 1).astype(F32)
    for s in range(STEPS):
        rows = got_ref[pl.ds(s, NT, stride=4), :]
        hot = [
            jnp.where(lane == rows[:, L_REQ + c : L_REQ + c + 1], 1.0, 0.0).astype(BF16)
            for c in range(2)
        ]
        hot = jnp.concatenate(hot, axis=0)
        res = lax.dot_general(
            hot, cells_ref[s], (((1,), (1,)), ((), ())), preferred_element_type=F32
        )
        for b in range(2):
            for c in range(2):
                scr_ref[pl.ds(b * 8 + s * 2 + c, NT, stride=16), :] = res[
                    c * W : (c + 1) * W, b * W : (b + 1) * W
                ]
    out_ref[...] = scr_ref[...].astype(BF16)


def regroup_kernel(bperm_ref, got_ref, out_ref, scr_ref, scr2_ref):
    scr_ref[...] = got_ref[...].astype(F32)
    sub = lax.broadcasted_iota(jnp.int32, (2 * NT, W), 0)
    lane = lax.broadcasted_iota(jnp.int32, (2 * NT, W), 1)
    parity = jnp.bitwise_and(jnp.right_shift(lane, 5), 1)
    target = sub - parity * NT
    for s in range(STEPS):
        owner = jnp.right_shift(bperm_ref[s : s + 1, :], 10)
        hot = jnp.where(target == owner, 1.0, 0.0).astype(BF16)
        values = jnp.concatenate(
            [
                jnp.concatenate(
                    [
                        scr_ref[pl.ds(b * 8 + s * 2 + c, NT, stride=16), :]
                        for b in range(2)
                    ],
                    axis=1,
                )
                for c in range(2)
            ],
            axis=0,
        ).astype(BF16)
        res = lax.dot_general(
            hot, values, (((0,), (0,)), ((), ())), preferred_element_type=F32
        )
        for b in range(2):
            for j in range(4):
                scr2_ref[pl.ds(b * 512 + s * 4 + j, 32, stride=16), :] = res[
                    j * 32 : (j + 1) * 32, b * W : (b + 1) * W
                ]
    for b in range(2):
        out_ref[b * 1024 : b * 1024 + 512, :] = scr2_ref[b * 512 : (b + 1) * 512, :].astype(
            BF16
        )
        out_ref[b * 1024 + 512 : (b + 1) * 1024, :] = jnp.zeros((512, W), BF16)


def plan_kernel(tile_ref, got_ref, mix_ref, hot_ref, base_ref):
    interior = jnp.where(jnp.bitwise_and(tile_ref[0], 63) < 32, 0, 1)
    n = 4 * NT
    turned = [got_ref[pl.ds(j, NT, stride=4), :].T for j in range(4)]
    sub = lax.broadcasted_iota(jnp.int32, (n, n), 0)

    def dest(s):
        row = jnp.concatenate(
            [t[L_DEST + s : L_DEST + s + 1, :] for t in turned], axis=1
        ).astype(jnp.int32)
        return jnp.right_shift(row, 8), jnp.bitwise_and(row, 3)

    tile_to, slot_to = dest(STEPS - 1)
    for s in range(STEPS - 1, -1, -1):
        if s < STEPS - 1:
            mid_tile, mid_slot = dest(s)
            move = jnp.where(sub == mid_slot * NT + mid_tile, 1.0, 0.0).astype(BF16)
            later = jnp.concatenate(
                [
                    jnp.broadcast_to(tile_to, (8, n)),
                    jnp.broadcast_to(slot_to, (8, n)),
                ],
                axis=0,
            )
            both = jnp.dot(
                later.astype(F32).astype(BF16), move, preferred_element_type=F32
            )
            tile_to = both[0:1, :].astype(jnp.int32)
            slot_to = both[8:9, :].astype(jnp.int32)
        hot_ref[s] = jnp.where(sub == tile_to * 4 + slot_to, 1.0, 0.0).astype(BF16)
    columns = jnp.concatenate(
        [got_ref[pl.ds(j, NT, stride=4), :] for j in range(4)], axis=0
    )
    mixed = lax.dot_general(
        columns,
        mix_ref[interior],
        (((1,), (0,)), ((), ())),
        precision=lax.Precision.HIGHEST,
        preferred_element_type=F32,
    )
    parts = []
    for _ in range(3):
        part = mixed.astype(BF16)
        parts.append(part)
        mixed = mixed - part.astype(F32)
    moved = jnp.dot(
        hot_ref[0], jnp.concatenate(parts, axis=1), preferred_element_type=F32
    )
    base_ref[...] = moved[:, :W] + (moved[:, W : 2 * W] + moved[:, 2 * W :])


def owner_kernel(tile_ref, got_ref, hot_ref, base_ref, mix_ref, out_ref, scr_ref):
    bound = jnp.bitwise_and(tile_ref[0], 63) < 32

    @pl.when(bound)
    def _():
        scr_ref[...] = got_ref[...].astype(F32)
        moved = []
        for s in range(STEPS):
            edge = jnp.concatenate(
                [scr_ref[pl.ds(s * 4 + j, NT, stride=16), :] for j in range(4)], axis=0
            ).astype(BF16)
            moved.append(
                jnp.dot(hot_ref[s], edge, preferred_element_type=F32).astype(BF16)
            )
        total = jnp.dot(
            jnp.concatenate(moved, axis=1), mix_ref[...], preferred_element_type=F32
        )
        out_ref[...] = base_ref[...] + (
            total[:, :W] + (total[:, W : 2 * W] + total[:, 2 * W :])
        )

    @pl.when(jnp.logical_not(bound))
    def _():
        out_ref[...] = base_ref[...]


def nest_kernel(got_ref, out_ref, scr_ref):
    for b in range(2):
        for half in range(2):
            start = b * 2 * W + half * W
            scr_ref[b, :, half * W : (half + 1) * W] = got_ref[start : start + W, :].T
    for b in range(2):
        out_ref[b] = scr_ref[b, :LEV, :]


def stats_kernel(own_ref, other_ref, mean_ref, var_ref):
    a0, a1 = own_ref[0], own_ref[1]
    b0, b1 = other_ref[0], other_ref[1]
    mean = ((a0 + a1) + (b0 + b1)) / 4.0
    mean_ref[...] = mean
    own = (a0 - mean) * (a0 - mean) + (a1 - mean) * (a1 - mean)
    other = (b0 - mean) * (b0 - mean) + (b1 - mean) * (b1 - mean)
    var_ref[...] = (own + other) / 4.0


def exchange(x):
    return lax.all_to_all(x, "tile", split_axis=0, concat_axis=0, tiled=True)


def on_device(parent_state, nest_state, terrain, shift_x, boundary_index, reloc_dest):
    q_mix, e_mix = constants()
    q_mix, e_mix = jnp.asarray(q_mix), jnp.asarray(e_mix)
    sds = jax.ShapeDtypeStruct
    tile = lax.axis_index("tile").astype(jnp.int32).reshape(1)
    parent = parent_state.reshape(2 * LEV, ROWS, W)

    message = call(
        send_kernel,
        sds((4 * NT, W), F32),
        in_specs=[SM, VM, VM, VM],
        scratch=[pltpu.VMEM((2, W, 2 * W), F32)],
        name="send",
        nbytes=1 << 19,
    )(shift_x, nest_state, boundary_index, reloc_dest)
    first = exchange(message.reshape(NT, 4, W)).reshape(4 * NT, W)

    down, up = call(
        halo_kernel,
        (sds((2 * LEV + 1, 4, W), F32), sds((2 * LEV + 1, 4, W), F32)),
        name="halo",
        nbytes=1 << 20,
    )(parent, terrain)
    forward = [(i, i + 1) for i in range(NT - 1)]
    backward = [(i + 1, i) for i in range(NT - 1)]
    from_prev = lax.ppermute(down, "tile", forward)
    from_next = lax.ppermute(up, "tile", backward)
    cells, ring = call(
        parent_kernel,
        (sds((STEPS, 2 * W, ROWS * W), BF16), sds((2 * LEV, RING, W), F32)),
        in_specs=[SM, VM, VM, VM, VM],
        scratch=[pltpu.VMEM((2 * BSTR, W), F32)] * 2,
        name="parent",
        flops=1 << 24,
        nbytes=4 << 20,
    )(tile, parent, from_next, from_prev, terrain)

    values = call(
        gather_kernel,
        sds((16 * NT, W), BF16),
        scratch=[pltpu.VMEM((16 * NT, W), F32)],
        name="gather",
        flops=1 << 29,
        nbytes=3 << 20,
    )(first, cells)
    second = exchange(values.reshape(NT, 16, W)).reshape(16 * NT, W)

    parent_out = call(
        last_parent_kernel,
        sds((2 * LEV, ROWS, W), F32),
        name="last_parent",
        flops=1 << 22,
        nbytes=2 << 20,
    )(ring, terrain)
    hot, base = call(
        plan_kernel,
        (sds((STEPS, 4 * NT, 4 * NT), BF16), sds((4 * NT, W), F32)),
        in_specs=[SM, VM, VM],
        name="plan",
        flops=1 << 28,
        nbytes=3 << 20,
    )(tile, first, q_mix)

    bperm = boundary_index.reshape(STEPS, 32, 4).transpose(0, 2, 1).reshape(STEPS, NT)
    edges = call(
        regroup_kernel,
        sds((16 * NT, W), BF16),
        scratch=[pltpu.VMEM((16 * NT, W), F32), pltpu.VMEM((8 * NT, W), F32)],
        name="regroup",
        flops=1 << 26,
        nbytes=1 << 20,
    )(bperm, second)
    third = exchange(edges.reshape(NT, 16, W)).reshape(16 * NT, W)

    columns = call(
        owner_kernel,
        sds((4 * NT, W), F32),
        in_specs=[SM, VM, VM, VM, VM],
        scratch=[pltpu.VMEM((16 * NT, W), F32)],
        name="owner",
        flops=1 << 29,
        nbytes=3 << 20,
    )(tile, third, hot, base, e_mix)
    fourth = exchange(columns.reshape(NT, 4, W)).reshape(4 * NT, W)

    nest_out = call(
        nest_kernel,
        sds((2, LEV, 2 * W), F32),
        scratch=[pltpu.VMEM((2, W, 2 * W), F32)],
        name="nest",
        nbytes=1 << 19,
    )(fourth)
    other = lax.ppermute(nest_out, "member", [(0, 1), (1, 0)])
    mean, variance = call(
        stats_kernel,
        (sds((LEV, 2 * W), F32), sds((LEV, 2 * W), F32)),
        name="stats",
        nbytes=1 << 19,
    )(nest_out, other)
    return (parent_out.reshape(parent_state.shape), nest_out, mean, variance)


def solution(mesh):
    in_specs = (
        P("member", None, "tile", None),
        P("member", None, "tile"),
        P("tile", None),
        P(),
        P(None, "tile"),
        P(None, "tile"),
    )
    out_specs = (
        P("member", None, "tile", None),
        P("member", None, "tile"),
        P(None, "tile"),
        P(None, "tile"),
    )
    return jax.shard_map(
        on_device, mesh=mesh, in_specs=in_specs, out_specs=out_specs, check_vma=False
    )
```

profile of v0, /device:TPU:1, one launch (start us, length us, event | category | flops | bytes accessed | tf_op | source)
XLA Modules:
  0.0 134.2 jit_solution(17785150395831638616)
XLA Ops:
  0.6 0.0 copy-start.1
  0.6 1.0 copy.16.nest_ref
  1.6 0.0 copy-start.12
  1.7 0.7 copy-done.12
  2.3 0.0 copy-start.14
  2.3 0.7 copy-done.14
  3.0 0.0 copy-start.15
  3.0 0.7 copy-done.15
  3.7 1.6 %send.1 = f32[512,128]{1,0:T(8,128)} custom-call(s32[4]{0:T(128)S(1)} %copy-done.15, f32[2,81,256]{2,1,0:T(8,128)S(1)} %copy.16.nest_ref, s32[4,128]{1,0:T(4,128)S(1)} %copy-done.12, s32[4,256]{1,0:T(4,128)S(1)} %copy-done.14), custom_call_target="tpu_custom_call" | custom-call | bytes 524288 | tf_op jit(solution)/shard_map/send/pallas_call | solution.py:410
  5.2 16.3 %all-to-all-start = ((f32[128,4,128]{2,1,0:T(4,128)}), f32[128,4,128]{2,1,0:T(4,128)S(1)}, u32[]{:S(2)}, u32[]{:S(2)}) async-start(f32[128,4,128]{2,1,0:T(4,128)} %bitcast.4), calls=%async_computation | async-start | bytes 524288 | tf_op jit(solution)/shard_map/all_to_all | solution.py:400
  21.6 0.0 copy-start
  21.6 1.1 copy-done
  22.7 0.0 copy-start.9
  22.7 0.7 copy-done.9
  23.4 0.1 halo.1
  23.5 1.3 collective-permute-start
  24.8 4.0 %collective-permute-start.1 = (f32[163,4,128]{2,1,0:T(4,128)S(1)}, f32[163,4,128]{2,1,0:T(4,128)S(1)}, u32[]{:S(2)}, u32[]{:S(2)}) collective-permute-start(f32[163,4,128]{2,1,0:T(4,128)S(1)} %get-tuple-element.13), channel_id=1, source_target_pairs={{0,1},{1,2},{2,3},{3,4},{4,5},{5,6},{6,7},{7,8},{8,9},{9,10},{10,1... | collective-permute-start | bytes 1001480 | tf_op jit(solution)/shard_map/ppermute | solution.py:428
  28.8 7.2 %collective-permute-done.next_ref = f32[163,4,128]{2,1,0:T(4,128)S(1)} collective-permute-done((f32[163,4,128]{2,1,0:T(4,128)S(1)}, f32[163,4,128]{2,1,0:T(4,128)S(1)}, u32[]{:S(2)}, u32[]{:S(2)}) %collective-permute-start) | collective-permute-done | bytes 333856 | tf_op jit(solution)/shard_map/ppermute | solution.py:429
  36.0 0.0 collective-permute-done.1.prev_ref
  36.0 0.0 copy-start.5
  36.0 0.7 copy-done.5
  36.7 0.0 copy-done.1
  36.7 0.0 copy-start.6
  36.7 1.0 copy-done.6
  37.7 0.0 copy-start.10
  37.7 0.7 copy-done.10
  38.3 6.2 %parent.1 = (bf16[4,256,1024]{2,1,0:T(8,128)(2,1)S(1)}, f32[162,16,128]{2,1,0:T(8,128)S(1)}) custom-call(s32[1]{0:T(128)} %bitcast.tile_ref, f32[162,8,128]{2,1,0:T(8,128)S(1)} %bitcast.13, f32[163,4,128]{2,1,0:T(4,128)S(1)} %collective-permute-done.next_ref, f32[163,4,128]{2,1,0:T(4,128)S(1)} %copy-done.6, s32[8,128]{1,0:T(8,128)S(1)} %copy-done.10), custom_call_target="tpu_custom_call" | custom-call | flops 16777216 | bytes 4194304 | tf_op jit(solution)/shard_map/parent/pallas_call | solution.py:430
  44.6 0.0 copy-start.2
  44.6 1.1 copy-done.2
  45.7 0.0 copy-start.13
  45.7 0.0 all-to-all-done
  45.7 1.8 %gather.1 = bf16[2048,128]{1,0:T(8,128)(2,1)} custom-call(f32[512,128]{1,0:T(8,128)S(1)} %bitcast.17, bf16[4,256,1024]{2,1,0:T(8,128)(2,1)S(1)} %get-tuple-element.15.cells_ref), custom_call_target="tpu_custom_call" | custom-call | flops 536870912 | bytes 3145728 | tf_op jit(solution)/shard_map/gather/pallas_call | solution.py:440
  47.5 0.0 copy-start.16
  47.5 0.0 copy-start.4
  47.5 15.8 %all-to-all-start.1 = ((bf16[128,16,128]{2,1,0:T(8,128)(2,1)}), bf16[128,16,128]{2,1,0:T(8,128)(2,1)S(1)}, u32[]{:S(2)}, u32[]{:S(2)}) async-start(bf16[128,16,128]{2,1,0:T(8,128)(2,1)} %bitcast.6), calls=%async_computation.1 | async-start | bytes 1048576 | tf_op jit(solution)/shard_map/all_to_all | solution.py:400
  63.3 0.0 copy-done.13
  63.3 0.1 reshape.50
  63.4 0.1 copy.15
  63.5 0.1 reshape.51.bperm_ref
  63.6 15.0 %all-to-all-done.1 = bf16[128,16,128]{2,1,0:T(8,128)(2,1)S(1)} async-done(((bf16[128,16,128]{2,1,0:T(8,128)(2,1)}), bf16[128,16,128]{2,1,0:T(8,128)(2,1)S(1)}, u32[]{:S(2)}, u32[]{:S(2)}) %all-to-all-start.1) | async-done | bytes 524320 | tf_op jit(solution)/shard_map/all_to_all | solution.py:400
  78.5 1.4 %regroup.1 = bf16[2048,128]{1,0:T(8,128)(2,1)} custom-call(s32[4,128]{1,0:T(4,128)S(1)} %reshape.51.bperm_ref, bf16[2048,128]{1,0:T(8,128)(2,1)S(1)} %bitcast.14), custom_call_target="tpu_custom_call" | custom-call | flops 67108864 | bytes 1048576 | tf_op jit(solution)/shard_map/regroup/pallas_call | solution.py:467
  80.0 8.4 %all-to-all-start.2 = ((bf16[128,16,128]{2,1,0:T(8,128)(2,1)}), bf16[128,16,128]{2,1,0:T(8,128)(2,1)S(1)}, u32[]{:S(2)}, u32[]{:S(2)}) async-start(bf16[128,16,128]{2,1,0:T(8,128)(2,1)} %bitcast.8), calls=%async_computation.2 | async-start | bytes 1048576 | tf_op jit(solution)/shard_map/all_to_all | solution.py:400
  88.4 0.0 copy-done.16
  88.4 2.2 %plan.1 = (bf16[4,512,512]{2,1,0:T(8,128)(2,1)S(1)}, f32[512,128]{1,0:T(8,128)S(1)}) custom-call(s32[1]{0:T(128)} %bitcast.tile_ref, f32[512,128]{1,0:T(8,128)S(1)} %bitcast.18, f32[2,128,128]{2,1,0:T(8,128)S(1)} %copy-done.16), custom_call_target="tpu_custom_call" | custom-call | flops 268435456 | bytes 3145728 | tf_op jit(solution)/shard_map/plan/pallas_call | solution.py:457
  90.6 0.0 copy-start.7
  90.6 0.7 copy-done.7
  91.3 11.2 %all-to-all-done.2 = bf16[128,16,128]{2,1,0:T(8,128)(2,1)S(1)} async-done(((bf16[128,16,128]{2,1,0:T(8,128)(2,1)}), bf16[128,16,128]{2,1,0:T(8,128)(2,1)S(1)}, u32[]{:S(2)}, u32[]{:S(2)}) %all-to-all-start.2) | async-done | bytes 524320 | tf_op jit(solution)/shard_map/all_to_all | solution.py:400
  102.5 0.0 copy-done.4
  102.5 0.0 copy-start.8
  102.5 0.9 copy-done.8
  103.5 0.0 copy-start.3
  103.5 0.0 copy-start.11
  103.5 1.1 owner.1
  104.6 20.3 %all_to_all.20 = f32[128,4,128]{2,1,0:T(4,128)S(1)} all-to-all(f32[128,4,128]{2,1,0:T(4,128)S(1)} %bitcast.19), channel_id=1, replica_groups=mesh['member'=2,'tile'=128] {'tile'}, dimensions={0} | all-to-all | bytes 524288 | tf_op jit(solution)/shard_map/all_to_all | solution.py:400
  124.9 0.1 nest.1.own_ref
  125.1 5.8 %collective-permute-start.2 = (f32[2,81,256]{2,1,0:T(8,128)S(1)}, f32[2,81,256]{2,1,0:T(8,128)S(1)}, u32[]{:S(2)}, u32[]{:S(2)}) collective-permute-start(f32[2,81,256]{2,1,0:T(8,128)S(1)} %nest.1.own_ref), channel_id=1, source_target_pairs={{0,128},{128,0},{1,129},{129,1},{2,130},{130,2},{3,131},{131,3},{4... | collective-permute-start | bytes 497672 | tf_op jit(solution)/shard_map/ppermute | solution.py:495
  130.9 0.0 copy-done.3
  130.9 0.0 copy-done.11
  130.9 1.8 %last_parent.1 = f32[162,8,128]{2,1,0:T(8,128)} custom-call(f32[162,16,128]{2,1,0:T(8,128)S(1)} %copy-done.3, s32[8,128]{1,0:T(8,128)S(1)} %copy-done.11), custom_call_target="tpu_custom_call" | custom-call | flops 4194304 | bytes 2097152 | tf_op jit(solution)/shard_map/last_parent/pallas_call | solution.py:450
  132.7 0.8 copy.17
  133.5 0.0 collective-permute-done.2.other_ref
  133.5 0.7 stats.1
Async XLA Ops:
  0.6 36.1 %copy-start.1 = (f32[2,81,8,128]{3,2,1,0:T(8,128)S(1)}, f32[2,81,8,128]{3,2,1,0:T(8,128)}, u32[]{:S(2)}) copy-start(f32[2,81,8,128]{3,2,1,0:T(8,128)} %param.8) | copy-start | bytes 1990660
  1.6 0.7 copy-start.12
  2.3 0.7 copy-start.14
  3.0 0.7 copy-start.15
  5.2 40.5 %all-to-all-start = ((f32[128,4,128]{2,1,0:T(4,128)}), f32[128,4,128]{2,1,0:T(4,128)S(1)}, u32[]{:S(2)}, u32[]{:S(2)}) async-start(f32[128,4,128]{2,1,0:T(4,128)} %bitcast.4), calls=%async_computation | async-start | bytes 524288 | tf_op jit(solution)/shard_map/all_to_all | solution.py:400
  21.6 1.1 copy-start
  22.7 0.7 copy-start.9
  23.5 12.5 %collective-permute-start = (f32[163,4,128]{2,1,0:T(4,128)S(1)}, f32[163,4,128]{2,1,0:T(4,128)S(1)}, u32[]{:S(2)}, u32[]{:S(2)}) collective-permute-start(f32[163,4,128]{2,1,0:T(4,128)S(1)} %get-tuple-element.12), channel_id=1, source_target_pairs={{1,0},{2,1},{3,2},{4,3},{5,4},{6,5},{7,6},{8,7},{9,8},{10,9},{11,1... | collective-permute-start | bytes 1001480 | tf_op jit(solution)/shard_map/ppermute | solution.py:429
  24.8 11.2 %collective-permute-start.1 = (f32[163,4,128]{2,1,0:T(4,128)S(1)}, f32[163,4,128]{2,1,0:T(4,128)S(1)}, u32[]{:S(2)}, u32[]{:S(2)}) collective-permute-start(f32[163,4,128]{2,1,0:T(4,128)S(1)} %get-tuple-element.13), channel_id=1, source_target_pairs={{0,1},{1,2},{2,3},{3,4},{4,5},{5,6},{6,7},{7,8},{8,9},{9,10},{10,1... | collective-permute-start | bytes 1001480 | tf_op jit(solution)/shard_map/ppermute | solution.py:428
  36.0 0.7 copy-start.5
  36.7 1.0 copy-start.6
  37.7 0.7 copy-start.10
  44.6 1.1 copy-start.2
  45.7 17.6 %copy-start.13 = (s32[4,128]{1,0:T(4,128)S(1)}, s32[4,128]{1,0:T(4,128)}, u32[]{:S(2)}) copy-start(s32[4,128]{1,0:T(4,128)} %bidx_ref.1) | copy-start | bytes 6148
  47.5 41.0 %copy-start.16 = (f32[2,128,128]{2,1,0:T(8,128)S(1)}, f32[2,128,128]{2,1,0:T(8,128)}, u32[]{:S(2)}) copy-start(f32[2,128,128]{2,1,0:T(8,128)} %constant.8.clone.mix_ref) | copy-start | bytes 393220
  47.5 55.1 %copy-start.4 = (bf16[512,384]{1,0:T(8,128)(2,1)S(1)}, bf16[512,384]{1,0:T(8,128)(2,1)}, u32[]{:S(2)}) copy-start(bf16[512,384]{1,0:T(8,128)(2,1)} %constant.9.clone.mix_ref) | copy-start | bytes 1179652
  47.5 31.1 %all-to-all-start.1 = ((bf16[128,16,128]{2,1,0:T(8,128)(2,1)}), bf16[128,16,128]{2,1,0:T(8,128)(2,1)S(1)}, u32[]{:S(2)}, u32[]{:S(2)}) async-start(bf16[128,16,128]{2,1,0:T(8,128)(2,1)} %bitcast.6), calls=%async_computation.1 | async-start | bytes 1048576 | tf_op jit(solution)/shard_map/all_to_all | solution.py:400
  80.0 22.6 %all-to-all-start.2 = ((bf16[128,16,128]{2,1,0:T(8,128)(2,1)}), bf16[128,16,128]{2,1,0:T(8,128)(2,1)S(1)}, u32[]{:S(2)}, u32[]{:S(2)}) async-start(bf16[128,16,128]{2,1,0:T(8,128)(2,1)} %bitcast.8), calls=%async_computation.2 | async-start | bytes 1048576 | tf_op jit(solution)/shard_map/all_to_all | solution.py:400
  90.6 0.7 copy-start.7
  102.5 1.0 copy-start.8
  103.5 27.4 %copy-start.3 = (f32[162,16,128]{2,1,0:T(8,128)S(1)}, f32[162,16,128]{2,1,0:T(8,128)}, u32[]{:S(2)}) copy-start(f32[162,16,128]{2,1,0:T(8,128)} %copy-done.2) | copy-start | bytes 3981316
  103.5 27.4 %copy-start.11 = (s32[8,128]{1,0:T(8,128)S(1)}, s32[8,128]{1,0:T(8,128)}, u32[]{:S(2)}) copy-start(s32[8,128]{1,0:T(8,128)} %terrain_ref.5) | copy-start | bytes 12292
  125.1 8.4 %collective-permute-start.2 = (f32[2,81,256]{2,1,0:T(8,128)S(1)}, f32[2,81,256]{2,1,0:T(8,128)S(1)}, u32[]{:S(2)}, u32[]{:S(2)}) collective-permute-start(f32[2,81,256]{2,1,0:T(8,128)S(1)} %nest.1.own_ref), channel_id=1, source_target_pairs={{0,128},{128,0},{1,129},{129,1},{2,130},{130,2},{3,131},{131,3},{4... | collective-permute-start | bytes 497672 | tf_op jit(solution)/shard_map/ppermute | solution.py:495
where the time goes:
time: 135 us; the launch traced here: 134 us
  starting transfers between devices  51.7 us (38%)
  waiting for transfers between devices  33.3 us (25%)
  blocking collectives  20.3 us (15%)
  Pallas kernels  17.1 us (13%)
  local copies, waits for them, and re-layouts  11 us (8%)
    all_to_all x3, starting transfers between devices, exchange(): return lax.all_to_all(x, 'tile', split_axis=0, concat_axis=0, tiled=True)  40.6 us
    all_to_all x3, waiting for transfers between devices, exchange(): return lax.all_to_all(x, 'tile', split_axis=0, concat_axis=0, tiled=True)  26.2 us
    all_to_all x1, blocking collectives, exchange(): return lax.all_to_all(x, 'tile', split_axis=0, concat_axis=0, tiled=True)  20.3 us
    unnamed x36, local copies, waits for them, and re-layouts  10.7 us
    ppermute x1, waiting for transfers between devices, on_device(): from_next = lax.ppermute(up, 'tile', backward)  7.16 us
    pallas_call x1, Pallas kernels, on_device(): call(parent_kernel, (sds((STEPS, 2 * W, ROWS * W), BF16), sds((2 * LEV, R...  6.22 us
    ppermute x1, starting transfers between devices, on_device(): other = lax.ppermute(nest_out, 'member', [(0, 1), (1, 0)])  5.84 us
    ppermute x1, starting transfers between devices, on_device(): from_prev = lax.ppermute(down, 'tile', forward)  4.01 us
  transfers between devices with their start and end apart: 6, of which 3 were waited for; matrix products, arithmetic and copies ran while one was open for 1% of the time, Pallas kernels for 8%

commit v1 on v0

--- a/solution.py
+++ b/solution.py
@@ -25,7 +25,7 @@
 DRAG = 0.1
 RELAX = 0.5
 IMPL = 0.8
-VMEM_LIMIT = 48 * 1024 * 1024
+VMEM_LIMIT = 20 * 1024 * 1024
 
 
 def solve_matrix():
@@ -85,14 +85,50 @@
 
 
 VM = pl.BlockSpec(memory_space=pltpu.VMEM)
+HB = pl.BlockSpec(memory_space=pltpu.HBM)
 SM = pl.BlockSpec(memory_space=pltpu.SMEM)
 
 
-def send_kernel(shift_ref, nest_ref, bidx_ref, dest_ref, msg_ref, pad_ref):
+def start_all(pairs, sems):
+    copies = [pltpu.make_async_copy(x, y, sems.at[i]) for i, (x, y) in enumerate(pairs)]
+    for copy in copies:
+        copy.start()
+    return copies
+
+
+def halo_kernel(parent_hbm, terrain_hbm, down_ref, up_ref, parent_ref, terrain_ref, sems):
+    copies = start_all([(parent_hbm, parent_ref), (terrain_hbm, terrain_ref)], sems)
+    for copy in copies:
+        copy.wait()
+    damping = DRAG * terrain_ref[...].astype(F32) / 3000.0
+    down_ref[: 2 * LEV, :, :] = parent_ref[:, 4:, :]
+    up_ref[: 2 * LEV, :, :] = parent_ref[:, :4, :]
+    down_ref[2 * LEV, :, :] = damping[4:, :]
+    up_ref[2 * LEV, :, :] = damping[:4, :]
+
+
+def send_kernel(
+    shift_hbm, nest_hbm, bidx_hbm, dest_hbm,
+    msg_ref,
+    shift_ref, nest_ref, bidx_ref, dest_ref, pad_ref, sems,
+):
+    copies = start_all(
+        [
+            (nest_hbm, nest_ref),
+            (bidx_hbm, bidx_ref),
+            (dest_hbm, dest_ref),
+            (shift_hbm, shift_ref),
+        ],
+        sems,
+    )
+    for copy in copies:
+        copy.wait()
     zeros = jnp.zeros((W - LEV + 1, 2 * W), F32)
     for b in range(2):
         pad_ref[b, LEV - 1 :, :] = zeros
-        pad_ref[b, :LEV, :] = nest_ref[b]
+        for half in range(2):
+            lanes = slice(half * W, (half + 1) * W)
+            pad_ref[b, :LEV, lanes] = nest_ref[:, half, b, :]
         pad_ref[b, L_DEST : L_DEST + STEPS, :] = dest_ref[...].astype(F32)
         for half in range(2):
             block = pad_ref[b, :, half * W : (half + 1) * W]
@@ -115,14 +151,6 @@
         rows = jnp.where(lane == L_REQ, first, rows)
         rows = jnp.where(lane == L_REQ + 1, second, rows)
         msg_ref[pl.ds(s, NT, stride=4), :] = rows
-
-
-def halo_kernel(parent_ref, terrain_ref, down_ref, up_ref):
-    damping = DRAG * terrain_ref[...].astype(F32) / 3000.0
-    down_ref[: 2 * LEV, :, :] = parent_ref[:, 4:, :]
-    up_ref[: 2 * LEV, :, :] = parent_ref[:, :4, :]
-    down_ref[2 * LEV, :, :] = damping[4:, :]
-    up_ref[2 * LEV, :, :] = damping[:4, :]
 
 
 def ring_step(read, write, level_stride, coef, own_only=False):
@@ -162,9 +190,22 @@
 
 
 def parent_kernel(
-    tile_ref, parent_ref, next_ref, prev_ref, terrain_ref, cells_ref, ring_ref, a_ref, b_ref
+    tile_ref, parent_hbm, next_hbm, prev_hbm, terrain_hbm,
+    cells_ref, ring_ref,
+    parent_ref, terrain_ref, next_ref, prev_ref, a_ref, b_ref, sems,
 ):
     tile = tile_ref[0]
+    copies = start_all(
+        [
+            (parent_hbm, parent_ref),
+            (terrain_hbm, terrain_ref),
+            (next_hbm, next_ref),
+            (prev_hbm, prev_ref),
+        ],
+        sems,
+    )
+    for copy in copies[1:]:
+        copy.wait()
     damping = DRAG * terrain_ref[...].astype(F32) / 3000.0
     pads = jnp.zeros(((LPAD - LEV) * RING, W), F32)
     for ref in (a_ref, b_ref):
@@ -176,6 +217,8 @@
             cells_ref[s, member * W + LPAD : (member + 1) * W, :] = jnp.zeros(
                 (W - LPAD, ROWS * W), BF16
             )
+
+    copies[0].wait()
 
     def fill(level, carry):
         for member in range(2):
@@ -381,19 +424,27 @@
     for b in range(2):
         for half in range(2):
             start = b * 2 * W + half * W
-            scr_ref[b, :, half * W : (half + 1) * W] = got_ref[start : start + W, :].T
-    for b in range(2):
-        out_ref[b] = scr_ref[b, :LEV, :]
+            scr_ref[...] = got_ref[start : start + W, :].T
+            out_ref[pl.ds(half * 2 + b, LEV, stride=4), :] = scr_ref[:LEV, :]
 
 
 def stats_kernel(own_ref, other_ref, mean_ref, var_ref):
-    a0, a1 = own_ref[0], own_ref[1]
-    b0, b1 = other_ref[0], other_ref[1]
-    mean = ((a0 + a1) + (b0 + b1)) / 4.0
-    mean_ref[...] = mean
-    own = (a0 - mean) * (a0 - mean) + (a1 - mean) * (a1 - mean)
-    other = (b0 - mean) * (b0 - mean) + (b1 - mean) * (b1 - mean)
-    var_ref[...] = (own + other) / 4.0
+    for half in range(2):
+        a0, a1, b0, b1 = (
+            ref[pl.ds(half * 2 + b, LEV, stride=4), :]
+            for ref in (own_ref, other_ref)
+            for b in range(2)
+        )
+        lanes = slice(half * W, (half + 1) * W)
+        mean = ((a0 + a1) + (b0 + b1)) / 4.0
+        mean_ref[:, lanes] = mean
+        own = (a0 - mean) * (a0 - mean) + (a1 - mean) * (a1 - mean)
+        other = (b0 - mean) * (b0 - mean) + (b1 - mean) * (b1 - mean)
+        var_ref[:, lanes] = (own + other) / 4.0
+
+
+def in_hbm(x):
+    return pltpu.with_memory_space_constraint(x, pltpu.HBM)
 
 
 def exchange(x):
@@ -407,35 +458,59 @@
     tile = lax.axis_index("tile").astype(jnp.int32).reshape(1)
     parent = parent_state.reshape(2 * LEV, ROWS, W)
 
+    nest = nest_state.reshape(2, LEV, 2, W).transpose(1, 2, 0, 3)
+    parent, terrain = in_hbm(parent), in_hbm(terrain)
+    down, up = call(
+        halo_kernel,
+        (sds((2 * LEV + 1, 4, W), F32), sds((2 * LEV + 1, 4, W), F32)),
+        in_specs=[HB] * 2,
+        scratch=[
+            pltpu.VMEM((2 * LEV, ROWS, W), F32),
+            pltpu.VMEM((ROWS, W), jnp.int32),
+            pltpu.SemaphoreType.DMA((2,)),
+        ],
+        name="halo",
+        nbytes=1 << 20,
+    )(parent, terrain)
+    nest, down, up = lax.optimization_barrier((nest, down, up))
+    nest = in_hbm(nest)
     message = call(
         send_kernel,
         sds((4 * NT, W), F32),
-        in_specs=[SM, VM, VM, VM],
-        scratch=[pltpu.VMEM((2, W, 2 * W), F32)],
+        in_specs=[HB] * 4,
+        scratch=[
+            pltpu.SMEM((STEPS,), jnp.int32),
+            pltpu.VMEM((LEV, 2, 2, W), F32),
+            pltpu.VMEM((STEPS, NT), jnp.int32),
+            pltpu.VMEM((STEPS, 2 * W), jnp.int32),
+            pltpu.VMEM((2, W, 2 * W), F32),
+            pltpu.SemaphoreType.DMA((4,)),
+        ],
         name="send",
-        nbytes=1 << 19,
-    )(shift_x, nest_state, boundary_index, reloc_dest)
-    first = exchange(message.reshape(NT, 4, W)).reshape(4 * NT, W)
-
-    down, up = call(
-        halo_kernel,
-        (sds((2 * LEV + 1, 4, W), F32), sds((2 * LEV + 1, 4, W), F32)),
-        name="halo",
-        nbytes=1 << 20,
-    )(parent, terrain)
+        nbytes=64 << 20,
+    )(in_hbm(shift_x), nest, in_hbm(boundary_index), in_hbm(reloc_dest))
     forward = [(i, i + 1) for i in range(NT - 1)]
     backward = [(i + 1, i) for i in range(NT - 1)]
     from_prev = lax.ppermute(down, "tile", forward)
     from_next = lax.ppermute(up, "tile", backward)
+    first = exchange(message.reshape(NT, 4, W)).reshape(4 * NT, W)
     cells, ring = call(
         parent_kernel,
         (sds((STEPS, 2 * W, ROWS * W), BF16), sds((2 * LEV, RING, W), F32)),
-        in_specs=[SM, VM, VM, VM, VM],
-        scratch=[pltpu.VMEM((2 * BSTR, W), F32)] * 2,
+        in_specs=[SM, HB, HB, HB, HB],
+        scratch=[
+            pltpu.VMEM((2 * LEV, ROWS, W), F32),
+            pltpu.VMEM((ROWS, W), jnp.int32),
+            pltpu.VMEM((2 * LEV + 1, 4, W), F32),
+            pltpu.VMEM((2 * LEV + 1, 4, W), F32),
+            pltpu.VMEM((2 * BSTR, W), F32),
+            pltpu.VMEM((2 * BSTR, W), F32),
+            pltpu.SemaphoreType.DMA((4,)),
+        ],
         name="parent",
         flops=1 << 24,
         nbytes=4 << 20,
-    )(tile, parent, from_next, from_prev, terrain)
+    )(tile, parent, in_hbm(from_next), in_hbm(from_prev), terrain)
 
     values = call(
         gather_kernel,
@@ -463,6 +538,7 @@
         nbytes=3 << 20,
     )(tile, first, q_mix)
 
+    second, parent_out = lax.optimization_barrier((second, parent_out))
     bperm = boundary_index.reshape(STEPS, 32, 4).transpose(0, 2, 1).reshape(STEPS, NT)
     edges = call(
         regroup_kernel,
@@ -487,8 +563,8 @@
 
     nest_out = call(
         nest_kernel,
-        sds((2, LEV, 2 * W), F32),
-        scratch=[pltpu.VMEM((2, W, 2 * W), F32)],
+        sds((4 * LEV, W), F32),
+        scratch=[pltpu.VMEM((W, W), F32)],
         name="nest",
         nbytes=1 << 19,
     )(fourth)
@@ -499,6 +575,8 @@
         name="stats",
         nbytes=1 << 19,
     )(nest_out, other)
+    nest_out = nest_out.reshape(LEV, 2, 2, W).transpose(2, 0, 1, 3)
+    nest_out = nest_out.reshape(nest_state.shape)
     return (parent_out.reshape(parent_state.shape), nest_out, mean, variance)
 
 

time: 135 us -> 129 us (0.956)
  local copies, waits for them, and re-layouts: 11 us -> 2.51 us
  Pallas kernels: 17.1 us -> 22.5 us
  waiting for transfers between devices: 33.3 us -> 31.5 us
    unnamed x36 -> x10, local copies, waits for them, and re-layouts: 10.7 us -> 1.47 us
    all_to_all x3, waiting for transfers between devices: 26.2 us -> 23.4 us  [exchange(): return lax.all_to_all(x, 'tile', split_axis=0, concat_axis=0, tiled=True)]
    pallas_call x1, Pallas kernels: 6.22 us -> 7.57 us  [on_device(): call(parent_kernel, (sds((STEPS, 2 * W, ROWS * W), BF16), sds((2 * LEV, R...]
  transfers between devices with their start and end apart: 6 -> 6, of which waited for: 3 -> 4; matrix products, arithmetic and copies ran while one was open for 1% -> 1% of each run, Pallas kernels for 8% -> 10%
where the time goes in v1:
time: 129 us; the launch traced here: 128 us
  starting transfers between devices  50.7 us (39%)
  waiting for transfers between devices  31.5 us (24%)
  Pallas kernels  22.5 us (17%)
  blocking collectives  20.3 us (16%)
  local copies, waits for them, and re-layouts  2.51 us (2%)
    all_to_all x3, starting transfers between devices, exchange(): return lax.all_to_all(x, 'tile', split_axis=0, concat_axis=0, tiled=True)  39.5 us
    all_to_all x3, waiting for transfers between devices, exchange(): return lax.all_to_all(x, 'tile', split_axis=0, concat_axis=0, tiled=True)  23.4 us
    all_to_all x1, blocking collectives, exchange(): return lax.all_to_all(x, 'tile', split_axis=0, concat_axis=0, tiled=True)  20.3 us
    ppermute x1, waiting for transfers between devices, on_device(): from_next = lax.ppermute(up, 'tile', backward)  7.82 us
    pallas_call x1, Pallas kernels, on_device(): call(parent_kernel, (sds((STEPS, 2 * W, ROWS * W), BF16), sds((2 * LEV, R...  7.57 us
    ppermute x1, starting transfers between devices, on_device(): other = lax.ppermute(nest_out, 'member', [(0, 1), (1, 0)])  5.84 us
    ppermute x1, starting transfers between devices, on_device(): from_prev = lax.ppermute(down, 'tile', forward)  4.01 us
    pallas_call x1, Pallas kernels, on_device(): call(plan_kernel, (sds((STEPS, 4 * NT, 4 * NT), BF16), sds((4 * NT, W), F...  3.13 us
  transfers between devices with their start and end apart: 6, of which 4 were waited for; matrix products, arithmetic and copies ran while one was open for 1% of the time, Pallas kernels for 10%

profile of v1, /device:TPU:1, one launch (start us, length us, event | category | flops | bytes accessed | tf_op | source)
XLA Modules:
  0.0 128.3 jit_solution(16866911046321270562)
XLA Ops:
  0.6 1.2 halo.1
  1.9 2.0 %send.1 = f32[512,128]{1,0:T(8,128)} custom-call(s32[4]{0:T(128)} %shift_hbm.1, f32[81,2,2,128]{3,2,1,0:T(2,128)} %bitcast.26, s32[4,128]{1,0:T(4,128)} %bidx_hbm.1, s32[4,256]{1,0:T(4,128)} %dest_hbm.1), custom_call_target="tpu_custom_call" | custom-call | bytes 67108864 | tf_op jit(solution)/shard_map/send/pallas_call | solution.py:477
  3.9 16.9 %all-to-all-start = ((f32[128,4,128]{2,1,0:T(4,128)}), f32[128,4,128]{2,1,0:T(4,128)}, u32[]{:S(2)}, u32[]{:S(2)}) async-start(f32[128,4,128]{2,1,0:T(4,128)} %bitcast.3), calls=%async_computation | async-start | bytes 524288 | tf_op jit(solution)/shard_map/all_to_all | solution.py:451
  20.8 1.3 %collective-permute-start = (f32[163,4,128]{2,1,0:T(4,128)S(1)}, f32[163,4,128]{2,1,0:T(4,128)S(1)}, u32[]{:S(2)}, u32[]{:S(2)}) collective-permute-start(f32[163,4,128]{2,1,0:T(4,128)S(1)} %get-tuple-element.20), channel_id=1, source_target_pairs={{1,0},{2,1},{3,2},{4,3},{5,4},{6,5},{7,6},{8,7},{9,8},{10,9},{11,1... | collective-permute-start | bytes 1001480 | tf_op jit(solution)/shard_map/ppermute | solution.py:495
  22.1 4.0 %collective-permute-start.1 = (f32[163,4,128]{2,1,0:T(4,128)S(1)}, f32[163,4,128]{2,1,0:T(4,128)S(1)}, u32[]{:S(2)}, u32[]{:S(2)}) collective-permute-start(f32[163,4,128]{2,1,0:T(4,128)S(1)} %get-tuple-element.21), channel_id=1, source_target_pairs={{0,1},{1,2},{2,3},{3,4},{4,5},{5,6},{6,7},{7,8},{8,9},{9,10},{10,1... | collective-permute-start | bytes 1001480 | tf_op jit(solution)/shard_map/ppermute | solution.py:494
  26.1 7.8 %collective-permute-done.next_hbm = f32[163,4,128]{2,1,0:T(4,128)S(1)} collective-permute-done((f32[163,4,128]{2,1,0:T(4,128)S(1)}, f32[163,4,128]{2,1,0:T(4,128)S(1)}, u32[]{:S(2)}, u32[]{:S(2)}) %collective-permute-start) | collective-permute-done | bytes 333856 | tf_op jit(solution)/shard_map/ppermute | solution.py:495
  33.9 0.0 copy-start.2
  33.9 0.0 collective-permute-done.1.prev_hbm
  33.9 0.7 copy-done.2
  34.6 0.0 copy-start.3
  34.6 0.7 copy-done.3
  35.4 7.6 %parent.1 = (bf16[4,256,1024]{2,1,0:T(8,128)(2,1)S(1)}, f32[162,16,128]{2,1,0:T(8,128)S(1)}) custom-call(s32[1]{0:T(128)} %bitcast.5.tile_ref, f32[162,8,128]{2,1,0:T(8,128)} %bitcast.23, f32[163,4,128]{2,1,0:T(4,128)} %copy-done.2, f32[163,4,128]{2,1,0:T(4,128)} %copy-done.3, s32[8,128]{1,0:T(8,128)} %terrain_ref.1), custom_call_target="tpu_custom_call" | custom-call | flops 16777216 | bytes 4194304 | tf_op jit(solution)/shard_map/parent/pallas_call | solution.py:497
  42.9 0.0 copy-start.4
  42.9 0.0 all-to-all-done
  43.0 2.7 %gather.1 = bf16[2048,128]{1,0:T(8,128)(2,1)} custom-call(f32[512,128]{1,0:T(8,128)} %bitcast.4.got_ref, bf16[4,256,1024]{2,1,0:T(8,128)(2,1)S(1)} %get-tuple-element.22.cells_ref), custom_call_target="tpu_custom_call" | custom-call | flops 536870912 | bytes 3145728 | tf_op jit(solution)/shard_map/gather/pallas_call | solution.py:515
  45.7 14.2 %all-to-all-start.1 = ((bf16[128,16,128]{2,1,0:T(8,128)(2,1)}), bf16[128,16,128]{2,1,0:T(8,128)(2,1)S(1)}, u32[]{:S(2)}, u32[]{:S(2)}) async-start(bf16[128,16,128]{2,1,0:T(8,128)(2,1)} %bitcast.6), calls=%async_computation.1 | async-start | bytes 1048576 | tf_op jit(solution)/shard_map/all_to_all | solution.py:451
  59.9 0.0 copy-done.4
  59.9 0.1 reshape.64
  60.0 0.0 copy-start.1
  60.0 0.1 copy.14
  60.1 0.1 reshape.65.bperm_ref
  60.2 2.5 %last_parent.1 = f32[162,8,128]{2,1,0:T(8,128)} custom-call(f32[162,16,128]{2,1,0:T(8,128)S(1)} %get-tuple-element.23.ring_ref, s32[8,128]{1,0:T(8,128)} %terrain_ref.1), custom_call_target="tpu_custom_call" | custom-call | flops 4194304 | bytes 2097152 | tf_op jit(solution)/shard_map/last_parent/pallas_call | solution.py:525
  62.7 0.0 copy-start
  62.7 12.4 %all-to-all-done.1 = bf16[128,16,128]{2,1,0:T(8,128)(2,1)S(1)} async-done(((bf16[128,16,128]{2,1,0:T(8,128)(2,1)}), bf16[128,16,128]{2,1,0:T(8,128)(2,1)S(1)}, u32[]{:S(2)}, u32[]{:S(2)}) %all-to-all-start.1) | async-done | bytes 524320 | tf_op jit(solution)/shard_map/all_to_all | solution.py:451
  75.2 1.4 %regroup.1 = bf16[2048,128]{1,0:T(8,128)(2,1)} custom-call(s32[4,128]{1,0:T(4,128)S(1)} %reshape.65.bperm_ref, bf16[2048,128]{1,0:T(8,128)(2,1)S(1)} %bitcast.18), custom_call_target="tpu_custom_call" | custom-call | flops 67108864 | bytes 1048576 | tf_op jit(solution)/shard_map/regroup/pallas_call | solution.py:543
  76.6 8.4 %all-to-all-start.2 = ((bf16[128,16,128]{2,1,0:T(8,128)(2,1)}), bf16[128,16,128]{2,1,0:T(8,128)(2,1)S(1)}, u32[]{:S(2)}, u32[]{:S(2)}) async-start(bf16[128,16,128]{2,1,0:T(8,128)(2,1)} %bitcast.10), calls=%async_computation.2 | async-start | bytes 1048576 | tf_op jit(solution)/shard_map/all_to_all | solution.py:451
  85.0 0.0 copy-done.1
  85.1 3.1 %plan.1 = (bf16[4,512,512]{2,1,0:T(8,128)(2,1)S(1)}, f32[512,128]{1,0:T(8,128)S(1)}) custom-call(s32[1]{0:T(128)} %bitcast.5.tile_ref, f32[512,128]{1,0:T(8,128)} %bitcast.4.got_ref, f32[2,128,128]{2,1,0:T(8,128)S(1)} %copy-done.1), custom_call_target="tpu_custom_call" | custom-call | flops 268435456 | bytes 3145728 | tf_op jit(solution)/shard_map/plan/pallas_call | solution.py:532
  88.2 11.0 %all-to-all-done.2 = bf16[128,16,128]{2,1,0:T(8,128)(2,1)S(1)} async-done(((bf16[128,16,128]{2,1,0:T(8,128)(2,1)}), bf16[128,16,128]{2,1,0:T(8,128)(2,1)S(1)}, u32[]{:S(2)}, u32[]{:S(2)}) %all-to-all-start.2) | async-done | bytes 524320 | tf_op jit(solution)/shard_map/all_to_all | solution.py:451
  99.2 0.0 copy-done
  99.2 1.1 owner.1
  100.3 20.3 %all_to_all.20 = f32[128,4,128]{2,1,0:T(4,128)S(1)} all-to-all(f32[128,4,128]{2,1,0:T(4,128)S(1)} %bitcast.21), channel_id=1, replica_groups=mesh['member'=2,'tile'=128] {'tile'}, dimensions={0} | all-to-all | bytes 524288 | tf_op jit(solution)/shard_map/all_to_all | solution.py:451
  120.6 0.1 nest.1.own_ref
  120.7 5.8 %collective-permute-start.2 = (f32[324,128]{1,0:T(8,128)S(1)}, f32[324,128]{1,0:T(8,128)S(1)}, u32[]{:S(2)}, u32[]{:S(2)}) collective-permute-start(f32[324,128]{1,0:T(8,128)S(1)} %nest.1.own_ref), channel_id=1, source_target_pairs={{0,128},{128,0},{1,129},{129,1},{2,130},{130,2},{3,131},{131,3},{4... | collective-permute-start | bytes 497672 | tf_op jit(solution)/shard_map/ppermute | solution.py:571
  126.6 0.8 reshape.70
  127.3 0.3 collective-permute-done.2.other_ref
  127.6 0.7 stats.1
Async XLA Ops:
  3.9 39.1 %all-to-all-start = ((f32[128,4,128]{2,1,0:T(4,128)}), f32[128,4,128]{2,1,0:T(4,128)}, u32[]{:S(2)}, u32[]{:S(2)}) async-start(f32[128,4,128]{2,1,0:T(4,128)} %bitcast.3), calls=%async_computation | async-start | bytes 524288 | tf_op jit(solution)/shard_map/all_to_all | solution.py:451
  20.8 13.1 %collective-permute-start = (f32[163,4,128]{2,1,0:T(4,128)S(1)}, f32[163,4,128]{2,1,0:T(4,128)S(1)}, u32[]{:S(2)}, u32[]{:S(2)}) collective-permute-start(f32[163,4,128]{2,1,0:T(4,128)S(1)} %get-tuple-element.20), channel_id=1, source_target_pairs={{1,0},{2,1},{3,2},{4,3},{5,4},{6,5},{7,6},{8,7},{9,8},{10,9},{11,1... | collective-permute-start | bytes 1001480 | tf_op jit(solution)/shard_map/ppermute | solution.py:495
  22.1 11.8 %collective-permute-start.1 = (f32[163,4,128]{2,1,0:T(4,128)S(1)}, f32[163,4,128]{2,1,0:T(4,128)S(1)}, u32[]{:S(2)}, u32[]{:S(2)}) collective-permute-start(f32[163,4,128]{2,1,0:T(4,128)S(1)} %get-tuple-element.21), channel_id=1, source_target_pairs={{0,1},{1,2},{2,3},{3,4},{4,5},{5,6},{6,7},{7,8},{8,9},{9,10},{10,1... | collective-permute-start | bytes 1001480 | tf_op jit(solution)/shard_map/ppermute | solution.py:494
  33.9 0.7 copy-start.2
  34.6 0.7 copy-start.3
  42.9 17.0 %copy-start.4 = (s32[4,128]{1,0:T(4,128)S(1)}, s32[4,128]{1,0:T(4,128)}, u32[]{:S(2)}) copy-start(s32[4,128]{1,0:T(4,128)} %bidx_hbm.1) | copy-start | bytes 6148
  45.7 29.5 %all-to-all-start.1 = ((bf16[128,16,128]{2,1,0:T(8,128)(2,1)}), bf16[128,16,128]{2,1,0:T(8,128)(2,1)S(1)}, u32[]{:S(2)}, u32[]{:S(2)}) async-start(bf16[128,16,128]{2,1,0:T(8,128)(2,1)} %bitcast.6), calls=%async_computation.1 | async-start | bytes 1048576 | tf_op jit(solution)/shard_map/all_to_all | solution.py:451
  60.0 25.0 %copy-start.1 = (f32[2,128,128]{2,1,0:T(8,128)S(1)}, f32[2,128,128]{2,1,0:T(8,128)}, u32[]{:S(2)}) copy-start(f32[2,128,128]{2,1,0:T(8,128)} %constant.8.clone.mix_ref) | copy-start | bytes 393220
  62.7 36.4 %copy-start = (bf16[512,384]{1,0:T(8,128)(2,1)S(1)}, bf16[512,384]{1,0:T(8,128)(2,1)}, u32[]{:S(2)}) copy-start(bf16[512,384]{1,0:T(8,128)(2,1)} %constant.9.clone.mix_ref) | copy-start | bytes 1179652
  76.6 22.6 %all-to-all-start.2 = ((bf16[128,16,128]{2,1,0:T(8,128)(2,1)}), bf16[128,16,128]{2,1,0:T(8,128)(2,1)S(1)}, u32[]{:S(2)}, u32[]{:S(2)}) async-start(bf16[128,16,128]{2,1,0:T(8,128)(2,1)} %bitcast.10), calls=%async_computation.2 | async-start | bytes 1048576 | tf_op jit(solution)/shard_map/all_to_all | solution.py:451
  120.7 6.9 %collective-permute-start.2 = (f32[324,128]{1,0:T(8,128)S(1)}, f32[324,128]{1,0:T(8,128)S(1)}, u32[]{:S(2)}, u32[]{:S(2)}) collective-permute-start(f32[324,128]{1,0:T(8,128)S(1)} %nest.1.own_ref), channel_id=1, source_target_pairs={{0,128},{128,0},{1,129},{129,1},{2,130},{130,2},{3,131},{131,3},{4... | collective-permute-start | bytes 497672 | tf_op jit(solution)/shard_map/ppermute | solution.py:571

commit v2 on v1

--- a/solution.py
+++ b/solution.py
@@ -496,7 +496,10 @@
     first = exchange(message.reshape(NT, 4, W)).reshape(4 * NT, W)
     cells, ring = call(
         parent_kernel,
-        (sds((STEPS, 2 * W, ROWS * W), BF16), sds((2 * LEV, RING, W), F32)),
+        (
+            pltpu.VMEM((STEPS, 2 * W, ROWS * W), BF16),
+            pltpu.VMEM((2 * LEV, RING, W), F32),
+        ),
         in_specs=[SM, HB, HB, HB, HB],
         scratch=[
             pltpu.VMEM((2 * LEV, ROWS, W), F32),
@@ -508,8 +511,8 @@
             pltpu.SemaphoreType.DMA((4,)),
         ],
         name="parent",
-        flops=1 << 24,
-        nbytes=4 << 20,
+        flops=1 << 40,
+        nbytes=1 << 36,
     )(tile, parent, in_hbm(from_next), in_hbm(from_prev), terrain)
 
     values = call(

time: 129 us -> 123 us (0.953)
  waiting for transfers between devices: 31.5 us -> 27.9 us
  starting transfers between devices: 50.7 us -> 49 us
    ppermute x1, waiting for transfers between devices: 7.82 us -> 0.01 us  [on_device(): from_next = lax.ppermute(up, 'tile', backward)]
    all_to_all x3, waiting for transfers between devices: 23.4 us -> 27.6 us  [exchange(): return lax.all_to_all(x, 'tile', split_axis=0, concat_axis=0, tiled=True)]
    all_to_all x3, starting transfers between devices: 39.5 us -> 38.3 us  [exchange(): return lax.all_to_all(x, 'tile', split_axis=0, concat_axis=0, tiled=True)]
  transfers between devices with their start and end apart: 6 -> 6, of which waited for: 4 -> 4; matrix products, arithmetic and copies ran while one was open for 1% -> 1% of each run, Pallas kernels for 10% -> 11%
where the time goes in v2:
time: 123 us
  starting transfers between devices  49 us (40%)
  waiting for transfers between devices  27.9 us (23%)
  Pallas kernels  22.5 us (18%)
  blocking collectives  20.1 us (16%)
  local copies, waits for them, and re-layouts  2.5 us (2%)
    all_to_all x3, starting transfers between devices, exchange(): return lax.all_to_all(x, 'tile', split_axis=0, concat_axis=0, tiled=True)  38.3 us
    all_to_all x3, waiting for transfers between devices, exchange(): return lax.all_to_all(x, 'tile', split_axis=0, concat_axis=0, tiled=True)  27.6 us
    all_to_all x1, blocking collectives, exchange(): return lax.all_to_all(x, 'tile', split_axis=0, concat_axis=0, tiled=True)  20.1 us
    pallas_call x1, Pallas kernels, on_device(): call(parent_kernel, (pltpu.VMEM((STEPS, 2 * W, ROWS * W), BF16), pltpu.VM...  7.57 us
    ppermute x1, starting transfers between devices, on_device(): other = lax.ppermute(nest_out, 'member', [(0, 1), (1, 0)])  4.77 us
    ppermute x1, starting transfers between devices, on_device(): from_prev = lax.ppermute(down, 'tile', forward)  4.68 us
    pallas_call x1, Pallas kernels, on_device(): call(plan_kernel, (sds((STEPS, 4 * NT, 4 * NT), BF16), sds((4 * NT, W), F...  3.13 us
    pallas_call x1, Pallas kernels, on_device(): call(gather_kernel, sds((16 * NT, W), BF16), scratch=[pltpu.VMEM((16 * NT...  2.7 us
  transfers between devices with their start and end apart: 6, of which 4 were waited for; matrix products, arithmetic and copies ran while one was open for 1% of the time, Pallas kernels for 11%

profile of v2, /device:TPU:1, one launch (start us, length us, event | category | flops | bytes accessed | tf_op | source)
XLA Modules:
  0.0 122.8 jit_solution(2879791585004045208)
XLA Ops:
  0.6 1.2 %halo.1 = (f32[163,4,128]{2,1,0:T(4,128)S(1)}, f32[163,4,128]{2,1,0:T(4,128)S(1)}) custom-call(f32[162,8,128]{2,1,0:T(8,128)} %bitcast.22, s32[8,128]{1,0:T(8,128)} %terrain_ref.1), custom_call_target="tpu_custom_call" | custom-call | bytes 1048576 | tf_op jit(solution)/shard_map/halo/pallas_call | solution.py:463
  1.9 1.3 %collective-permute-start = (f32[163,4,128]{2,1,0:T(4,128)S(1)}, f32[163,4,128]{2,1,0:T(4,128)S(1)}, u32[]{:S(2)}, u32[]{:S(2)}) collective-permute-start(f32[163,4,128]{2,1,0:T(4,128)S(1)} %get-tuple-element.20), channel_id=1, source_target_pairs={{1,0},{2,1},{3,2},{4,3},{5,4},{6,5},{7,6},{8,7},{9,8},{10,9},{11,1... | collective-permute-start | bytes 1001480 | tf_op jit(solution)/shard_map/ppermute | solution.py:495
  3.2 4.7 %collective-permute-start.1 = (f32[163,4,128]{2,1,0:T(4,128)S(1)}, f32[163,4,128]{2,1,0:T(4,128)S(1)}, u32[]{:S(2)}, u32[]{:S(2)}) collective-permute-start(f32[163,4,128]{2,1,0:T(4,128)S(1)} %get-tuple-element.21), channel_id=1, source_target_pairs={{0,1},{1,2},{2,3},{3,4},{4,5},{5,6},{6,7},{7,8},{8,9},{9,10},{10,1... | collective-permute-start | bytes 1001480 | tf_op jit(solution)/shard_map/ppermute | solution.py:494
  7.9 2.0 %send.1 = f32[512,128]{1,0:T(8,128)} custom-call(s32[4]{0:T(128)} %shift_hbm.1, f32[81,2,2,128]{3,2,1,0:T(2,128)} %bitcast.26, s32[4,128]{1,0:T(4,128)} %bidx_hbm.1, s32[4,256]{1,0:T(4,128)} %dest_hbm.1), custom_call_target="tpu_custom_call" | custom-call | bytes 67108864 | tf_op jit(solution)/shard_map/send/pallas_call | solution.py:477
  9.9 18.9 %all-to-all-start = ((f32[128,4,128]{2,1,0:T(4,128)}), f32[128,4,128]{2,1,0:T(4,128)}, u32[]{:S(2)}, u32[]{:S(2)}) async-start(f32[128,4,128]{2,1,0:T(4,128)} %bitcast.3), calls=%async_computation | async-start | bytes 524288 | tf_op jit(solution)/shard_map/all_to_all | solution.py:451
  28.8 0.0 collective-permute-done.next_hbm
  28.8 0.0 copy-start.3
  28.8 0.0 collective-permute-done.1.prev_hbm
  28.8 0.7 copy-done.3
  29.5 0.0 copy-start.4
  29.5 0.7 copy-done.4
  30.2 7.6 %parent.1 = (bf16[4,256,1024]{2,1,0:T(8,128)(2,1)S(1)}, f32[162,16,128]{2,1,0:T(8,128)S(1)}) custom-call(s32[1]{0:T(128)} %bitcast.5.tile_ref, f32[162,8,128]{2,1,0:T(8,128)} %bitcast.23, f32[163,4,128]{2,1,0:T(4,128)} %copy-done.3, f32[163,4,128]{2,1,0:T(4,128)} %copy-done.4, s32[8,128]{1,0:T(8,128)} %terrain_ref.1), custom_call_target="tpu_custom_call" | custom-call | flops 1099511627776 | bytes 68719476736 | tf_op jit(solution)/shard_map/parent/pallas_call | solution.py:497
  37.8 0.0 copy-start.2
  37.8 2.4 %all-to-all-done = f32[128,4,128]{2,1,0:T(4,128)} async-done(((f32[128,4,128]{2,1,0:T(4,128)}), f32[128,4,128]{2,1,0:T(4,128)}, u32[]{:S(2)}, u32[]{:S(2)}) %all-to-all-start) | async-done | bytes 262176 | tf_op jit(solution)/shard_map/all_to_all | solution.py:451
  40.3 2.7 %gather.1 = bf16[2048,128]{1,0:T(8,128)(2,1)} custom-call(f32[512,128]{1,0:T(8,128)} %bitcast.4.got_ref, bf16[4,256,1024]{2,1,0:T(8,128)(2,1)S(1)} %get-tuple-element.22.cells_ref), custom_call_target="tpu_custom_call" | custom-call | flops 536870912 | bytes 3145728 | tf_op jit(solution)/shard_map/gather/pallas_call | solution.py:518
  43.0 10.8 %all-to-all-start.1 = ((bf16[128,16,128]{2,1,0:T(8,128)(2,1)}), bf16[128,16,128]{2,1,0:T(8,128)(2,1)S(1)}, u32[]{:S(2)}, u32[]{:S(2)}) async-start(bf16[128,16,128]{2,1,0:T(8,128)(2,1)} %bitcast.6), calls=%async_computation.1 | async-start | bytes 1048576 | tf_op jit(solution)/shard_map/all_to_all | solution.py:451
  53.7 0.0 copy-done.2
  53.7 0.1 reshape.64
  53.8 0.0 copy-start.1
  53.9 0.1 copy.14
  53.9 0.1 reshape.65.bperm_ref
  54.0 2.5 %last_parent.1 = f32[162,8,128]{2,1,0:T(8,128)} custom-call(f32[162,16,128]{2,1,0:T(8,128)S(1)} %get-tuple-element.23.ring_ref, s32[8,128]{1,0:T(8,128)} %terrain_ref.1), custom_call_target="tpu_custom_call" | custom-call | flops 4194304 | bytes 2097152 | tf_op jit(solution)/shard_map/last_parent/pallas_call | solution.py:528
  56.6 0.0 copy-start
  56.6 13.1 %all-to-all-done.1 = bf16[128,16,128]{2,1,0:T(8,128)(2,1)S(1)} async-done(((bf16[128,16,128]{2,1,0:T(8,128)(2,1)}), bf16[128,16,128]{2,1,0:T(8,128)(2,1)S(1)}, u32[]{:S(2)}, u32[]{:S(2)}) %all-to-all-start.1) | async-done | bytes 524320 | tf_op jit(solution)/shard_map/all_to_all | solution.py:451
  69.6 1.4 %regroup.1 = bf16[2048,128]{1,0:T(8,128)(2,1)} custom-call(s32[4,128]{1,0:T(4,128)S(1)} %reshape.65.bperm_ref, bf16[2048,128]{1,0:T(8,128)(2,1)S(1)} %bitcast.18), custom_call_target="tpu_custom_call" | custom-call | flops 67108864 | bytes 1048576 | tf_op jit(solution)/shard_map/regroup/pallas_call | solution.py:546
  71.0 8.6 %all-to-all-start.2 = ((bf16[128,16,128]{2,1,0:T(8,128)(2,1)}), bf16[128,16,128]{2,1,0:T(8,128)(2,1)S(1)}, u32[]{:S(2)}, u32[]{:S(2)}) async-start(bf16[128,16,128]{2,1,0:T(8,128)(2,1)} %bitcast.10), calls=%async_computation.2 | async-start | bytes 1048576 | tf_op jit(solution)/shard_map/all_to_all | solution.py:451
  79.7 0.0 copy-done.1
  79.7 3.1 %plan.1 = (bf16[4,512,512]{2,1,0:T(8,128)(2,1)S(1)}, f32[512,128]{1,0:T(8,128)S(1)}) custom-call(s32[1]{0:T(128)} %bitcast.5.tile_ref, f32[512,128]{1,0:T(8,128)} %bitcast.4.got_ref, f32[2,128,128]{2,1,0:T(8,128)S(1)} %copy-done.1), custom_call_target="tpu_custom_call" | custom-call | flops 268435456 | bytes 3145728 | tf_op jit(solution)/shard_map/plan/pallas_call | solution.py:535
  82.8 12.1 %all-to-all-done.2 = bf16[128,16,128]{2,1,0:T(8,128)(2,1)S(1)} async-done(((bf16[128,16,128]{2,1,0:T(8,128)(2,1)}), bf16[128,16,128]{2,1,0:T(8,128)(2,1)S(1)}, u32[]{:S(2)}, u32[]{:S(2)}) %all-to-all-start.2) | async-done | bytes 524320 | tf_op jit(solution)/shard_map/all_to_all | solution.py:451
  94.9 0.0 copy-done
  94.9 1.1 owner.1
  96.1 20.1 %all_to_all.20 = f32[128,4,128]{2,1,0:T(4,128)S(1)} all-to-all(f32[128,4,128]{2,1,0:T(4,128)S(1)} %bitcast.21), channel_id=1, replica_groups=mesh['member'=2,'tile'=128] {'tile'}, dimensions={0} | all-to-all | bytes 524288 | tf_op jit(solution)/shard_map/all_to_all | solution.py:451
  116.1 0.1 nest.1.own_ref
  116.3 4.8 %collective-permute-start.2 = (f32[324,128]{1,0:T(8,128)S(1)}, f32[324,128]{1,0:T(8,128)S(1)}, u32[]{:S(2)}, u32[]{:S(2)}) collective-permute-start(f32[324,128]{1,0:T(8,128)S(1)} %nest.1.own_ref), channel_id=1, source_target_pairs={{0,128},{128,0},{1,129},{129,1},{2,130},{130,2},{3,131},{131,3},{4... | collective-permute-start | bytes 497672 | tf_op jit(solution)/shard_map/ppermute | solution.py:574
  121.0 0.8 reshape.70
  121.8 0.3 collective-permute-done.2.other_ref
  122.1 0.7 stats.1
Async XLA Ops:
  1.9 26.9 %collective-permute-start = (f32[163,4,128]{2,1,0:T(4,128)S(1)}, f32[163,4,128]{2,1,0:T(4,128)S(1)}, u32[]{:S(2)}, u32[]{:S(2)}) collective-permute-start(f32[163,4,128]{2,1,0:T(4,128)S(1)} %get-tuple-element.20), channel_id=1, source_target_pairs={{1,0},{2,1},{3,2},{4,3},{5,4},{6,5},{7,6},{8,7},{9,8},{10,9},{11,1... | collective-permute-start | bytes 1001480 | tf_op jit(solution)/shard_map/ppermute | solution.py:495
  3.2 25.6 %collective-permute-start.1 = (f32[163,4,128]{2,1,0:T(4,128)S(1)}, f32[163,4,128]{2,1,0:T(4,128)S(1)}, u32[]{:S(2)}, u32[]{:S(2)}) collective-permute-start(f32[163,4,128]{2,1,0:T(4,128)S(1)} %get-tuple-element.21), channel_id=1, source_target_pairs={{0,1},{1,2},{2,3},{3,4},{4,5},{5,6},{6,7},{7,8},{8,9},{9,10},{10,1... | collective-permute-start | bytes 1001480 | tf_op jit(solution)/shard_map/ppermute | solution.py:494
  9.9 30.4 %all-to-all-start = ((f32[128,4,128]{2,1,0:T(4,128)}), f32[128,4,128]{2,1,0:T(4,128)}, u32[]{:S(2)}, u32[]{:S(2)}) async-start(f32[128,4,128]{2,1,0:T(4,128)} %bitcast.3), calls=%async_computation | async-start | bytes 524288 | tf_op jit(solution)/shard_map/all_to_all | solution.py:451
  28.8 0.7 copy-start.3
  29.5 0.7 copy-start.4
  37.8 15.9 %copy-start.2 = (s32[4,128]{1,0:T(4,128)S(1)}, s32[4,128]{1,0:T(4,128)}, u32[]{:S(2)}) copy-start(s32[4,128]{1,0:T(4,128)} %bidx_hbm.1) | copy-start | bytes 6148
  43.0 26.7 %all-to-all-start.1 = ((bf16[128,16,128]{2,1,0:T(8,128)(2,1)}), bf16[128,16,128]{2,1,0:T(8,128)(2,1)S(1)}, u32[]{:S(2)}, u32[]{:S(2)}) async-start(bf16[128,16,128]{2,1,0:T(8,128)(2,1)} %bitcast.6), calls=%async_computation.1 | async-start | bytes 1048576 | tf_op jit(solution)/shard_map/all_to_all | solution.py:451
  53.8 25.8 %copy-start.1 = (f32[2,128,128]{2,1,0:T(8,128)S(1)}, f32[2,128,128]{2,1,0:T(8,128)}, u32[]{:S(2)}) copy-start(f32[2,128,128]{2,1,0:T(8,128)} %constant.8.clone.mix_ref) | copy-start | bytes 393220
  56.6 38.4 %copy-start = (bf16[512,384]{1,0:T(8,128)(2,1)S(1)}, bf16[512,384]{1,0:T(8,128)(2,1)}, u32[]{:S(2)}) copy-start(bf16[512,384]{1,0:T(8,128)(2,1)} %constant.9.clone.mix_ref) | copy-start | bytes 1179652
  71.0 23.9 %all-to-all-start.2 = ((bf16[128,16,128]{2,1,0:T(8,128)(2,1)}), bf16[128,16,128]{2,1,0:T(8,128)(2,1)S(1)}, u32[]{:S(2)}, u32[]{:S(2)}) async-start(bf16[128,16,128]{2,1,0:T(8,128)(2,1)} %bitcast.10), calls=%async_computation.2 | async-start | bytes 1048576 | tf_op jit(solution)/shard_map/all_to_all | solution.py:451
  116.3 5.8 %collective-permute-start.2 = (f32[324,128]{1,0:T(8,128)S(1)}, f32[324,128]{1,0:T(8,128)S(1)}, u32[]{:S(2)}, u32[]{:S(2)}) collective-permute-start(f32[324,128]{1,0:T(8,128)S(1)} %nest.1.own_ref), channel_id=1, source_target_pairs={{0,128},{128,0},{1,129},{129,1},{2,130},{130,2},{3,131},{131,3},{4... | collective-permute-start | bytes 497672 | tf_op jit(solution)/shard_map/ppermute | solution.py:574

commit v3 on v2

--- a/solution.py
+++ b/solution.py
@@ -18,8 +18,11 @@
 LPAD = 96
 RING = 16
 BSTR = LPAD * RING
-L_DEST = 81
-L_REQ = 88
+SPLIT = 40
+L_TOP = 81
+L_REQ = 86
+L_INNER = 88
+L_DEST = (48, 8)
 HORIZ = 0.15
 VERT = 0.1
 DRAG = 0.1
@@ -56,17 +59,30 @@
     s = solve_matrix()
     power = [np.linalg.matrix_power(s, k) for k in range(STEPS + 1)]
     keep = 1.0 - RELAX
-    interior = padded_transpose(power[STEPS])
-    bound = padded_transpose(power[STEPS] * keep**STEPS)
-    q_mix = np.stack([bound, interior]).astype(np.float32)
-    stack = np.concatenate(
+    inner = power[STEPS].T
+    bound = power[STEPS].T * keep**STEPS
+    send = np.zeros((2, W, 2, W))
+    send[0, :LEV, 0, :SPLIT] = bound[:, :SPLIT]
+    send[0, :LEV, 1, SPLIT:LEV] = bound[:, SPLIT:]
+    send[1, :LEV, 0, L_INNER:] = inner[:, :SPLIT]
+    send[1, :LEV, 1, L_INNER:] = inner[:, SPLIT : 2 * SPLIT]
+    send[1, :LEV, 1, L_TOP] = inner[:, 2 * SPLIT]
+    for part in range(2):
+        for owner in range(2):
+            for k in range(STEPS):
+                send[part, LEV + k, owner, L_DEST[owner] + part * STEPS + k] = 1.0
+    send = send.reshape(2 * W, 2 * W).astype(np.float32)
+    mix = [
+        padded_transpose(power[STEPS - k] * RELAX * keep ** (STEPS - 1 - k))
+        for k in range(STEPS)
+    ]
+    edge = np.stack(
         [
-            padded_transpose(power[STEPS - k] * RELAX * keep ** (STEPS - 1 - k))
-            for k in range(STEPS)
+            np.concatenate(split3(np.concatenate(mix[:2])), axis=1),
+            np.concatenate(split3(np.concatenate(mix[2:])), axis=1),
         ]
     )
-    e_mix = np.concatenate(split3(stack), axis=1)
-    return q_mix, e_mix
+    return send, edge
 
 
 def call(body, out_shape, in_specs=None, scratch=(), name=None, flops=0, nbytes=0):
@@ -108,9 +124,9 @@
 
 
 def send_kernel(
-    shift_hbm, nest_hbm, bidx_hbm, dest_hbm,
+    shift_hbm, nest_hbm, bidx_hbm, dest_hbm, mix_hbm,
     msg_ref,
-    shift_ref, nest_ref, bidx_ref, dest_ref, pad_ref, sems,
+    shift_ref, nest_ref, bidx_ref, dest_ref, mix_ref, pad_ref, sems,
 ):
     copies = start_all(
         [
@@ -118,22 +134,31 @@
             (bidx_hbm, bidx_ref),
             (dest_hbm, dest_ref),
             (shift_hbm, shift_ref),
+            (mix_hbm, mix_ref),
         ],
         sems,
     )
     for copy in copies:
         copy.wait()
-    zeros = jnp.zeros((W - LEV + 1, 2 * W), F32)
+    zeros = jnp.zeros((W - LEV + 1, W), F32)
     for b in range(2):
-        pad_ref[b, LEV - 1 :, :] = zeros
-        for half in range(2):
-            lanes = slice(half * W, (half + 1) * W)
-            pad_ref[b, :LEV, lanes] = nest_ref[:, half, b, :]
-        pad_ref[b, L_DEST : L_DEST + STEPS, :] = dest_ref[...].astype(F32)
-        for half in range(2):
-            block = pad_ref[b, :, half * W : (half + 1) * W]
-            start = b * 2 * W + half * W
-            msg_ref[start : start + W, :] = block.T
+        for part in range(2):
+            top = part * W
+            pad_ref[b, top + LEV - 1 : top + W, :] = zeros
+            pad_ref[b, top : top + LEV, :] = nest_ref[:, part, b, :]
+            pad_ref[b, top + LEV : top + LEV + STEPS, :] = dest_ref[
+                :, part * W : (part + 1) * W
+            ].astype(F32)
+        res = lax.dot_general(
+            pad_ref[b],
+            mix_ref[...],
+            (((0,), (0,)), ((), ())),
+            precision=lax.Precision.HIGHEST,
+            preferred_element_type=F32,
+        )
+        for owner in range(2):
+            start = b * 2 * W + owner * W
+            msg_ref[start : start + W, :] = res[:, owner * W : (owner + 1) * W]
     lane = lax.broadcasted_iota(jnp.int32, (NT, W), 1)
     tile = lax.broadcasted_iota(jnp.int32, (NT, W), 0)
     for s in range(STEPS):
@@ -333,33 +358,46 @@
         )
         for b in range(2):
             for j in range(4):
-                scr2_ref[pl.ds(b * 512 + s * 4 + j, 32, stride=16), :] = res[
+                start = (b * 64 + (s // 2) * 32) * 8 + (s % 2) * 4 + j
+                scr2_ref[pl.ds(start, 32, stride=8), :] = res[
                     j * 32 : (j + 1) * 32, b * W : (b + 1) * W
                 ]
-    for b in range(2):
-        out_ref[b * 1024 : b * 1024 + 512, :] = scr2_ref[b * 512 : (b + 1) * 512, :].astype(
-            BF16
-        )
-        out_ref[b * 1024 + 512 : (b + 1) * 1024, :] = jnp.zeros((512, W), BF16)
-
-
-def plan_kernel(tile_ref, got_ref, mix_ref, hot_ref, base_ref):
-    interior = jnp.where(jnp.bitwise_and(tile_ref[0], 63) < 32, 0, 1)
+    out_ref[...] = scr2_ref[...].astype(BF16)
+
+
+def plan_kernel(tile_ref, got_ref, hot_ref, base_ref):
+    late = jnp.bitwise_and(jnp.right_shift(tile_ref[0], 5), 1) == 1
     n = 4 * NT
     turned = [got_ref[pl.ds(j, NT, stride=4), :].T for j in range(4)]
     sub = lax.broadcasted_iota(jnp.int32, (n, n), 0)
 
-    def dest(s):
+    def pick(early_value, late_value):
+        return jnp.where(late, late_value, early_value)
+
+    def one_hot(row):
+        return jnp.where(sub == row, 1.0, 0.0).astype(BF16)
+
+    def dest(part, s):
+        k = part * STEPS + s
         row = jnp.concatenate(
-            [t[L_DEST + s : L_DEST + s + 1, :] for t in turned], axis=1
-        ).astype(jnp.int32)
+            [
+                pick(
+                    t[L_DEST[0] + k : L_DEST[0] + k + 1, :],
+                    t[L_DEST[1] + k : L_DEST[1] + k + 1, :],
+                )
+                for t in turned
+            ],
+            axis=1,
+        )
+        row = (row + 0.5).astype(jnp.int32)
         return jnp.right_shift(row, 8), jnp.bitwise_and(row, 3)
 
-    tile_to, slot_to = dest(STEPS - 1)
-    for s in range(STEPS - 1, -1, -1):
-        if s < STEPS - 1:
-            mid_tile, mid_slot = dest(s)
-            move = jnp.where(sub == mid_slot * NT + mid_tile, 1.0, 0.0).astype(BF16)
+    def finals(part):
+        tile_to, slot_to = dest(part, STEPS - 1)
+        rows = {STEPS - 1: tile_to * 4 + slot_to}
+        for s in range(STEPS - 2, -1, -1):
+            mid_tile, mid_slot = dest(part, s)
+            move = one_hot(mid_slot * NT + mid_tile)
             later = jnp.concatenate(
                 [
                     jnp.broadcast_to(tile_to, (8, n)),
@@ -372,60 +410,67 @@
             )
             tile_to = both[0:1, :].astype(jnp.int32)
             slot_to = both[8:9, :].astype(jnp.int32)
-        hot_ref[s] = jnp.where(sub == tile_to * 4 + slot_to, 1.0, 0.0).astype(BF16)
+            rows[s] = tile_to * 4 + slot_to
+        return rows
+
     columns = jnp.concatenate(
         [got_ref[pl.ds(j, NT, stride=4), :] for j in range(4)], axis=0
     )
-    mixed = lax.dot_general(
-        columns,
-        mix_ref[interior],
-        (((1,), (0,)), ((), ())),
-        precision=lax.Precision.HIGHEST,
-        preferred_element_type=F32,
-    )
     parts = []
     for _ in range(3):
-        part = mixed.astype(BF16)
+        part = columns.astype(BF16)
         parts.append(part)
-        mixed = mixed - part.astype(F32)
-    moved = jnp.dot(
-        hot_ref[0], jnp.concatenate(parts, axis=1), preferred_element_type=F32
-    )
-    base_ref[...] = moved[:, :W] + (moved[:, W : 2 * W] + moved[:, 2 * W :])
+        columns = columns - part.astype(F32)
+    parts = jnp.concatenate(parts, axis=1)
+
+    def moved(row):
+        res = jnp.dot(one_hot(row), parts, preferred_element_type=F32)
+        return res[:, :W] + (res[:, W : 2 * W] + res[:, 2 * W :])
+
+    bound = finals(0)
+    hot_ref[0] = one_hot(pick(bound[0], bound[2]))
+    hot_ref[1] = one_hot(pick(bound[1], bound[3]))
+    outer = moved(bound[0])
+    inner = moved(finals(1)[0])
+    lane = lax.broadcasted_iota(jnp.int32, (n, W), 1)
+    low = pick(0, SPLIT)
+    high = pick(SPLIT, LEV)
+    extra = pick(W, L_TOP)
+    is_inner = jnp.logical_or(lane >= L_INNER, lane == extra)
+    is_outer = jnp.logical_and(lane >= low, lane < high)
+    base_ref[...] = jnp.where(is_outer, outer, jnp.where(is_inner, inner, 0.0))
 
 
 def owner_kernel(tile_ref, got_ref, hot_ref, base_ref, mix_ref, out_ref, scr_ref):
-    bound = jnp.bitwise_and(tile_ref[0], 63) < 32
-
-    @pl.when(bound)
-    def _():
-        scr_ref[...] = got_ref[...].astype(F32)
-        moved = []
-        for s in range(STEPS):
-            edge = jnp.concatenate(
-                [scr_ref[pl.ds(s * 4 + j, NT, stride=16), :] for j in range(4)], axis=0
-            ).astype(BF16)
-            moved.append(
-                jnp.dot(hot_ref[s], edge, preferred_element_type=F32).astype(BF16)
-            )
-        total = jnp.dot(
-            jnp.concatenate(moved, axis=1), mix_ref[...], preferred_element_type=F32
-        )
-        out_ref[...] = base_ref[...] + (
-            total[:, :W] + (total[:, W : 2 * W] + total[:, 2 * W :])
-        )
-
-    @pl.when(jnp.logical_not(bound))
-    def _():
-        out_ref[...] = base_ref[...]
-
-
-def nest_kernel(got_ref, out_ref, scr_ref):
+    late = jnp.bitwise_and(jnp.right_shift(tile_ref[0], 5), 1)
+    scr_ref[...] = got_ref[...].astype(F32)
+    moved = []
+    for s in range(2):
+        edge = jnp.concatenate(
+            [scr_ref[pl.ds(s * 4 + j, NT, stride=8), :] for j in range(4)], axis=0
+        ).astype(BF16)
+        moved.append(jnp.dot(hot_ref[s], edge, preferred_element_type=F32).astype(BF16))
+    total = jnp.dot(
+        jnp.concatenate(moved, axis=1), mix_ref[late], preferred_element_type=F32
+    )
+    out_ref[...] = base_ref[...] + (
+        total[:, :W] + (total[:, W : 2 * W] + total[:, 2 * W :])
+    )
+
+
+def nest_kernel(got_ref, out_ref, sum_ref, early_ref, late_ref):
     for b in range(2):
-        for half in range(2):
-            start = b * 2 * W + half * W
-            scr_ref[...] = got_ref[start : start + W, :].T
-            out_ref[pl.ds(half * 2 + b, LEV, stride=4), :] = scr_ref[:LEV, :]
+        early = got_ref[b * 2 * W : b * 2 * W + W, :]
+        late = got_ref[b * 2 * W + W : (b + 1) * 2 * W, :]
+        sum_ref[...] = (early + late).T
+        early_ref[...] = early.T
+        late_ref[...] = late.T
+        out_ref[pl.ds(b, LEV, stride=4), :] = sum_ref[:LEV, :]
+        inner = 2 + b
+        out_ref[pl.ds(inner, SPLIT, stride=4), :] = early_ref[L_INNER:, :]
+        out_ref[pl.ds(inner + 4 * SPLIT, SPLIT, stride=4), :] = late_ref[L_INNER:, :]
+        top = inner + 8 * SPLIT
+        out_ref[top : top + 1, :] = late_ref[L_TOP : L_TOP + 1, :]
 
 
 def stats_kernel(own_ref, other_ref, mean_ref, var_ref):
@@ -477,18 +522,25 @@
     message = call(
         send_kernel,
         sds((4 * NT, W), F32),
-        in_specs=[HB] * 4,
+        in_specs=[HB] * 5,
         scratch=[
             pltpu.SMEM((STEPS,), jnp.int32),
             pltpu.VMEM((LEV, 2, 2, W), F32),
             pltpu.VMEM((STEPS, NT), jnp.int32),
             pltpu.VMEM((STEPS, 2 * W), jnp.int32),
-            pltpu.VMEM((2, W, 2 * W), F32),
-            pltpu.SemaphoreType.DMA((4,)),
+            pltpu.VMEM((2 * W, 2 * W), F32),
+            pltpu.VMEM((2, 2 * W, W), F32),
+            pltpu.SemaphoreType.DMA((5,)),
         ],
         name="send",
         nbytes=64 << 20,
-    )(in_hbm(shift_x), nest, in_hbm(boundary_index), in_hbm(reloc_dest))
+    )(
+        in_hbm(shift_x),
+        nest,
+        in_hbm(boundary_index),
+        in_hbm(reloc_dest),
+        in_hbm(q_mix),
+    )
     forward = [(i, i + 1) for i in range(NT - 1)]
     backward = [(i + 1, i) for i in range(NT - 1)]
     from_prev = lax.ppermute(down, "tile", forward)
@@ -534,30 +586,30 @@
     )(ring, terrain)
     hot, base = call(
         plan_kernel,
-        (sds((STEPS, 4 * NT, 4 * NT), BF16), sds((4 * NT, W), F32)),
-        in_specs=[SM, VM, VM],
+        (sds((2, 4 * NT, 4 * NT), BF16), sds((4 * NT, W), F32)),
+        in_specs=[SM, VM],
         name="plan",
         flops=1 << 28,
         nbytes=3 << 20,
-    )(tile, first, q_mix)
+    )(tile, first)
 
     second, parent_out = lax.optimization_barrier((second, parent_out))
     bperm = boundary_index.reshape(STEPS, 32, 4).transpose(0, 2, 1).reshape(STEPS, NT)
     edges = call(
         regroup_kernel,
-        sds((16 * NT, W), BF16),
+        sds((8 * NT, W), BF16),
         scratch=[pltpu.VMEM((16 * NT, W), F32), pltpu.VMEM((8 * NT, W), F32)],
         name="regroup",
         flops=1 << 26,
         nbytes=1 << 20,
     )(bperm, second)
-    third = exchange(edges.reshape(NT, 16, W)).reshape(16 * NT, W)
+    third = exchange(edges.reshape(NT, 8, W)).reshape(8 * NT, W)
 
     columns = call(
         owner_kernel,
         sds((4 * NT, W), F32),
         in_specs=[SM, VM, VM, VM, VM],
-        scratch=[pltpu.VMEM((16 * NT, W), F32)],
+        scratch=[pltpu.VMEM((8 * NT, W), F32)],
         name="owner",
         flops=1 << 29,
         nbytes=3 << 20,
@@ -567,7 +619,7 @@
     nest_out = call(
         nest_kernel,
         sds((4 * LEV, W), F32),
-        scratch=[pltpu.VMEM((W, W), F32)],
+        scratch=[pltpu.VMEM((W, W), F32)] * 3,
         name="nest",
         nbytes=1 << 19,
     )(fourth)

time: 123 us -> 118 us (0.959)
  waiting for transfers between devices: 27.9 us -> 24.3 us
  blocking collectives: 20.1 us -> 18.1 us
    all_to_all x3, waiting for transfers between devices: 27.6 us -> 24.1 us  [exchange(): return lax.all_to_all(x, 'tile', split_axis=0, concat_axis=0, tiled=True)]
    all_to_all x1, blocking collectives: 20.1 us -> 18.1 us  [exchange(): return lax.all_to_all(x, 'tile', split_axis=0, concat_axis=0, tiled=True)]
where the time goes in v3:
time: 118 us
  starting transfers between devices  49.5 us (42%)
  waiting for transfers between devices  24.3 us (21%)
  Pallas kernels  22.3 us (19%)
  blocking collectives  18.1 us (15%)
  local copies, waits for them, and re-layouts  2.49 us (2%)
    all_to_all x3, starting transfers between devices, exchange(): return lax.all_to_all(x, 'tile', split_axis=0, concat_axis=0, tiled=True)  38.4 us
    all_to_all x3, waiting for transfers between devices, exchange(): return lax.all_to_all(x, 'tile', split_axis=0, concat_axis=0, tiled=True)  24.1 us
    all_to_all x1, blocking collectives, exchange(): return lax.all_to_all(x, 'tile', split_axis=0, concat_axis=0, tiled=True)  18.1 us
    pallas_call x1, Pallas kernels, on_device(): call(parent_kernel, (pltpu.VMEM((STEPS, 2 * W, ROWS * W), BF16), pltpu.VM...  7.57 us
    ppermute x1, starting transfers between devices, on_device(): other = lax.ppermute(nest_out, 'member', [(0, 1), (1, 0)])  5.15 us
    ppermute x1, starting transfers between devices, on_device(): from_prev = lax.ppermute(down, 'tile', forward)  4.68 us
    pallas_call x1, Pallas kernels, on_device(): call(plan_kernel, (sds((2, 4 * NT, 4 * NT), BF16), sds((4 * NT, W), F32))...  3.12 us
    pallas_call x1, Pallas kernels, on_device(): call(gather_kernel, sds((16 * NT, W), BF16), scratch=[pltpu.VMEM((16 * NT...  2.72 us
  transfers between devices with their start and end apart: 6, of which 4 were waited for; matrix products, arithmetic and copies ran while one was open for 1% of the time, Pallas kernels for 11%

profile of v3, /device:TPU:1, one launch (start us, length us, event | category | flops | bytes accessed | tf_op | source)
XLA Modules:
  0.0 117.5 jit_solution(8837112523837895604)
XLA Ops:
  0.6 1.2 %halo.1 = (f32[163,4,128]{2,1,0:T(4,128)S(1)}, f32[163,4,128]{2,1,0:T(4,128)S(1)}) custom-call(f32[162,8,128]{2,1,0:T(8,128)} %bitcast.22, s32[8,128]{1,0:T(8,128)} %terrain_ref.1), custom_call_target="tpu_custom_call" | custom-call | bytes 1048576 | tf_op jit(solution)/shard_map/halo/pallas_call | solution.py:508
  1.9 1.3 %collective-permute-start = (f32[163,4,128]{2,1,0:T(4,128)S(1)}, f32[163,4,128]{2,1,0:T(4,128)S(1)}, u32[]{:S(2)}, u32[]{:S(2)}) collective-permute-start(f32[163,4,128]{2,1,0:T(4,128)S(1)} %get-tuple-element.20), channel_id=1, source_target_pairs={{1,0},{2,1},{3,2},{4,3},{5,4},{6,5},{7,6},{8,7},{9,8},{10,9},{11,1... | collective-permute-start | bytes 1001480 | tf_op jit(solution)/shard_map/ppermute | solution.py:547
  3.2 4.7 %collective-permute-start.1 = (f32[163,4,128]{2,1,0:T(4,128)S(1)}, f32[163,4,128]{2,1,0:T(4,128)S(1)}, u32[]{:S(2)}, u32[]{:S(2)}) collective-permute-start(f32[163,4,128]{2,1,0:T(4,128)S(1)} %get-tuple-element.21), channel_id=1, source_target_pairs={{0,1},{1,2},{2,3},{3,4},{4,5},{5,6},{6,7},{7,8},{8,9},{9,10},{10,1... | collective-permute-start | bytes 1001480 | tf_op jit(solution)/shard_map/ppermute | solution.py:546
  7.9 2.4 %send.1 = f32[512,128]{1,0:T(8,128)} custom-call(s32[4]{0:T(128)} %shift_hbm.1, f32[81,2,2,128]{3,2,1,0:T(2,128)} %bitcast.26, s32[4,128]{1,0:T(4,128)} %bidx_hbm.1, s32[4,256]{1,0:T(4,128)} %dest_hbm.1, f32[256,256]{1,0:T(8,128)} %constant.8.clone.mix_hbm), custom_call_target="tpu_custom_call" | custom-call | bytes 67108864 | tf_op jit(solution)/shard_map/send/pallas_call | solution.py:522
  10.2 18.9 %all-to-all-start = ((f32[128,4,128]{2,1,0:T(4,128)}), f32[128,4,128]{2,1,0:T(4,128)}, u32[]{:S(2)}, u32[]{:S(2)}) async-start(f32[128,4,128]{2,1,0:T(4,128)} %bitcast.3), calls=%async_computation | async-start | bytes 524288 | tf_op jit(solution)/shard_map/all_to_all | solution.py:496
  29.1 0.0 collective-permute-done.next_hbm
  29.1 0.0 copy-start.2
  29.2 0.0 collective-permute-done.1.prev_hbm
  29.2 0.7 copy-done.2
  29.9 0.0 copy-start.3
  29.9 0.7 copy-done.3
  30.6 7.6 %parent.1 = (bf16[4,256,1024]{2,1,0:T(8,128)(2,1)S(1)}, f32[162,16,128]{2,1,0:T(8,128)S(1)}) custom-call(s32[1]{0:T(128)} %bitcast.5.tile_ref, f32[162,8,128]{2,1,0:T(8,128)} %bitcast.23, f32[163,4,128]{2,1,0:T(4,128)} %copy-done.2, f32[163,4,128]{2,1,0:T(4,128)} %copy-done.3, s32[8,128]{1,0:T(8,128)} %terrain_ref.1), custom_call_target="tpu_custom_call" | custom-call | flops 1099511627776 | bytes 68719476736 | tf_op jit(solution)/shard_map/parent/pallas_call | solution.py:549
  38.2 0.0 copy-start.1
  38.2 2.4 %all-to-all-done = f32[128,4,128]{2,1,0:T(4,128)} async-done(((f32[128,4,128]{2,1,0:T(4,128)}), f32[128,4,128]{2,1,0:T(4,128)}, u32[]{:S(2)}, u32[]{:S(2)}) %all-to-all-start) | async-done | bytes 262176 | tf_op jit(solution)/shard_map/all_to_all | solution.py:496
  40.6 2.7 %gather.1 = bf16[2048,128]{1,0:T(8,128)(2,1)} custom-call(f32[512,128]{1,0:T(8,128)} %bitcast.4.got_ref, bf16[4,256,1024]{2,1,0:T(8,128)(2,1)S(1)} %get-tuple-element.22.cells_ref), custom_call_target="tpu_custom_call" | custom-call | flops 536870912 | bytes 3145728 | tf_op jit(solution)/shard_map/gather/pallas_call | solution.py:570
  43.3 10.7 %all-to-all-start.1 = ((bf16[128,16,128]{2,1,0:T(8,128)(2,1)}), bf16[128,16,128]{2,1,0:T(8,128)(2,1)S(1)}, u32[]{:S(2)}, u32[]{:S(2)}) async-start(bf16[128,16,128]{2,1,0:T(8,128)(2,1)} %bitcast.6), calls=%async_computation.1 | async-start | bytes 1048576 | tf_op jit(solution)/shard_map/all_to_all | solution.py:496
  54.1 0.0 copy-done.1
  54.1 0.1 reshape.64
  54.2 0.1 copy.14
  54.3 0.1 reshape.65.bperm_ref
  54.4 0.0 copy-start
  54.4 2.6 %last_parent.1 = f32[162,8,128]{2,1,0:T(8,128)} custom-call(f32[162,16,128]{2,1,0:T(8,128)S(1)} %get-tuple-element.23.ring_ref, s32[8,128]{1,0:T(8,128)} %terrain_ref.1), custom_call_target="tpu_custom_call" | custom-call | flops 4194304 | bytes 2097152 | tf_op jit(solution)/shard_map/last_parent/pallas_call | solution.py:580
  57.0 13.0 %all-to-all-done.1 = bf16[128,16,128]{2,1,0:T(8,128)(2,1)S(1)} async-done(((bf16[128,16,128]{2,1,0:T(8,128)(2,1)}), bf16[128,16,128]{2,1,0:T(8,128)(2,1)S(1)}, u32[]{:S(2)}, u32[]{:S(2)}) %all-to-all-start.1) | async-done | bytes 524320 | tf_op jit(solution)/shard_map/all_to_all | solution.py:496
  70.0 1.3 %regroup.1 = bf16[1024,128]{1,0:T(8,128)(2,1)} custom-call(s32[4,128]{1,0:T(4,128)S(1)} %reshape.65.bperm_ref, bf16[2048,128]{1,0:T(8,128)(2,1)S(1)} %bitcast.18), custom_call_target="tpu_custom_call" | custom-call | flops 67108864 | bytes 1048576 | tf_op jit(solution)/shard_map/regroup/pallas_call | solution.py:598
  71.3 8.8 %all-to-all-start.2 = ((bf16[128,8,128]{2,1,0:T(8,128)(2,1)}), bf16[128,8,128]{2,1,0:T(8,128)(2,1)S(1)}, u32[]{:S(2)}, u32[]{:S(2)}) async-start(bf16[128,8,128]{2,1,0:T(8,128)(2,1)} %bitcast.10), calls=%async_computation.2 | async-start | bytes 524288 | tf_op jit(solution)/shard_map/all_to_all | solution.py:496
  80.1 3.1 %plan.1 = (bf16[2,512,512]{2,1,0:T(8,128)(2,1)S(1)}, f32[512,128]{1,0:T(8,128)S(1)}) custom-call(s32[1]{0:T(128)} %bitcast.5.tile_ref, f32[512,128]{1,0:T(8,128)} %bitcast.4.got_ref), custom_call_target="tpu_custom_call" | custom-call | flops 268435456 | bytes 3145728 | tf_op jit(solution)/shard_map/plan/pallas_call | solution.py:587
  83.2 8.6 %all-to-all-done.2 = bf16[128,8,128]{2,1,0:T(8,128)(2,1)S(1)} async-done(((bf16[128,8,128]{2,1,0:T(8,128)(2,1)}), bf16[128,8,128]{2,1,0:T(8,128)(2,1)S(1)}, u32[]{:S(2)}, u32[]{:S(2)}) %all-to-all-start.2) | async-done | bytes 262176 | tf_op jit(solution)/shard_map/all_to_all | solution.py:496
  91.8 0.0 copy-done
  91.8 0.6 owner.1
  92.4 18.1 %all_to_all.20 = f32[128,4,128]{2,1,0:T(4,128)S(1)} all-to-all(f32[128,4,128]{2,1,0:T(4,128)S(1)} %bitcast.20), channel_id=1, replica_groups=mesh['member'=2,'tile'=128] {'tile'}, dimensions={0} | all-to-all | bytes 524288 | tf_op jit(solution)/shard_map/all_to_all | solution.py:496
  110.5 0.2 nest.1.own_ref
  110.7 5.1 %collective-permute-start.2 = (f32[324,128]{1,0:T(8,128)S(1)}, f32[324,128]{1,0:T(8,128)S(1)}, u32[]{:S(2)}, u32[]{:S(2)}) collective-permute-start(f32[324,128]{1,0:T(8,128)S(1)} %nest.1.own_ref), channel_id=1, source_target_pairs={{0,128},{128,0},{1,129},{129,1},{2,130},{130,2},{3,131},{131,3},{4... | collective-permute-start | bytes 497672 | tf_op jit(solution)/shard_map/ppermute | solution.py:626
  115.8 0.8 reshape.70
  116.6 0.3 collective-permute-done.2.other_ref
  116.8 0.7 stats.1
Async XLA Ops:
  1.9 27.3 %collective-permute-start = (f32[163,4,128]{2,1,0:T(4,128)S(1)}, f32[163,4,128]{2,1,0:T(4,128)S(1)}, u32[]{:S(2)}, u32[]{:S(2)}) collective-permute-start(f32[163,4,128]{2,1,0:T(4,128)S(1)} %get-tuple-element.20), channel_id=1, source_target_pairs={{1,0},{2,1},{3,2},{4,3},{5,4},{6,5},{7,6},{8,7},{9,8},{10,9},{11,1... | collective-permute-start | bytes 1001480 | tf_op jit(solution)/shard_map/ppermute | solution.py:547
  3.2 26.0 %collective-permute-start.1 = (f32[163,4,128]{2,1,0:T(4,128)S(1)}, f32[163,4,128]{2,1,0:T(4,128)S(1)}, u32[]{:S(2)}, u32[]{:S(2)}) collective-permute-start(f32[163,4,128]{2,1,0:T(4,128)S(1)} %get-tuple-element.21), channel_id=1, source_target_pairs={{0,1},{1,2},{2,3},{3,4},{4,5},{5,6},{6,7},{7,8},{8,9},{9,10},{10,1... | collective-permute-start | bytes 1001480 | tf_op jit(solution)/shard_map/ppermute | solution.py:546
  10.2 30.4 %all-to-all-start = ((f32[128,4,128]{2,1,0:T(4,128)}), f32[128,4,128]{2,1,0:T(4,128)}, u32[]{:S(2)}, u32[]{:S(2)}) async-start(f32[128,4,128]{2,1,0:T(4,128)} %bitcast.3), calls=%async_computation | async-start | bytes 524288 | tf_op jit(solution)/shard_map/all_to_all | solution.py:496
  29.1 0.7 copy-start.2
  29.9 0.7 copy-start.3
  38.2 15.9 %copy-start.1 = (s32[4,128]{1,0:T(4,128)S(1)}, s32[4,128]{1,0:T(4,128)}, u32[]{:S(2)}) copy-start(s32[4,128]{1,0:T(4,128)} %bidx_hbm.1) | copy-start | bytes 6148
  43.3 26.6 %all-to-all-start.1 = ((bf16[128,16,128]{2,1,0:T(8,128)(2,1)}), bf16[128,16,128]{2,1,0:T(8,128)(2,1)S(1)}, u32[]{:S(2)}, u32[]{:S(2)}) async-start(bf16[128,16,128]{2,1,0:T(8,128)(2,1)} %bitcast.6), calls=%async_computation.1 | async-start | bytes 1048576 | tf_op jit(solution)/shard_map/all_to_all | solution.py:496
  54.4 37.4 %copy-start = (bf16[2,256,384]{2,1,0:T(8,128)(2,1)S(1)}, bf16[2,256,384]{2,1,0:T(8,128)(2,1)}, u32[]{:S(2)}) copy-start(bf16[2,256,384]{2,1,0:T(8,128)(2,1)} %constant.9.clone.mix_ref) | copy-start | bytes 1179652
  71.3 20.5 %all-to-all-start.2 = ((bf16[128,8,128]{2,1,0:T(8,128)(2,1)}), bf16[128,8,128]{2,1,0:T(8,128)(2,1)S(1)}, u32[]{:S(2)}, u32[]{:S(2)}) async-start(bf16[128,8,128]{2,1,0:T(8,128)(2,1)} %bitcast.10), calls=%async_computation.2 | async-start | bytes 524288 | tf_op jit(solution)/shard_map/all_to_all | solution.py:496
  110.7 6.2 %collective-permute-start.2 = (f32[324,128]{1,0:T(8,128)S(1)}, f32[324,128]{1,0:T(8,128)S(1)}, u32[]{:S(2)}, u32[]{:S(2)}) collective-permute-start(f32[324,128]{1,0:T(8,128)S(1)} %nest.1.own_ref), channel_id=1, source_target_pairs={{0,128},{128,0},{1,129},{129,1},{2,130},{130,2},{3,131},{131,3},{4... | collective-permute-start | bytes 497672 | tf_op jit(solution)/shard_map/ppermute | solution.py:626

commit v4 on v3

--- a/solution.py
+++ b/solution.py
@@ -18,6 +18,10 @@
 LPAD = 96
 RING = 16
 BSTR = LPAD * RING
+SENT = 6
+FLAT = 2 * LEV * ROWS
+HALO_ROWS = 992
+DIST = ((0, 1), (2, 3), (4, None), (5, None))
 SPLIT = 40
 L_TOP = 81
 L_REQ = 86
@@ -85,8 +89,12 @@
     return send, edge
 
 
-def call(body, out_shape, in_specs=None, scratch=(), name=None, flops=0, nbytes=0):
+def call(
+    body, out_shape, in_specs=None, out_specs=None, scratch=(), name=None, flops=0, nbytes=0
+):
     kwargs = {} if in_specs is None else {"in_specs": in_specs}
+    if out_specs is not None:
+        kwargs["out_specs"] = out_specs
     return pl.pallas_call(
         body,
         out_shape=out_shape,
@@ -112,15 +120,30 @@
     return copies
 
 
-def halo_kernel(parent_hbm, terrain_hbm, down_ref, up_ref, parent_ref, terrain_ref, sems):
+def halo_kernel(
+    tile_ref, parent_hbm, terrain_hbm,
+    parent_ref, first_ref, second_ref,
+    terrain_ref, down_ref, up_ref, damp_ref, sems,
+):
     copies = start_all([(parent_hbm, parent_ref), (terrain_hbm, terrain_ref)], sems)
     for copy in copies:
         copy.wait()
-    damping = DRAG * terrain_ref[...].astype(F32) / 3000.0
-    down_ref[: 2 * LEV, :, :] = parent_ref[:, 4:, :]
-    up_ref[: 2 * LEV, :, :] = parent_ref[:, :4, :]
-    down_ref[2 * LEV, :, :] = damping[4:, :]
-    up_ref[2 * LEV, :, :] = damping[:4, :]
+    damp_ref[...] = DRAG * terrain_ref[...].astype(F32) / 3000.0
+    for ref, rows in ((down_ref, (7, 6, 5, 4)), (up_ref, (0, 1, 2, 3))):
+        ref[HALO_ROWS - 24 :, :] = jnp.zeros((24, W), F32)
+        for row, (coarse, fine) in zip(rows, DIST):
+            for count, base, value in (
+                (2 * LEV, 0, parent_ref[pl.ds(row, 2 * LEV, stride=ROWS), :]),
+                (1, 2 * LEV * SENT, damp_ref[row : row + 1, :]),
+            ):
+                ref[pl.ds(base + coarse, count, stride=SENT), :] = value
+                if fine is not None:
+                    rest = value - value.astype(BF16).astype(F32)
+                    ref[pl.ds(base + fine, count, stride=SENT), :] = rest
+    even = jnp.bitwise_and(tile_ref[0], 1) == 0
+    down, up = down_ref[...], up_ref[...]
+    first_ref[...] = jnp.where(even, down, up).astype(BF16)
+    second_ref[...] = jnp.where(even, up, down).astype(BF16)
 
 
 def send_kernel(
@@ -215,100 +238,93 @@
 
 
 def parent_kernel(
-    tile_ref, parent_hbm, next_hbm, prev_hbm, terrain_hbm,
-    cells_ref, ring_ref,
-    parent_ref, terrain_ref, next_ref, prev_ref, a_ref, b_ref, sems,
+    tile_ref, parent_ref, first_ref, second_ref, terrain_hbm,
+    cells_ref, ring_hbm,
+    next_ref, prev_ref, halo_ref, damp_ref, a_ref, b_ref, ring_ref, terrain_ref, sems,
 ):
+    copies = start_all([(terrain_hbm, terrain_ref)], sems)
+    store = pltpu.make_async_copy(ring_ref, ring_hbm, sems.at[1])
     tile = tile_ref[0]
-    copies = start_all(
-        [
-            (parent_hbm, parent_ref),
-            (terrain_hbm, terrain_ref),
-            (next_hbm, next_ref),
-            (prev_hbm, prev_ref),
-        ],
-        sems,
-    )
-    for copy in copies[1:]:
-        copy.wait()
+    even = jnp.bitwise_and(tile, 1) == 0
+    first, second = first_ref[...].astype(F32), second_ref[...].astype(F32)
+    next_ref[...] = jnp.where(even, first, second)
+    prev_ref[...] = jnp.where(even, second, first)
+    for ref, rows in ((next_ref, (0, 1, 2, 3)), (prev_ref, (7, 6, 5, 4))):
+        for row, (coarse, fine) in zip(rows, DIST):
+            for count, base, out in ((2 * LEV, 0, halo_ref), (1, 2 * LEV * SENT, damp_ref)):
+                value = ref[pl.ds(base + coarse, count, stride=SENT), :]
+                if fine is not None:
+                    value = value + ref[pl.ds(base + fine, count, stride=SENT), :]
+                out[pl.ds(row, count, stride=ROWS), :] = value
+    copies[0].wait()
     damping = DRAG * terrain_ref[...].astype(F32) / 3000.0
     pads = jnp.zeros(((LPAD - LEV) * RING, W), F32)
-    for ref in (a_ref, b_ref):
+    for ref in (a_ref, b_ref, ring_ref):
         for member in range(2):
             top = member * BSTR + LEV * RING
             ref[top : top + (LPAD - LEV) * RING, :] = pads
     for s in range(STEPS):
         for member in range(2):
-            cells_ref[s, member * W + LPAD : (member + 1) * W, :] = jnp.zeros(
-                (W - LPAD, ROWS * W), BF16
+            start = LPAD if s else LEV - 1
+            cells_ref[s, member * W + start : (member + 1) * W, :] = jnp.zeros(
+                (W - start, ROWS * W), BF16
             )
-
-    copies[0].wait()
-
-    def fill(level, carry):
-        for member in range(2):
-            src = member * LEV + level
-            base = pl.multiple_of(member * BSTR + level * RING, RING)
-            a_ref[pl.ds(base, ROWS), :] = parent_ref[src]
-            a_ref[pl.ds(base + 8, 4), :] = next_ref[src]
-            a_ref[pl.ds(base + 12, 4), :] = prev_ref[src]
-        return carry
-
-    lax.fori_loop(0, LEV, fill, 0)
-    b_ref[0:4, :] = next_ref[2 * LEV]
-    b_ref[4:8, :] = prev_ref[2 * LEV]
     row = lax.broadcasted_iota(jnp.int32, (ROWS, W), 0)
     south = jnp.where(tile < NT - 1, 1.0, 0.0).astype(F32)
     north = jnp.where(tile > 0, 1.0, 0.0).astype(F32)
     valid = jnp.where(row < 4, south, north)
     stay = 1.0 - 4.0 * HORIZ - 2.0 * VERT
-    coef = (stay - damping, (stay - b_ref[0:8, :]) * valid, HORIZ * valid, VERT * valid)
-
-    def emit(s, ref):
+    coef = (stay - damping, (stay - damp_ref[...]) * valid, HORIZ * valid, VERT * valid)
+
+    def emit(s, ref, count, stride):
         for member in range(2):
             for y in range(ROWS):
-                rows = ref[pl.ds(member * BSTR + y, LPAD, stride=RING), :]
-                cells_ref[s, member * W : member * W + LPAD, y * W : (y + 1) * W] = (
+                start = member * count * stride + y
+                rows = ref[pl.ds(start, count, stride=stride), :]
+                cells_ref[s, member * W : member * W + count, y * W : (y + 1) * W] = (
                     rows.astype(BF16)
                 )
 
-    emit(0, a_ref)
-    src, dst = a_ref, b_ref
-    for s in range(1, STEPS):
-
-        def read(index, src=src):
-            base = pl.multiple_of(index * RING, RING)
-            return src[pl.ds(base, ROWS), :], src[pl.ds(base + ROWS, ROWS), :]
+    def read_first(index):
+        base = pl.multiple_of(index * ROWS, ROWS)
+        return parent_ref[pl.ds(base, ROWS), :], halo_ref[pl.ds(base, ROWS), :]
+
+    emit(0, parent_ref, LEV, ROWS)
+    read, stride = read_first, LEV
+    for s, dst in zip(range(1, STEPS), (a_ref, b_ref, ring_ref)):
 
         def write(member, level, y0, y1, dst=dst):
             base = pl.multiple_of((member * LPAD + level) * RING, RING)
             dst[pl.ds(base, ROWS), :] = y0
             dst[pl.ds(base + ROWS, ROWS), :] = y1
 
-        ring_step(read, write, LPAD, coef)
-        emit(s, dst)
-        src, dst = dst, src
-
-    def drain(level, carry):
-        for member in range(2):
-            base = pl.multiple_of((member * LPAD + level) * RING, RING)
-            ring_ref[member * LEV + level] = src[pl.ds(base, RING), :]
-        return carry
-
-    lax.fori_loop(0, LEV, drain, 0)
-
-
-def last_parent_kernel(ring_ref, terrain_ref, out_ref):
+        ring_step(read, write, stride, coef)
+        if s == STEPS - 1:
+            store.start()
+        emit(s, dst, LPAD, RING)
+
+        def read(index, src=dst):
+            base = pl.multiple_of(index * RING, RING)
+            return src[pl.ds(base, ROWS), :], src[pl.ds(base + ROWS, ROWS), :]
+
+        stride = LPAD
+    store.wait()
+
+
+def last_parent_kernel(ring_hbm, terrain_hbm, out_ref, ring_ref, terrain_ref, sems):
+    for copy in start_all([(ring_hbm, ring_ref), (terrain_hbm, terrain_ref)], sems):
+        copy.wait()
     damping = DRAG * terrain_ref[...].astype(F32) / 3000.0
     stay = 1.0 - 4.0 * HORIZ - 2.0 * VERT
 
     def read(index):
-        return ring_ref[index, 0:ROWS, :], ring_ref[index, ROWS:RING, :]
+        base = pl.multiple_of(index * RING, RING)
+        return ring_ref[pl.ds(base, ROWS), :], ring_ref[pl.ds(base + ROWS, ROWS), :]
 
     def write(member, level, y0, y1):
         out_ref[member * LEV + level] = y0
 
-    ring_step(read, write, LEV, (stay - damping, None, None, None), own_only=True)
+    ring_step(read, write, LPAD, (stay - damping, None, None, None), own_only=True)
 
 
 def gather_kernel(got_ref, cells_ref, out_ref, scr_ref):
@@ -501,22 +517,27 @@
     q_mix, e_mix = jnp.asarray(q_mix), jnp.asarray(e_mix)
     sds = jax.ShapeDtypeStruct
     tile = lax.axis_index("tile").astype(jnp.int32).reshape(1)
-    parent = parent_state.reshape(2 * LEV, ROWS, W)
+    parent = parent_state.reshape(FLAT, W)
 
     nest = nest_state.reshape(2, LEV, 2, W).transpose(1, 2, 0, 3)
-    parent, terrain = in_hbm(parent), in_hbm(terrain)
-    down, up = call(
+    kept, down, up = call(
         halo_kernel,
-        (sds((2 * LEV + 1, 4, W), F32), sds((2 * LEV + 1, 4, W), F32)),
-        in_specs=[HB] * 2,
+        (
+            pltpu.VMEM((FLAT, W), F32),
+            sds((HALO_ROWS, W), BF16),
+            sds((HALO_ROWS, W), BF16),
+        ),
+        in_specs=[SM, HB, HB],
         scratch=[
-            pltpu.VMEM((2 * LEV, ROWS, W), F32),
             pltpu.VMEM((ROWS, W), jnp.int32),
+            pltpu.VMEM((HALO_ROWS, W), F32),
+            pltpu.VMEM((HALO_ROWS, W), F32),
+            pltpu.VMEM((ROWS, W), F32),
             pltpu.SemaphoreType.DMA((2,)),
         ],
         name="halo",
         nbytes=1 << 20,
-    )(parent, terrain)
+    )(tile, in_hbm(parent), in_hbm(terrain))
     nest, down, up = lax.optimization_barrier((nest, down, up))
     nest = in_hbm(nest)
     message = call(
@@ -541,31 +562,35 @@
         in_hbm(reloc_dest),
         in_hbm(q_mix),
     )
-    forward = [(i, i + 1) for i in range(NT - 1)]
-    backward = [(i + 1, i) for i in range(NT - 1)]
-    from_prev = lax.ppermute(down, "tile", forward)
-    from_next = lax.ppermute(up, "tile", backward)
+    pairs = [(i, i + 1) for i in range(0, NT, 2)] + [(i + 1, i) for i in range(0, NT, 2)]
+    gaps = [(i, i + 1) for i in range(1, NT - 1, 2)]
+    gaps = gaps + [(i + 1, i) for i in range(1, NT - 1, 2)]
+    from_pair = lax.ppermute(down, "tile", pairs)
+    from_gap = lax.ppermute(up, "tile", gaps)
     first = exchange(message.reshape(NT, 4, W)).reshape(4 * NT, W)
     cells, ring = call(
         parent_kernel,
         (
             pltpu.VMEM((STEPS, 2 * W, ROWS * W), BF16),
-            pltpu.VMEM((2 * LEV, RING, W), F32),
+            pltpu.HBM((2 * BSTR, W), F32),
         ),
-        in_specs=[SM, HB, HB, HB, HB],
+        in_specs=[SM, VM, VM, VM, HB],
+        out_specs=(VM, HB),
         scratch=[
-            pltpu.VMEM((2 * LEV, ROWS, W), F32),
-            pltpu.VMEM((ROWS, W), jnp.int32),
-            pltpu.VMEM((2 * LEV + 1, 4, W), F32),
-            pltpu.VMEM((2 * LEV + 1, 4, W), F32),
+            pltpu.VMEM((HALO_ROWS, W), F32),
+            pltpu.VMEM((HALO_ROWS, W), F32),
+            pltpu.VMEM((FLAT, W), F32),
+            pltpu.VMEM((ROWS, W), F32),
             pltpu.VMEM((2 * BSTR, W), F32),
             pltpu.VMEM((2 * BSTR, W), F32),
-            pltpu.SemaphoreType.DMA((4,)),
+            pltpu.VMEM((2 * BSTR, W), F32),
+            pltpu.VMEM((ROWS, W), jnp.int32),
+            pltpu.SemaphoreType.DMA((2,)),
         ],
         name="parent",
         flops=1 << 40,
         nbytes=1 << 36,
-    )(tile, parent, in_hbm(from_next), in_hbm(from_prev), terrain)
+    )(tile, kept, from_pair, from_gap, in_hbm(terrain))
 
     values = call(
         gather_kernel,
@@ -580,10 +605,16 @@
     parent_out = call(
         last_parent_kernel,
         sds((2 * LEV, ROWS, W), F32),
+        in_specs=[HB, HB],
+        scratch=[
+            pltpu.VMEM((2 * BSTR, W), F32),
+            pltpu.VMEM((ROWS, W), jnp.int32),
+            pltpu.SemaphoreType.DMA((2,)),
+        ],
         name="last_parent",
         flops=1 << 22,
         nbytes=2 << 20,
-    )(ring, terrain)
+    )(in_hbm(ring), in_hbm(terrain))
     hot, base = call(
         plan_kernel,
         (sds((2, 4 * NT, 4 * NT), BF16), sds((4 * NT, W), F32)),

time: 118 us -> 111 us (0.941)
  starting transfers between devices: 49.5 us -> 42.7 us
  waiting for transfers between devices: 24.3 us -> 26 us
  local copies, waits for them, and re-layouts: 2.49 us -> 1.05 us
    all_to_all x3, starting transfers between devices: 38.4 us -> 34.7 us  [exchange(): return lax.all_to_all(x, 'tile', split_axis=0, concat_axis=0, tiled=True)]
    ppermute x2, starting transfers between devices: 5.97 us -> 2.88 us  [the longest x1 2.21 us: on_device(): from_pair = lax.ppermute(down, 'tile', pairs)]
    all_to_all x3, waiting for transfers between devices: 24.1 us -> 25.7 us  [exchange(): return lax.all_to_all(x, 'tile', split_axis=0, concat_axis=0, tiled=True)]
    unnamed x8 -> x4, local copies, waits for them, and re-layouts: 1.45 us -> 0.01 us
  transfers between devices with their start and end apart: 6 -> 6, of which waited for: 4 -> 4; matrix products, arithmetic and copies ran while one was open for 1% -> 1% of each run, Pallas kernels for 11% -> 12%
where the time goes in v4:
time: 111 us
  starting transfers between devices  42.7 us (38%)
  waiting for transfers between devices  26 us (23%)
  Pallas kernels  22.3 us (20%)
  blocking collectives  18 us (16%)
    all_to_all x3, starting transfers between devices, exchange(): return lax.all_to_all(x, 'tile', split_axis=0, concat_axis=0, tiled=True)  34.7 us
    all_to_all x3, waiting for transfers between devices, exchange(): return lax.all_to_all(x, 'tile', split_axis=0, concat_axis=0, tiled=True)  25.7 us
    all_to_all x1, blocking collectives, exchange(): return lax.all_to_all(x, 'tile', split_axis=0, concat_axis=0, tiled=True)  18 us
    pallas_call x1, Pallas kernels, on_device(): call(parent_kernel, (pltpu.VMEM((STEPS, 2 * W, ROWS * W), BF16), pltpu.HB...  6.66 us
    ppermute x1, starting transfers between devices, on_device(): other = lax.ppermute(nest_out, 'member', [(0, 1), (1, 0)])  5.15 us
    pallas_call x1, Pallas kernels, on_device(): call(last_parent_kernel, sds((2 * LEV, ROWS, W), F32), in_specs=[HB, HB],...  3.31 us
    pallas_call x1, Pallas kernels, on_device(): call(plan_kernel, (sds((2, 4 * NT, 4 * NT), BF16), sds((4 * NT, W), F32))...  3.12 us
    pallas_call x1, Pallas kernels, on_device(): call(gather_kernel, sds((16 * NT, W), BF16), scratch=[pltpu.VMEM((16 * NT...  2.71 us
  transfers between devices with their start and end apart: 6, of which 4 were waited for; matrix products, arithmetic and copies ran while one was open for 1% of the time, Pallas kernels for 12%

profile of v4, /device:TPU:1, one launch (start us, length us, event | category | flops | bytes accessed | tf_op | source)
XLA Modules:
  0.0 110.9 jit_solution(18422200405140378366)
XLA Ops:
  0.6 1.4 %halo.1 = (f32[1296,128]{1,0:T(8,128)S(1)}, bf16[992,128]{1,0:T(8,128)(2,1)S(1)}, bf16[992,128]{1,0:T(8,128)(2,1)S(1)}) custom-call(s32[1]{0:T(128)} %bitcast.2.tile_ref, f32[1296,128]{1,0:T(8,128)} %bitcast.22, s32[8,128]{1,0:T(8,128)} %terrain_hbm.5), custom_call_target="tpu_custom_call" | custom-call | bytes 1048576 | tf_op jit(solution)/shard_map/halo/pallas_call | solution.py:523
  2.1 2.2 %collective-permute-start = (bf16[992,128]{1,0:T(8,128)(2,1)S(1)}, bf16[992,128]{1,0:T(8,128)(2,1)S(1)}, u32[]{:S(2)}, u32[]{:S(2)}) collective-permute-start(bf16[992,128]{1,0:T(8,128)(2,1)S(1)} %get-tuple-element.22), channel_id=1, source_target_pairs={{0,1},{2,3},{4,5},{6,7},{8,9},{10,11},{12,13},{14,15},{16,17},{18,... | collective-permute-start | bytes 761864 | tf_op jit(solution)/shard_map/ppermute | solution.py:568
  4.3 0.7 collective-permute-start.1
  4.9 2.4 %send.1 = f32[512,128]{1,0:T(8,128)} custom-call(s32[4]{0:T(128)} %shift_hbm.1, f32[81,2,2,128]{3,2,1,0:T(2,128)} %bitcast.25, s32[4,128]{1,0:T(4,128)} %bidx_hbm.1, s32[4,256]{1,0:T(4,128)} %dest_hbm.1, f32[256,256]{1,0:T(8,128)} %constant.8.clone.mix_hbm), custom_call_target="tpu_custom_call" | custom-call | bytes 67108864 | tf_op jit(solution)/shard_map/send/pallas_call | solution.py:543
  7.3 17.5 %all-to-all-start = ((f32[128,4,128]{2,1,0:T(4,128)}), f32[128,4,128]{2,1,0:T(4,128)}, u32[]{:S(2)}, u32[]{:S(2)}) async-start(f32[128,4,128]{2,1,0:T(4,128)} %bitcast.4), calls=%async_computation | async-start | bytes 524288 | tf_op jit(solution)/shard_map/all_to_all | solution.py:512
  24.8 0.0 collective-permute-done.first_ref
  24.8 0.0 collective-permute-done.1.second_ref
  24.8 6.7 %parent.1 = (bf16[4,256,1024]{2,1,0:T(8,128)(2,1)S(1)}, f32[3072,128]{1,0:T(8,128)}) custom-call(s32[1]{0:T(128)} %bitcast.2.tile_ref, f32[1296,128]{1,0:T(8,128)S(1)} %get-tuple-element.21.parent_ref, bf16[992,128]{1,0:T(8,128)(2,1)S(1)} %collective-permute-done.first_ref, bf16[992,128]{1,0:T(8,128)(2,1)S(1)} %collective-permute-done.1.second_ref, ...), custom_call_target="tpu_custom_call" | custom-call | flops 1099511627776 | bytes 68719476736 | tf_op jit(solution)/shard_map/parent/pallas_call | solution.py:571
  31.5 0.0 copy-start.1
  31.5 4.8 %all-to-all-done = f32[128,4,128]{2,1,0:T(4,128)} async-done(((f32[128,4,128]{2,1,0:T(4,128)}), f32[128,4,128]{2,1,0:T(4,128)}, u32[]{:S(2)}, u32[]{:S(2)}) %all-to-all-start) | async-done | bytes 262176 | tf_op jit(solution)/shard_map/all_to_all | solution.py:512
  36.3 2.7 %gather.1 = bf16[2048,128]{1,0:T(8,128)(2,1)} custom-call(f32[512,128]{1,0:T(8,128)} %bitcast.5.got_ref, bf16[4,256,1024]{2,1,0:T(8,128)(2,1)S(1)} %get-tuple-element.24.cells_ref), custom_call_target="tpu_custom_call" | custom-call | flops 536870912 | bytes 3145728 | tf_op jit(solution)/shard_map/gather/pallas_call | solution.py:595
  39.0 8.4 %all-to-all-start.1 = ((bf16[128,16,128]{2,1,0:T(8,128)(2,1)}), bf16[128,16,128]{2,1,0:T(8,128)(2,1)S(1)}, u32[]{:S(2)}, u32[]{:S(2)}) async-start(bf16[128,16,128]{2,1,0:T(8,128)(2,1)} %bitcast.6), calls=%async_computation.1 | async-start | bytes 1048576 | tf_op jit(solution)/shard_map/all_to_all | solution.py:512
  47.4 0.0 copy-done.1
  47.4 0.1 reshape.64
  47.5 0.1 copy.14
  47.6 0.1 reshape.65.bperm_ref
  47.7 0.0 copy-start
  47.7 3.3 %last_parent.1 = f32[162,8,128]{2,1,0:T(8,128)} custom-call(f32[3072,128]{1,0:T(8,128)} %get-tuple-element.25.ring_hbm, s32[8,128]{1,0:T(8,128)} %terrain_hbm.5), custom_call_target="tpu_custom_call" | custom-call | flops 4194304 | bytes 2097152 | tf_op jit(solution)/shard_map/last_parent/pallas_call | solution.py:605
  51.0 12.3 %all-to-all-done.1 = bf16[128,16,128]{2,1,0:T(8,128)(2,1)S(1)} async-done(((bf16[128,16,128]{2,1,0:T(8,128)(2,1)}), bf16[128,16,128]{2,1,0:T(8,128)(2,1)S(1)}, u32[]{:S(2)}, u32[]{:S(2)}) %all-to-all-start.1) | async-done | bytes 524320 | tf_op jit(solution)/shard_map/all_to_all | solution.py:512
  63.3 1.3 %regroup.1 = bf16[1024,128]{1,0:T(8,128)(2,1)} custom-call(s32[4,128]{1,0:T(4,128)S(1)} %reshape.65.bperm_ref, bf16[2048,128]{1,0:T(8,128)(2,1)S(1)} %bitcast.18), custom_call_target="tpu_custom_call" | custom-call | flops 67108864 | bytes 1048576 | tf_op jit(solution)/shard_map/regroup/pallas_call | solution.py:629
  64.6 8.8 %all-to-all-start.2 = ((bf16[128,8,128]{2,1,0:T(8,128)(2,1)}), bf16[128,8,128]{2,1,0:T(8,128)(2,1)S(1)}, u32[]{:S(2)}, u32[]{:S(2)}) async-start(bf16[128,8,128]{2,1,0:T(8,128)(2,1)} %bitcast.10), calls=%async_computation.2 | async-start | bytes 524288 | tf_op jit(solution)/shard_map/all_to_all | solution.py:512
  73.4 3.1 %plan.1 = (bf16[2,512,512]{2,1,0:T(8,128)(2,1)S(1)}, f32[512,128]{1,0:T(8,128)S(1)}) custom-call(s32[1]{0:T(128)} %bitcast.2.tile_ref, f32[512,128]{1,0:T(8,128)} %bitcast.5.got_ref), custom_call_target="tpu_custom_call" | custom-call | flops 268435456 | bytes 3145728 | tf_op jit(solution)/shard_map/plan/pallas_call | solution.py:618
  76.5 8.6 %all-to-all-done.2 = bf16[128,8,128]{2,1,0:T(8,128)(2,1)S(1)} async-done(((bf16[128,8,128]{2,1,0:T(8,128)(2,1)}), bf16[128,8,128]{2,1,0:T(8,128)(2,1)S(1)}, u32[]{:S(2)}, u32[]{:S(2)}) %all-to-all-start.2) | async-done | bytes 262176 | tf_op jit(solution)/shard_map/all_to_all | solution.py:512
  85.1 0.0 copy-done
  85.1 0.6 owner.1
  85.8 18.0 %all_to_all.20 = f32[128,4,128]{2,1,0:T(4,128)S(1)} all-to-all(f32[128,4,128]{2,1,0:T(4,128)S(1)} %bitcast.20), channel_id=1, replica_groups=mesh['member'=2,'tile'=128] {'tile'}, dimensions={0} | all-to-all | bytes 524288 | tf_op jit(solution)/shard_map/all_to_all | solution.py:512
  103.8 0.2 nest.1.own_ref
  104.0 5.1 %collective-permute-start.2 = (f32[324,128]{1,0:T(8,128)S(1)}, f32[324,128]{1,0:T(8,128)S(1)}, u32[]{:S(2)}, u32[]{:S(2)}) collective-permute-start(f32[324,128]{1,0:T(8,128)S(1)} %nest.1.own_ref), channel_id=1, source_target_pairs={{0,128},{128,0},{1,129},{129,1},{2,130},{130,2},{3,131},{131,3},{4... | collective-permute-start | bytes 497672 | tf_op jit(solution)/shard_map/ppermute | solution.py:657
  109.1 0.8 reshape.70
  109.9 0.3 collective-permute-done.2.other_ref
  110.2 0.7 stats.1
Async XLA Ops:
  2.1 22.8 %collective-permute-start = (bf16[992,128]{1,0:T(8,128)(2,1)S(1)}, bf16[992,128]{1,0:T(8,128)(2,1)S(1)}, u32[]{:S(2)}, u32[]{:S(2)}) collective-permute-start(bf16[992,128]{1,0:T(8,128)(2,1)S(1)} %get-tuple-element.22), channel_id=1, source_target_pairs={{0,1},{2,3},{4,5},{6,7},{8,9},{10,11},{12,13},{14,15},{16,17},{18,... | collective-permute-start | bytes 761864 | tf_op jit(solution)/shard_map/ppermute | solution.py:568
  4.3 20.6 %collective-permute-start.1 = (bf16[992,128]{1,0:T(8,128)(2,1)S(1)}, bf16[992,128]{1,0:T(8,128)(2,1)S(1)}, u32[]{:S(2)}, u32[]{:S(2)}) collective-permute-start(bf16[992,128]{1,0:T(8,128)(2,1)S(1)} %get-tuple-element.23), channel_id=1, source_target_pairs={{1,2},{3,4},{5,6},{7,8},{9,10},{11,12},{13,14},{15,16},{17,18},{19... | collective-permute-start | bytes 761864 | tf_op jit(solution)/shard_map/ppermute | solution.py:569
  7.3 29.0 %all-to-all-start = ((f32[128,4,128]{2,1,0:T(4,128)}), f32[128,4,128]{2,1,0:T(4,128)}, u32[]{:S(2)}, u32[]{:S(2)}) async-start(f32[128,4,128]{2,1,0:T(4,128)} %bitcast.4), calls=%async_computation | async-start | bytes 524288 | tf_op jit(solution)/shard_map/all_to_all | solution.py:512
  31.5 15.9 %copy-start.1 = (s32[4,128]{1,0:T(4,128)S(1)}, s32[4,128]{1,0:T(4,128)}, u32[]{:S(2)}) copy-start(s32[4,128]{1,0:T(4,128)} %bidx_hbm.1) | copy-start | bytes 6148
  39.0 24.3 %all-to-all-start.1 = ((bf16[128,16,128]{2,1,0:T(8,128)(2,1)}), bf16[128,16,128]{2,1,0:T(8,128)(2,1)S(1)}, u32[]{:S(2)}, u32[]{:S(2)}) async-start(bf16[128,16,128]{2,1,0:T(8,128)(2,1)} %bitcast.6), calls=%async_computation.1 | async-start | bytes 1048576 | tf_op jit(solution)/shard_map/all_to_all | solution.py:512
  47.7 37.4 %copy-start = (bf16[2,256,384]{2,1,0:T(8,128)(2,1)S(1)}, bf16[2,256,384]{2,1,0:T(8,128)(2,1)}, u32[]{:S(2)}) copy-start(bf16[2,256,384]{2,1,0:T(8,128)(2,1)} %constant.9.clone.mix_ref) | copy-start | bytes 1179652
  64.6 20.5 %all-to-all-start.2 = ((bf16[128,8,128]{2,1,0:T(8,128)(2,1)}), bf16[128,8,128]{2,1,0:T(8,128)(2,1)S(1)}, u32[]{:S(2)}, u32[]{:S(2)}) async-start(bf16[128,8,128]{2,1,0:T(8,128)(2,1)} %bitcast.10), calls=%async_computation.2 | async-start | bytes 524288 | tf_op jit(solution)/shard_map/all_to_all | solution.py:512
  104.0 6.2 %collective-permute-start.2 = (f32[324,128]{1,0:T(8,128)S(1)}, f32[324,128]{1,0:T(8,128)S(1)}, u32[]{:S(2)}, u32[]{:S(2)}) collective-permute-start(f32[324,128]{1,0:T(8,128)S(1)} %nest.1.own_ref), channel_id=1, source_target_pairs={{0,128},{128,0},{1,129},{129,1},{2,130},{130,2},{3,131},{131,3},{4... | collective-permute-start | bytes 497672 | tf_op jit(solution)/shard_map/ppermute | solution.py:657

commit v5 on v4

--- a/solution.py
+++ b/solution.py
@@ -23,6 +23,8 @@
 HALO_ROWS = 992
 DIST = ((0, 1), (2, 3), (4, None), (5, None))
 SPLIT = 40
+PACK = 12
+CUT = W - LEV
 L_TOP = 81
 L_REQ = 86
 L_INNER = 88
@@ -121,12 +123,22 @@
 
 
 def halo_kernel(
-    tile_ref, parent_hbm, terrain_hbm,
-    parent_ref, first_ref, second_ref,
+    tile_ref, parent_hbm, terrain_hbm, nest_hbm, bidx_hbm, dest_hbm, mix_hbm,
+    parent_ref, first_ref, second_ref, nest_ref, bidx_ref, dest_ref, mix_ref,
     terrain_ref, down_ref, up_ref, damp_ref, sems,
 ):
-    copies = start_all([(parent_hbm, parent_ref), (terrain_hbm, terrain_ref)], sems)
-    for copy in copies:
+    copies = start_all(
+        [
+            (parent_hbm, parent_ref),
+            (terrain_hbm, terrain_ref),
+            (nest_hbm, nest_ref),
+            (bidx_hbm, bidx_ref),
+            (dest_hbm, dest_ref),
+            (mix_hbm, mix_ref),
+        ],
+        sems,
+    )
+    for copy in copies[:2]:
         copy.wait()
     damp_ref[...] = DRAG * terrain_ref[...].astype(F32) / 3000.0
     for ref, rows in ((down_ref, (7, 6, 5, 4)), (up_ref, (0, 1, 2, 3))):
@@ -144,25 +156,16 @@
     down, up = down_ref[...], up_ref[...]
     first_ref[...] = jnp.where(even, down, up).astype(BF16)
     second_ref[...] = jnp.where(even, up, down).astype(BF16)
+    for copy in copies[2:]:
+        copy.wait()
 
 
 def send_kernel(
-    shift_hbm, nest_hbm, bidx_hbm, dest_hbm, mix_hbm,
+    shift_hbm, nest_ref, bidx_ref, dest_ref, mix_ref,
     msg_ref,
-    shift_ref, nest_ref, bidx_ref, dest_ref, mix_ref, pad_ref, sems,
+    shift_ref, pad_ref, sems,
 ):
-    copies = start_all(
-        [
-            (nest_hbm, nest_ref),
-            (bidx_hbm, bidx_ref),
-            (dest_hbm, dest_ref),
-            (shift_hbm, shift_ref),
-            (mix_hbm, mix_ref),
-        ],
-        sems,
-    )
-    for copy in copies:
-        copy.wait()
+    copies = start_all([(shift_hbm, shift_ref)], sems)
     zeros = jnp.zeros((W - LEV + 1, W), F32)
     for b in range(2):
         for part in range(2):
@@ -182,6 +185,7 @@
         for owner in range(2):
             start = b * 2 * W + owner * W
             msg_ref[start : start + W, :] = res[:, owner * W : (owner + 1) * W]
+    copies[0].wait()
     lane = lax.broadcasted_iota(jnp.int32, (NT, W), 1)
     tile = lax.broadcasted_iota(jnp.int32, (NT, W), 0)
     for s in range(STEPS):
@@ -328,11 +332,13 @@
 
 
 def gather_kernel(got_ref, cells_ref, out_ref, scr_ref):
-    lane = lax.broadcasted_iota(jnp.int32, (NT, ROWS * W), 1).astype(F32)
+    cell = lax.broadcasted_iota(jnp.int32, (NT, ROWS * W), 1).astype(F32)
+    lane = lax.broadcasted_iota(jnp.int32, (NT, W), 1)
+    rows = {}
     for s in range(STEPS):
-        rows = got_ref[pl.ds(s, NT, stride=4), :]
+        asked = got_ref[pl.ds(s, NT, stride=4), :]
         hot = [
-            jnp.where(lane == rows[:, L_REQ + c : L_REQ + c + 1], 1.0, 0.0).astype(BF16)
+            jnp.where(cell == asked[:, L_REQ + c : L_REQ + c + 1], 1.0, 0.0).astype(BF16)
             for c in range(2)
         ]
         hot = jnp.concatenate(hot, axis=0)
@@ -341,14 +347,30 @@
         )
         for b in range(2):
             for c in range(2):
-                scr_ref[pl.ds(b * 8 + s * 2 + c, NT, stride=16), :] = res[
-                    c * W : (c + 1) * W, b * W : (b + 1) * W
-                ]
+                rows[b * 8 + s * 2 + c] = res[c * W : (c + 1) * W, b * W : (b + 1) * W]
+    for r in range(PACK):
+        row = rows[r]
+        if r < 8:
+            extra = rows[PACK + r // 2]
+            if r % 2 == 0:
+                row = row + pltpu.roll(jnp.where(lane < CUT, extra, 0.0), LEV, 1)
+            else:
+                row = row + pltpu.roll(jnp.where(lane < CUT, 0.0, extra), LEV - CUT, 1)
+        scr_ref[pl.ds(r, NT, stride=PACK), :] = row
     out_ref[...] = scr_ref[...].astype(BF16)
 
 
 def regroup_kernel(bperm_ref, got_ref, out_ref, scr_ref, scr2_ref):
     scr_ref[...] = got_ref[...].astype(F32)
+    low = lax.broadcasted_iota(jnp.int32, (NT, W), 1) < CUT
+
+    def row(r):
+        if r < PACK:
+            return scr_ref[pl.ds(r, NT, stride=PACK), :]
+        first = pltpu.roll(row(2 * (r - PACK)), W - LEV, 1)
+        second = pltpu.roll(row(2 * (r - PACK) + 1), W - LEV + CUT, 1)
+        return jnp.where(low, first, second)
+
     sub = lax.broadcasted_iota(jnp.int32, (2 * NT, W), 0)
     lane = lax.broadcasted_iota(jnp.int32, (2 * NT, W), 1)
     parity = jnp.bitwise_and(jnp.right_shift(lane, 5), 1)
@@ -359,10 +381,7 @@
         values = jnp.concatenate(
             [
                 jnp.concatenate(
-                    [
-                        scr_ref[pl.ds(b * 8 + s * 2 + c, NT, stride=16), :]
-                        for b in range(2)
-                    ],
+                    [row(b * 8 + s * 2 + c) for b in range(2)],
                     axis=1,
                 )
                 for c in range(2)
@@ -520,48 +539,48 @@
     parent = parent_state.reshape(FLAT, W)
 
     nest = nest_state.reshape(2, LEV, 2, W).transpose(1, 2, 0, 3)
-    kept, down, up = call(
+    kept, down, up, nest, bidx, dest, q_mix = call(
         halo_kernel,
         (
             pltpu.VMEM((FLAT, W), F32),
             sds((HALO_ROWS, W), BF16),
             sds((HALO_ROWS, W), BF16),
+            pltpu.VMEM((LEV, 2, 2, W), F32),
+            pltpu.VMEM((STEPS, NT), jnp.int32),
+            pltpu.VMEM((STEPS, 2 * W), jnp.int32),
+            pltpu.VMEM((2 * W, 2 * W), F32),
         ),
-        in_specs=[SM, HB, HB],
+        in_specs=[SM, HB, HB, HB, HB, HB, HB],
         scratch=[
             pltpu.VMEM((ROWS, W), jnp.int32),
             pltpu.VMEM((HALO_ROWS, W), F32),
             pltpu.VMEM((HALO_ROWS, W), F32),
             pltpu.VMEM((ROWS, W), F32),
-            pltpu.SemaphoreType.DMA((2,)),
+            pltpu.SemaphoreType.DMA((6,)),
         ],
         name="halo",
         nbytes=1 << 20,
-    )(tile, in_hbm(parent), in_hbm(terrain))
-    nest, down, up = lax.optimization_barrier((nest, down, up))
-    nest = in_hbm(nest)
+    )(
+        tile,
+        in_hbm(parent),
+        in_hbm(terrain),
+        in_hbm(nest),
+        in_hbm(boundary_index),
+        in_hbm(reloc_dest),
+        in_hbm(q_mix),
+    )
     message = call(
         send_kernel,
         sds((4 * NT, W), F32),
-        in_specs=[HB] * 5,
+        in_specs=[HB, VM, VM, VM, VM],
         scratch=[
             pltpu.SMEM((STEPS,), jnp.int32),
-            pltpu.VMEM((LEV, 2, 2, W), F32),
-            pltpu.VMEM((STEPS, NT), jnp.int32),
-            pltpu.VMEM((STEPS, 2 * W), jnp.int32),
-            pltpu.VMEM((2 * W, 2 * W), F32),
             pltpu.VMEM((2, 2 * W, W), F32),
-            pltpu.SemaphoreType.DMA((5,)),
+            pltpu.SemaphoreType.DMA((1,)),
         ],
         name="send",
         nbytes=64 << 20,
-    )(
-        in_hbm(shift_x),
-        nest,
-        in_hbm(boundary_index),
-        in_hbm(reloc_dest),
-        in_hbm(q_mix),
-    )
+    )(in_hbm(shift_x), nest, bidx, dest, q_mix)
     pairs = [(i, i + 1) for i in range(0, NT, 2)] + [(i + 1, i) for i in range(0, NT, 2)]
     gaps = [(i, i + 1) for i in range(1, NT - 1, 2)]
     gaps = gaps + [(i + 1, i) for i in range(1, NT - 1, 2)]
@@ -594,13 +613,13 @@
 
     values = call(
         gather_kernel,
-        sds((16 * NT, W), BF16),
-        scratch=[pltpu.VMEM((16 * NT, W), F32)],
+        sds((PACK * NT, W), BF16),
+        scratch=[pltpu.VMEM((PACK * NT, W), F32)],
         name="gather",
         flops=1 << 29,
         nbytes=3 << 20,
     )(first, cells)
-    second = exchange(values.reshape(NT, 16, W)).reshape(16 * NT, W)
+    second = exchange(values.reshape(PACK // 4 * NT, 4, W)).reshape(PACK * NT, W)
 
     parent_out = call(
         last_parent_kernel,
@@ -629,7 +648,7 @@
     edges = call(
         regroup_kernel,
         sds((8 * NT, W), BF16),
-        scratch=[pltpu.VMEM((16 * NT, W), F32), pltpu.VMEM((8 * NT, W), F32)],
+        scratch=[pltpu.VMEM((PACK * NT, W), F32), pltpu.VMEM((8 * NT, W), F32)],
         name="regroup",
         flops=1 << 26,
         nbytes=1 << 20,

time: 111 us -> 108 us (0.973)
  waiting for transfers between devices: 26 us -> 23.3 us
    all_to_all x3, waiting for transfers between devices: 25.7 us -> 23.1 us  [exchange(): return lax.all_to_all(x, 'tile', split_axis=0, concat_axis=0, tiled=True)]
where the time goes in v5:
time: 108 us; the launch traced here: 107 us
  starting transfers between devices  42.4 us (39%)
  waiting for transfers between devices  23.3 us (22%)
  Pallas kernels  21.5 us (20%)
  blocking collectives  18 us (17%)
    all_to_all x3, starting transfers between devices, exchange(): return lax.all_to_all(x, 'tile', split_axis=0, concat_axis=0, tiled=True)  34.3 us
    all_to_all x3, waiting for transfers between devices, exchange(): return lax.all_to_all(x, 'tile', split_axis=0, concat_axis=0, tiled=True)  23.1 us
    all_to_all x1, blocking collectives, exchange(): return lax.all_to_all(x, 'tile', split_axis=0, concat_axis=0, tiled=True)  18 us
    pallas_call x1, Pallas kernels, on_device(): call(parent_kernel, (pltpu.VMEM((STEPS, 2 * W, ROWS * W), BF16), pltpu.HB...  6.66 us
    ppermute x1, starting transfers between devices, on_device(): other = lax.ppermute(nest_out, 'member', [(0, 1), (1, 0)])  5.15 us
    pallas_call x1, Pallas kernels, on_device(): call(last_parent_kernel, sds((2 * LEV, ROWS, W), F32), in_specs=[HB, HB],...  3.31 us
    pallas_call x1, Pallas kernels, on_device(): call(plan_kernel, (sds((2, 4 * NT, 4 * NT), BF16), sds((4 * NT, W), F32))...  3.12 us
    pallas_call x1, Pallas kernels, on_device(): call(gather_kernel, sds((PACK * NT, W), BF16), scratch=[pltpu.VMEM((PACK...  2.62 us
  transfers between devices with their start and end apart: 6, of which 4 were waited for; matrix products, arithmetic and copies ran while one was open for 1% of the time, Pallas kernels for 12%

profile of v5, /device:TPU:1, one launch (start us, length us, event | category | flops | bytes accessed | tf_op | source)
XLA Modules:
  0.0 107.1 jit_solution(13251303805806088750)
XLA Ops:
  0.6 1.5 %halo.1 = (f32[1296,128]{1,0:T(8,128)S(1)}, bf16[992,128]{1,0:T(8,128)(2,1)S(1)}, bf16[992,128]{1,0:T(8,128)(2,1)S(1)}, f32[81,2,2,128]{3,2,1,0:T(2,128)S(1)}, s...) custom-call(s32[1]{0:T(128)} %bitcast.tile_ref, f32[1296,128]{1,0:T(8,128)} %bitcast.22, ...), custom_call_target="tpu_custom_call" | custom-call | bytes 1048576 | tf_op jit(solution)/shard_map/halo/pallas_call | solution.py:542
  2.1 2.2 %collective-permute-start = (bf16[992,128]{1,0:T(8,128)(2,1)S(1)}, bf16[992,128]{1,0:T(8,128)(2,1)S(1)}, u32[]{:S(2)}, u32[]{:S(2)}) collective-permute-start(bf16[992,128]{1,0:T(8,128)(2,1)S(1)} %get-tuple-element.24), channel_id=1, source_target_pairs={{0,1},{2,3},{4,5},{6,7},{8,9},{10,11},{12,13},{14,15},{16,17},{18,... | collective-permute-start | bytes 761864 | tf_op jit(solution)/shard_map/ppermute | solution.py:587
  4.3 0.7 collective-permute-start.1
  5.0 1.7 %send.1 = f32[512,128]{1,0:T(8,128)} custom-call(s32[4]{0:T(128)} %shift_hbm.1, f32[81,2,2,128]{3,2,1,0:T(2,128)S(1)} %get-tuple-element.19.nest_ref, s32[4,128]{1,0:T(4,128)S(1)} %get-tuple-element.20.bidx_ref, s32[4,256]{1,0:T(4,128)S(1)} %get-tuple-element.21.dest_ref, f32[256,256]{1,0:T(8,128)S(1)} %get-tuple-element.22.mix_ref), custom_call_target="tpu_custom_call" | custom-call | bytes 67108864 | tf_op jit(solution)/shard_map/send/pallas_call | solution.py:572
  6.7 17.5 %all-to-all-start = ((f32[128,4,128]{2,1,0:T(4,128)}), f32[128,4,128]{2,1,0:T(4,128)}, u32[]{:S(2)}, u32[]{:S(2)}) async-start(f32[128,4,128]{2,1,0:T(4,128)} %bitcast.4), calls=%async_computation | async-start | bytes 524288 | tf_op jit(solution)/shard_map/all_to_all | solution.py:531
  24.2 0.0 collective-permute-done.first_ref
  24.2 0.0 collective-permute-done.1.second_ref
  24.2 6.7 %parent.1 = (bf16[4,256,1024]{2,1,0:T(8,128)(2,1)S(1)}, f32[3072,128]{1,0:T(8,128)}) custom-call(s32[1]{0:T(128)} %bitcast.tile_ref, f32[1296,128]{1,0:T(8,128)S(1)} %get-tuple-element.23.parent_ref, bf16[992,128]{1,0:T(8,128)(2,1)S(1)} %collective-permute-done.first_ref, bf16[992,128]{1,0:T(8,128)(2,1)S(1)} %collective-permute-done.1.second_ref, ...), custom_call_target="tpu_custom_call" | custom-call | flops 1099511627776 | bytes 68719476736 | tf_op jit(solution)/shard_map/parent/pallas_call | solution.py:590
  30.9 0.0 copy-start.1
  30.9 4.8 %all-to-all-done = f32[128,4,128]{2,1,0:T(4,128)} async-done(((f32[128,4,128]{2,1,0:T(4,128)}), f32[128,4,128]{2,1,0:T(4,128)}, u32[]{:S(2)}, u32[]{:S(2)}) %all-to-all-start) | async-done | bytes 262176 | tf_op jit(solution)/shard_map/all_to_all | solution.py:531
  35.7 2.6 %gather.1 = bf16[1536,128]{1,0:T(8,128)(2,1)} custom-call(f32[512,128]{1,0:T(8,128)} %bitcast.5.got_ref, bf16[4,256,1024]{2,1,0:T(8,128)(2,1)S(1)} %get-tuple-element.26.cells_ref), custom_call_target="tpu_custom_call" | custom-call | flops 536870912 | bytes 3145728 | tf_op jit(solution)/shard_map/gather/pallas_call | solution.py:614
  38.3 8.4 %all-to-all-start.1 = ((bf16[384,4,128]{2,1,0:T(4,128)(2,1)}), bf16[384,4,128]{2,1,0:T(4,128)(2,1)S(1)}, u32[]{:S(2)}, u32[]{:S(2)}) async-start(bf16[384,4,128]{2,1,0:T(4,128)(2,1)} %bitcast.6), calls=%async_computation.1 | async-start | bytes 786432 | tf_op jit(solution)/shard_map/all_to_all | solution.py:531
  46.7 0.0 copy-done.1
  46.7 0.1 reshape.64
  46.8 0.1 copy.14
  46.9 0.1 reshape.65.bperm_ref
  47.0 0.0 copy-start
  47.0 3.3 %last_parent.1 = f32[162,8,128]{2,1,0:T(8,128)} custom-call(f32[3072,128]{1,0:T(8,128)} %get-tuple-element.27.ring_hbm, s32[8,128]{1,0:T(8,128)} %terrain_hbm.5), custom_call_target="tpu_custom_call" | custom-call | flops 4194304 | bytes 2097152 | tf_op jit(solution)/shard_map/last_parent/pallas_call | solution.py:624
  50.3 9.7 %all-to-all-done.1 = bf16[384,4,128]{2,1,0:T(4,128)(2,1)S(1)} async-done(((bf16[384,4,128]{2,1,0:T(4,128)(2,1)}), bf16[384,4,128]{2,1,0:T(4,128)(2,1)S(1)}, u32[]{:S(2)}, u32[]{:S(2)}) %all-to-all-start.1) | async-done | bytes 393248 | tf_op jit(solution)/shard_map/all_to_all | solution.py:531
  60.0 1.1 %regroup.1 = bf16[1024,128]{1,0:T(8,128)(2,1)} custom-call(s32[4,128]{1,0:T(4,128)S(1)} %reshape.65.bperm_ref, bf16[1536,128]{1,0:T(8,128)(2,1)S(1)} %bitcast.18), custom_call_target="tpu_custom_call" | custom-call | flops 67108864 | bytes 1048576 | tf_op jit(solution)/shard_map/regroup/pallas_call | solution.py:648
  61.1 8.5 %all-to-all-start.2 = ((bf16[128,8,128]{2,1,0:T(8,128)(2,1)}), bf16[128,8,128]{2,1,0:T(8,128)(2,1)S(1)}, u32[]{:S(2)}, u32[]{:S(2)}) async-start(bf16[128,8,128]{2,1,0:T(8,128)(2,1)} %bitcast.10), calls=%async_computation.2 | async-start | bytes 524288 | tf_op jit(solution)/shard_map/all_to_all | solution.py:531
  69.6 3.1 %plan.1 = (bf16[2,512,512]{2,1,0:T(8,128)(2,1)S(1)}, f32[512,128]{1,0:T(8,128)S(1)}) custom-call(s32[1]{0:T(128)} %bitcast.tile_ref, f32[512,128]{1,0:T(8,128)} %bitcast.5.got_ref), custom_call_target="tpu_custom_call" | custom-call | flops 268435456 | bytes 3145728 | tf_op jit(solution)/shard_map/plan/pallas_call | solution.py:637
  72.7 8.6 %all-to-all-done.2 = bf16[128,8,128]{2,1,0:T(8,128)(2,1)S(1)} async-done(((bf16[128,8,128]{2,1,0:T(8,128)(2,1)}), bf16[128,8,128]{2,1,0:T(8,128)(2,1)S(1)}, u32[]{:S(2)}, u32[]{:S(2)}) %all-to-all-start.2) | async-done | bytes 262176 | tf_op jit(solution)/shard_map/all_to_all | solution.py:531
  81.4 0.0 copy-done
  81.4 0.6 owner.1
  82.0 18.0 %all_to_all.20 = f32[128,4,128]{2,1,0:T(4,128)S(1)} all-to-all(f32[128,4,128]{2,1,0:T(4,128)S(1)} %bitcast.20), channel_id=1, replica_groups=mesh['member'=2,'tile'=128] {'tile'}, dimensions={0} | all-to-all | bytes 524288 | tf_op jit(solution)/shard_map/all_to_all | solution.py:531
  100.0 0.2 nest.1.own_ref
  100.2 5.1 %collective-permute-start.2 = (f32[324,128]{1,0:T(8,128)S(1)}, f32[324,128]{1,0:T(8,128)S(1)}, u32[]{:S(2)}, u32[]{:S(2)}) collective-permute-start(f32[324,128]{1,0:T(8,128)S(1)} %nest.1.own_ref), channel_id=1, source_target_pairs={{0,128},{128,0},{1,129},{129,1},{2,130},{130,2},{3,131},{131,3},{4... | collective-permute-start | bytes 497672 | tf_op jit(solution)/shard_map/ppermute | solution.py:676
  105.3 0.8 reshape.70
  106.1 0.3 collective-permute-done.2.other_ref
  106.4 0.7 stats.1
Async XLA Ops:
  2.1 22.1 %collective-permute-start = (bf16[992,128]{1,0:T(8,128)(2,1)S(1)}, bf16[992,128]{1,0:T(8,128)(2,1)S(1)}, u32[]{:S(2)}, u32[]{:S(2)}) collective-permute-start(bf16[992,128]{1,0:T(8,128)(2,1)S(1)} %get-tuple-element.24), channel_id=1, source_target_pairs={{0,1},{2,3},{4,5},{6,7},{8,9},{10,11},{12,13},{14,15},{16,17},{18,... | collective-permute-start | bytes 761864 | tf_op jit(solution)/shard_map/ppermute | solution.py:587
  4.3 19.9 %collective-permute-start.1 = (bf16[992,128]{1,0:T(8,128)(2,1)S(1)}, bf16[992,128]{1,0:T(8,128)(2,1)S(1)}, u32[]{:S(2)}, u32[]{:S(2)}) collective-permute-start(bf16[992,128]{1,0:T(8,128)(2,1)S(1)} %get-tuple-element.25), channel_id=1, source_target_pairs={{1,2},{3,4},{5,6},{7,8},{9,10},{11,12},{13,14},{15,16},{17,18},{19... | collective-permute-start | bytes 761864 | tf_op jit(solution)/shard_map/ppermute | solution.py:588
  6.7 29.0 %all-to-all-start = ((f32[128,4,128]{2,1,0:T(4,128)}), f32[128,4,128]{2,1,0:T(4,128)}, u32[]{:S(2)}, u32[]{:S(2)}) async-start(f32[128,4,128]{2,1,0:T(4,128)} %bitcast.4), calls=%async_computation | async-start | bytes 524288 | tf_op jit(solution)/shard_map/all_to_all | solution.py:531
  30.9 15.8 %copy-start.1 = (s32[4,128]{1,0:T(4,128)S(1)}, s32[4,128]{1,0:T(4,128)}, u32[]{:S(2)}) copy-start(s32[4,128]{1,0:T(4,128)} %bidx_hbm.1) | copy-start | bytes 6148
  38.3 21.7 %all-to-all-start.1 = ((bf16[384,4,128]{2,1,0:T(4,128)(2,1)}), bf16[384,4,128]{2,1,0:T(4,128)(2,1)S(1)}, u32[]{:S(2)}, u32[]{:S(2)}) async-start(bf16[384,4,128]{2,1,0:T(4,128)(2,1)} %bitcast.6), calls=%async_computation.1 | async-start | bytes 786432 | tf_op jit(solution)/shard_map/all_to_all | solution.py:531
  47.0 34.3 %copy-start = (bf16[2,256,384]{2,1,0:T(8,128)(2,1)S(1)}, bf16[2,256,384]{2,1,0:T(8,128)(2,1)}, u32[]{:S(2)}) copy-start(bf16[2,256,384]{2,1,0:T(8,128)(2,1)} %constant.9.clone.mix_ref) | copy-start | bytes 1179652
  61.1 20.2 %all-to-all-start.2 = ((bf16[128,8,128]{2,1,0:T(8,128)(2,1)}), bf16[128,8,128]{2,1,0:T(8,128)(2,1)S(1)}, u32[]{:S(2)}, u32[]{:S(2)}) async-start(bf16[128,8,128]{2,1,0:T(8,128)(2,1)} %bitcast.10), calls=%async_computation.2 | async-start | bytes 524288 | tf_op jit(solution)/shard_map/all_to_all | solution.py:531
  100.2 6.2 %collective-permute-start.2 = (f32[324,128]{1,0:T(8,128)S(1)}, f32[324,128]{1,0:T(8,128)S(1)}, u32[]{:S(2)}, u32[]{:S(2)}) collective-permute-start(f32[324,128]{1,0:T(8,128)S(1)} %nest.1.own_ref), channel_id=1, source_target_pairs={{0,128},{128,0},{1,129},{129,1},{2,130},{130,2},{3,131},{131,3},{4... | collective-permute-start | bytes 497672 | tf_op jit(solution)/shard_map/ppermute | solution.py:676

commit v6 on v5

--- a/solution.py
+++ b/solution.py
@@ -242,7 +242,7 @@
 
 
 def parent_kernel(
-    tile_ref, parent_ref, first_ref, second_ref, terrain_hbm,
+    tile_ref, parent_ref, second_ref, first_ref, terrain_hbm,
     cells_ref, ring_hbm,
     next_ref, prev_ref, halo_ref, damp_ref, a_ref, b_ref, ring_ref, terrain_ref, sems,
 ):
@@ -584,8 +584,8 @@
     pairs = [(i, i + 1) for i in range(0, NT, 2)] + [(i + 1, i) for i in range(0, NT, 2)]
     gaps = [(i, i + 1) for i in range(1, NT - 1, 2)]
     gaps = gaps + [(i + 1, i) for i in range(1, NT - 1, 2)]
+    from_gap = lax.ppermute(up, "tile", gaps)
     from_pair = lax.ppermute(down, "tile", pairs)
-    from_gap = lax.ppermute(up, "tile", gaps)
     first = exchange(message.reshape(NT, 4, W)).reshape(4 * NT, W)
     cells, ring = call(
         parent_kernel,
@@ -607,9 +607,9 @@
             pltpu.SemaphoreType.DMA((2,)),
         ],
         name="parent",
-        flops=1 << 40,
-        nbytes=1 << 36,
-    )(tile, kept, from_pair, from_gap, in_hbm(terrain))
+        flops=1 << 33,
+        nbytes=1 << 27,
+    )(tile, kept, from_gap, from_pair, in_hbm(terrain))
 
     values = call(
         gather_kernel,
@@ -620,6 +620,27 @@
         nbytes=3 << 20,
     )(first, cells)
     second = exchange(values.reshape(PACK // 4 * NT, 4, W)).reshape(PACK * NT, W)
+
+    hot, base = call(
+        plan_kernel,
+        (sds((2, 4 * NT, 4 * NT), BF16), sds((4 * NT, W), F32)),
+        in_specs=[SM, VM],
+        name="plan",
+        flops=1 << 28,
+        nbytes=3 << 20,
+    )(tile, first)
+
+    second, hot, base = lax.optimization_barrier((second, hot, base))
+    bperm = boundary_index.reshape(STEPS, 32, 4).transpose(0, 2, 1).reshape(STEPS, NT)
+    edges = call(
+        regroup_kernel,
+        sds((8 * NT, W), BF16),
+        scratch=[pltpu.VMEM((PACK * NT, W), F32), pltpu.VMEM((8 * NT, W), F32)],
+        name="regroup",
+        flops=1 << 26,
+        nbytes=1 << 20,
+    )(bperm, second)
+    third = exchange(edges.reshape(NT, 8, W)).reshape(8 * NT, W)
 
     parent_out = call(
         last_parent_kernel,
@@ -634,27 +655,7 @@
         flops=1 << 22,
         nbytes=2 << 20,
     )(in_hbm(ring), in_hbm(terrain))
-    hot, base = call(
-        plan_kernel,
-        (sds((2, 4 * NT, 4 * NT), BF16), sds((4 * NT, W), F32)),
-        in_specs=[SM, VM],
-        name="plan",
-        flops=1 << 28,
-        nbytes=3 << 20,
-    )(tile, first)
-
-    second, parent_out = lax.optimization_barrier((second, parent_out))
-    bperm = boundary_index.reshape(STEPS, 32, 4).transpose(0, 2, 1).reshape(STEPS, NT)
-    edges = call(
-        regroup_kernel,
-        sds((8 * NT, W), BF16),
-        scratch=[pltpu.VMEM((PACK * NT, W), F32), pltpu.VMEM((8 * NT, W), F32)],
-        name="regroup",
-        flops=1 << 26,
-        nbytes=1 << 20,
-    )(bperm, second)
-    third = exchange(edges.reshape(NT, 8, W)).reshape(8 * NT, W)
-
+    third, parent_out = lax.optimization_barrier((third, parent_out))
     columns = call(
         owner_kernel,
         sds((4 * NT, W), F32),

time: 108 us -> 106 us (0.981)
  Pallas kernels: 21.5 us -> 19.6 us
  waiting for transfers between devices: 23.3 us -> 25 us
  starting transfers between devices: 42.4 us -> 41.2 us
    all_to_all x3, starting transfers between devices: 34.3 us -> 30.6 us  [exchange(): return lax.all_to_all(x, 'tile', split_axis=0, concat_axis=0, tiled=True)]
    ppermute x1, starting transfers between devices: 2.21 us -> 4.74 us  [on_device(): from_pair = lax.ppermute(down, 'tile', pairs)]
    all_to_all x3, waiting for transfers between devices: 23.1 us -> 24.7 us  [exchange(): return lax.all_to_all(x, 'tile', split_axis=0, concat_axis=0, tiled=True)]
  transfers between devices with their start and end apart: 6 -> 6, of which waited for: 4 -> 4; matrix products, arithmetic and copies ran while one was open for 1% -> 1% of each run, Pallas kernels for 12% -> 11%
where the time goes in v6:
time: 106 us
  starting transfers between devices  41.2 us (39%)
  waiting for transfers between devices  25 us (24%)
  Pallas kernels  19.6 us (18%)
  blocking collectives  18 us (17%)
    all_to_all x3, starting transfers between devices, exchange(): return lax.all_to_all(x, 'tile', split_axis=0, concat_axis=0, tiled=True)  30.6 us
    all_to_all x3, waiting for transfers between devices, exchange(): return lax.all_to_all(x, 'tile', split_axis=0, concat_axis=0, tiled=True)  24.7 us
    all_to_all x1, blocking collectives, exchange(): return lax.all_to_all(x, 'tile', split_axis=0, concat_axis=0, tiled=True)  18 us
    pallas_call x1, Pallas kernels, on_device(): call(parent_kernel, (pltpu.VMEM((STEPS, 2 * W, ROWS * W), BF16), pltpu.HB...  6.66 us
    ppermute x1, starting transfers between devices, on_device(): other = lax.ppermute(nest_out, 'member', [(0, 1), (1, 0)])  5.15 us
    ppermute x1, starting transfers between devices, on_device(): from_pair = lax.ppermute(down, 'tile', pairs)  4.74 us
    pallas_call x1, Pallas kernels, on_device(): call(last_parent_kernel, sds((2 * LEV, ROWS, W), F32), in_specs=[HB, HB],...  3.25 us
    pallas_call x1, Pallas kernels, on_device(): call(plan_kernel, (sds((2, 4 * NT, 4 * NT), BF16), sds((4 * NT, W), F32))...  2.18 us
  transfers between devices with their start and end apart: 6, of which 4 were waited for; matrix products, arithmetic and copies ran while one was open for 1% of the time, Pallas kernels for 11%

profile of v6, /device:TPU:1, one launch (start us, length us, event | category | flops | bytes accessed | tf_op | source)
XLA Modules:
  0.0 105.6 jit_solution(14737790454352689243)
XLA Ops:
  0.6 1.5 %halo.1 = (f32[1296,128]{1,0:T(8,128)S(1)}, bf16[992,128]{1,0:T(8,128)(2,1)S(1)}, bf16[992,128]{1,0:T(8,128)(2,1)S(1)}, f32[81,2,2,128]{3,2,1,0:T(2,128)S(1)}, s...) custom-call(s32[1]{0:T(128)} %bitcast.1.tile_ref, f32[1296,128]{1,0:T(8,128)} %bitcast.24, ...), custom_call_target="tpu_custom_call" | custom-call | bytes 1048576 | tf_op jit(solution)/shard_map/halo/pallas_call | solution.py:542
  2.1 0.7 collective-permute-start
  2.8 4.7 %collective-permute-start.1 = (bf16[992,128]{1,0:T(8,128)(2,1)S(1)}, bf16[992,128]{1,0:T(8,128)(2,1)S(1)}, u32[]{:S(2)}, u32[]{:S(2)}) collective-permute-start(bf16[992,128]{1,0:T(8,128)(2,1)S(1)} %get-tuple-element.28), channel_id=1, source_target_pairs={{0,1},{2,3},{4,5},{6,7},{8,9},{10,11},{12,13},{14,15},{16,17},{18,... | collective-permute-start | bytes 761864 | tf_op jit(solution)/shard_map/ppermute | solution.py:588
  7.5 1.7 %send.1 = f32[512,128]{1,0:T(8,128)} custom-call(s32[4]{0:T(128)} %shift_hbm.1, f32[81,2,2,128]{3,2,1,0:T(2,128)S(1)} %get-tuple-element.22.nest_ref, s32[4,128]{1,0:T(4,128)S(1)} %get-tuple-element.23.bidx_ref, s32[4,256]{1,0:T(4,128)S(1)} %get-tuple-element.24.dest_ref, f32[256,256]{1,0:T(8,128)S(1)} %get-tuple-element.25.mix_ref), custom_call_target="tpu_custom_call" | custom-call | bytes 67108864 | tf_op jit(solution)/shard_map/send/pallas_call | solution.py:572
  9.3 14.3 %all-to-all-start = ((f32[128,4,128]{2,1,0:T(4,128)}), f32[128,4,128]{2,1,0:T(4,128)S(1)}, u32[]{:S(2)}, u32[]{:S(2)}) async-start(f32[128,4,128]{2,1,0:T(4,128)} %bitcast.5), calls=%async_computation | async-start | bytes 524288 | tf_op jit(solution)/shard_map/all_to_all | solution.py:531
  23.6 0.0 collective-permute-done.second_ref
  23.6 0.0 collective-permute-done.1.first_ref
  23.6 6.7 %parent.1 = (bf16[4,256,1024]{2,1,0:T(8,128)(2,1)S(1)}, f32[3072,128]{1,0:T(8,128)}) custom-call(s32[1]{0:T(128)} %bitcast.1.tile_ref, f32[1296,128]{1,0:T(8,128)S(1)} %get-tuple-element.26.parent_ref, bf16[992,128]{1,0:T(8,128)(2,1)S(1)} %collective-permute-done.second_ref, bf16[992,128]{1,0:T(8,128)(2,1)S(1)} %collective-permute-done.1.first_ref, ...), custom_call_target="tpu_custom_call" | custom-call | flops 8589934592 | bytes 134217728 | tf_op jit(solution)/shard_map/parent/pallas_call | solution.py:590
  30.3 0.0 copy-start.1
  30.3 5.2 %all-to-all-done = f32[128,4,128]{2,1,0:T(4,128)S(1)} async-done(((f32[128,4,128]{2,1,0:T(4,128)}), f32[128,4,128]{2,1,0:T(4,128)S(1)}, u32[]{:S(2)}, u32[]{:S(2)}) %all-to-all-start) | async-done | bytes 262176 | tf_op jit(solution)/shard_map/all_to_all | solution.py:531
  35.5 1.7 %gather.1 = bf16[1536,128]{1,0:T(8,128)(2,1)} custom-call(f32[512,128]{1,0:T(8,128)S(1)} %bitcast.22, bf16[4,256,1024]{2,1,0:T(8,128)(2,1)S(1)} %get-tuple-element.29.cells_ref), custom_call_target="tpu_custom_call" | custom-call | flops 536870912 | bytes 3145728 | tf_op jit(solution)/shard_map/gather/pallas_call | solution.py:614
  37.2 8.0 %all-to-all-start.1 = ((bf16[384,4,128]{2,1,0:T(4,128)(2,1)}), bf16[384,4,128]{2,1,0:T(4,128)(2,1)S(1)}, u32[]{:S(2)}, u32[]{:S(2)}) async-start(bf16[384,4,128]{2,1,0:T(4,128)(2,1)} %bitcast.7), calls=%async_computation.1 | async-start | bytes 786432 | tf_op jit(solution)/shard_map/all_to_all | solution.py:531
  45.2 0.0 copy-done.1
  45.2 0.1 reshape.56
  45.3 0.1 copy.14
  45.4 0.1 reshape.57.bperm_ref
  45.5 0.0 copy-start
  45.5 2.2 %plan.1 = (bf16[2,512,512]{2,1,0:T(8,128)(2,1)S(1)}, f32[512,128]{1,0:T(8,128)S(1)}) custom-call(s32[1]{0:T(128)} %bitcast.1.tile_ref, f32[512,128]{1,0:T(8,128)S(1)} %bitcast.23), custom_call_target="tpu_custom_call" | custom-call | flops 268435456 | bytes 3145728 | tf_op jit(solution)/shard_map/plan/pallas_call | solution.py:624
  47.7 10.8 %all-to-all-done.1 = bf16[384,4,128]{2,1,0:T(4,128)(2,1)S(1)} async-done(((bf16[384,4,128]{2,1,0:T(4,128)(2,1)}), bf16[384,4,128]{2,1,0:T(4,128)(2,1)S(1)}, u32[]{:S(2)}, u32[]{:S(2)}) %all-to-all-start.1) | async-done | bytes 393248 | tf_op jit(solution)/shard_map/all_to_all | solution.py:531
  58.5 1.2 %regroup.1 = bf16[1024,128]{1,0:T(8,128)(2,1)} custom-call(s32[4,128]{1,0:T(4,128)S(1)} %reshape.57.bperm_ref, bf16[1536,128]{1,0:T(8,128)(2,1)S(1)} %bitcast.18), custom_call_target="tpu_custom_call" | custom-call | flops 67108864 | bytes 1048576 | tf_op jit(solution)/shard_map/regroup/pallas_call | solution.py:635
  59.6 8.3 %all-to-all-start.2 = ((bf16[128,8,128]{2,1,0:T(8,128)(2,1)}), bf16[128,8,128]{2,1,0:T(8,128)(2,1)S(1)}, u32[]{:S(2)}, u32[]{:S(2)}) async-start(bf16[128,8,128]{2,1,0:T(8,128)(2,1)} %bitcast.9), calls=%async_computation.2 | async-start | bytes 524288 | tf_op jit(solution)/shard_map/all_to_all | solution.py:531
  67.9 3.3 %last_parent.1 = f32[162,8,128]{2,1,0:T(8,128)} custom-call(f32[3072,128]{1,0:T(8,128)} %get-tuple-element.33.ring_hbm, s32[8,128]{1,0:T(8,128)} %terrain_hbm.5), custom_call_target="tpu_custom_call" | custom-call | flops 4194304 | bytes 2097152 | tf_op jit(solution)/shard_map/last_parent/pallas_call | solution.py:645
  71.2 8.7 %all-to-all-done.2 = bf16[128,8,128]{2,1,0:T(8,128)(2,1)S(1)} async-done(((bf16[128,8,128]{2,1,0:T(8,128)(2,1)}), bf16[128,8,128]{2,1,0:T(8,128)(2,1)S(1)}, u32[]{:S(2)}, u32[]{:S(2)}) %all-to-all-start.2) | async-done | bytes 262176 | tf_op jit(solution)/shard_map/all_to_all | solution.py:531
  79.9 0.0 copy-done
  79.9 0.6 owner.1
  80.5 18.0 %all_to_all.20 = f32[128,4,128]{2,1,0:T(4,128)S(1)} all-to-all(f32[128,4,128]{2,1,0:T(4,128)S(1)} %bitcast.20), channel_id=1, replica_groups=mesh['member'=2,'tile'=128] {'tile'}, dimensions={0} | all-to-all | bytes 524288 | tf_op jit(solution)/shard_map/all_to_all | solution.py:531
  98.5 0.2 nest.1.own_ref
  98.7 5.1 %collective-permute-start.2 = (f32[324,128]{1,0:T(8,128)S(1)}, f32[324,128]{1,0:T(8,128)S(1)}, u32[]{:S(2)}, u32[]{:S(2)}) collective-permute-start(f32[324,128]{1,0:T(8,128)S(1)} %nest.1.own_ref), channel_id=1, source_target_pairs={{0,128},{128,0},{1,129},{129,1},{2,130},{130,2},{3,131},{131,3},{4... | collective-permute-start | bytes 497672 | tf_op jit(solution)/shard_map/ppermute | solution.py:677
  103.8 0.8 reshape.70
  104.6 0.3 collective-permute-done.2.other_ref
  104.9 0.7 stats.1
Async XLA Ops:
  2.1 21.5 %collective-permute-start = (bf16[992,128]{1,0:T(8,128)(2,1)S(1)}, bf16[992,128]{1,0:T(8,128)(2,1)S(1)}, u32[]{:S(2)}, u32[]{:S(2)}) collective-permute-start(bf16[992,128]{1,0:T(8,128)(2,1)S(1)} %get-tuple-element.27), channel_id=1, source_target_pairs={{1,2},{3,4},{5,6},{7,8},{9,10},{11,12},{13,14},{15,16},{17,18},{19... | collective-permute-start | bytes 761864 | tf_op jit(solution)/shard_map/ppermute | solution.py:587
  2.8 20.8 %collective-permute-start.1 = (bf16[992,128]{1,0:T(8,128)(2,1)S(1)}, bf16[992,128]{1,0:T(8,128)(2,1)S(1)}, u32[]{:S(2)}, u32[]{:S(2)}) collective-permute-start(bf16[992,128]{1,0:T(8,128)(2,1)S(1)} %get-tuple-element.28), channel_id=1, source_target_pairs={{0,1},{2,3},{4,5},{6,7},{8,9},{10,11},{12,13},{14,15},{16,17},{18,... | collective-permute-start | bytes 761864 | tf_op jit(solution)/shard_map/ppermute | solution.py:588
  9.3 26.3 %all-to-all-start = ((f32[128,4,128]{2,1,0:T(4,128)}), f32[128,4,128]{2,1,0:T(4,128)S(1)}, u32[]{:S(2)}, u32[]{:S(2)}) async-start(f32[128,4,128]{2,1,0:T(4,128)} %bitcast.5), calls=%async_computation | async-start | bytes 524288 | tf_op jit(solution)/shard_map/all_to_all | solution.py:531
  30.3 14.9 %copy-start.1 = (s32[4,128]{1,0:T(4,128)S(1)}, s32[4,128]{1,0:T(4,128)}, u32[]{:S(2)}) copy-start(s32[4,128]{1,0:T(4,128)} %bidx_hbm.1) | copy-start | bytes 6148
  37.2 21.3 %all-to-all-start.1 = ((bf16[384,4,128]{2,1,0:T(4,128)(2,1)}), bf16[384,4,128]{2,1,0:T(4,128)(2,1)S(1)}, u32[]{:S(2)}, u32[]{:S(2)}) async-start(bf16[384,4,128]{2,1,0:T(4,128)(2,1)} %bitcast.7), calls=%async_computation.1 | async-start | bytes 786432 | tf_op jit(solution)/shard_map/all_to_all | solution.py:531
  45.5 34.3 %copy-start = (bf16[2,256,384]{2,1,0:T(8,128)(2,1)S(1)}, bf16[2,256,384]{2,1,0:T(8,128)(2,1)}, u32[]{:S(2)}) copy-start(bf16[2,256,384]{2,1,0:T(8,128)(2,1)} %constant.9.clone.mix_ref) | copy-start | bytes 1179652
  59.6 20.2 %all-to-all-start.2 = ((bf16[128,8,128]{2,1,0:T(8,128)(2,1)}), bf16[128,8,128]{2,1,0:T(8,128)(2,1)S(1)}, u32[]{:S(2)}, u32[]{:S(2)}) async-start(bf16[128,8,128]{2,1,0:T(8,128)(2,1)} %bitcast.9), calls=%async_computation.2 | async-start | bytes 524288 | tf_op jit(solution)/shard_map/all_to_all | solution.py:531
  98.7 6.2 %collective-permute-start.2 = (f32[324,128]{1,0:T(8,128)S(1)}, f32[324,128]{1,0:T(8,128)S(1)}, u32[]{:S(2)}, u32[]{:S(2)}) collective-permute-start(f32[324,128]{1,0:T(8,128)S(1)} %nest.1.own_ref), channel_id=1, source_target_pairs={{0,128},{128,0},{1,129},{129,1},{2,130},{130,2},{3,131},{131,3},{4... | collective-permute-start | bytes 497672 | tf_op jit(solution)/shard_map/ppermute | solution.py:677

commit v7 on v6

--- a/solution.py
+++ b/solution.py
@@ -213,15 +213,14 @@
     chunk = 9
 
     def body(step, carry):
+        start = step * chunk
+        ends = jnp.maximum(start - 1, 0), jnp.minimum(start + chunk, LEV - 1)
         for member in range(2):
+            base = member * level_stride
+            column = [read(base + start + k) for k in range(chunk)]
+            column = [read(base + ends[0])] + column + [read(base + ends[1])]
             for k in range(chunk):
-                level = step * chunk + k
-                base = member * level_stride
-                below = base + jnp.maximum(level - 1, 0)
-                above = base + jnp.minimum(level + 1, LEV - 1)
-                x0, x1 = read(base + level)
-                d0, d1 = read(below)
-                u0, u1 = read(above)
+                (d0, d1), (x0, x1), (u0, u1) = column[k : k + 3]
                 f0 = pltpu.roll(x0, ROWS - 1, 0)
                 f1 = pltpu.roll(x1, ROWS - 1, 0)
                 g0 = pltpu.roll(x0, 1, 0)
@@ -230,12 +229,12 @@
                 near0 = near0 + (pltpu.roll(x0, 1, 1) + pltpu.roll(x0, W - 1, 1))
                 y0 = c0 * x0 + HORIZ * near0 + VERT * (d0 + u0)
                 if own_only:
-                    write(member, level, y0, None)
+                    write(member, start + k, y0, None)
                     continue
                 near1 = jnp.where(last, f0, f1) + jnp.where(head, g0, g1)
                 near1 = near1 + (pltpu.roll(x1, 1, 1) + pltpu.roll(x1, W - 1, 1))
                 y1 = c1 * x1 + h1 * near1 + v1 * (d1 + u1)
-                write(member, level, y0, y1)
+                write(member, start + k, y0, y1)
         return carry
 
     lax.fori_loop(0, LEV // chunk, body, 0)
@@ -607,8 +606,8 @@
             pltpu.SemaphoreType.DMA((2,)),
         ],
         name="parent",
-        flops=1 << 33,
-        nbytes=1 << 27,
+        flops=1 << 24,
+        nbytes=4 << 20,
     )(tile, kept, from_gap, from_pair, in_hbm(terrain))
 
     values = call(

time: 106 us -> 113 us (1.066)
  starting transfers between devices: 41.2 us -> 46.2 us
  waiting for transfers between devices: 25 us -> 27.5 us
    ppermute x1, waiting for transfers between devices: 0.01 us -> 7.64 us  [on_device(): from_pair = lax.ppermute(down, 'tile', pairs)]
    all_to_all x3, starting transfers between devices: 30.6 us -> 37.3 us  [exchange(): return lax.all_to_all(x, 'tile', split_axis=0, concat_axis=0, tiled=True)]
    all_to_all x3, waiting for transfers between devices: 24.7 us -> 19.5 us  [exchange(): return lax.all_to_all(x, 'tile', split_axis=0, concat_axis=0, tiled=True)]
    ppermute x1, starting transfers between devices: 4.74 us -> 3.07 us  [on_device(): from_pair = lax.ppermute(down, 'tile', pairs)]
where the time goes in v7:
time: 113 us
  starting transfers between devices  46.2 us (41%)
  waiting for transfers between devices  27.5 us (24%)
  Pallas kernels  19.6 us (17%)
  blocking collectives  18.1 us (16%)
    all_to_all x3, starting transfers between devices, exchange(): return lax.all_to_all(x, 'tile', split_axis=0, concat_axis=0, tiled=True)  37.3 us
    all_to_all x3, waiting for transfers between devices, exchange(): return lax.all_to_all(x, 'tile', split_axis=0, concat_axis=0, tiled=True)  19.5 us
    all_to_all x1, blocking collectives, exchange(): return lax.all_to_all(x, 'tile', split_axis=0, concat_axis=0, tiled=True)  18.1 us
    ppermute x1, waiting for transfers between devices, on_device(): from_pair = lax.ppermute(down, 'tile', pairs)  7.64 us
    pallas_call x1, Pallas kernels, on_device(): call(parent_kernel, (pltpu.VMEM((STEPS, 2 * W, ROWS * W), BF16), pltpu.HB...  6.63 us
    ppermute x1, starting transfers between devices, on_device(): other = lax.ppermute(nest_out, 'member', [(0, 1), (1, 0)])  5.15 us
    pallas_call x1, Pallas kernels, on_device(): call(last_parent_kernel, sds((2 * LEV, ROWS, W), F32), in_specs=[HB, HB],...  3.26 us
    ppermute x1, starting transfers between devices, on_device(): from_pair = lax.ppermute(down, 'tile', pairs)  3.07 us
  transfers between devices with their start and end apart: 6, of which 4 were waited for; matrix products, arithmetic and copies ran while one was open for 1% of the time, Pallas kernels for 11%

profile of v7, /device:TPU:1, one launch (start us, length us, event | category | flops | bytes accessed | tf_op | source)
XLA Modules:
  0.0 113.1 jit_solution(7397851942834300666)
XLA Ops:
  0.6 1.5 %halo.1 = (f32[1296,128]{1,0:T(8,128)S(1)}, bf16[992,128]{1,0:T(8,128)(2,1)S(1)}, bf16[992,128]{1,0:T(8,128)(2,1)S(1)}, f32[81,2,2,128]{3,2,1,0:T(2,128)S(1)}, s...) custom-call(s32[1]{0:T(128)} %bitcast.1.tile_ref, f32[1296,128]{1,0:T(8,128)} %bitcast.24, ...), custom_call_target="tpu_custom_call" | custom-call | bytes 1048576 | tf_op jit(solution)/shard_map/halo/pallas_call | solution.py:541
  2.1 1.7 %send.1 = f32[512,128]{1,0:T(8,128)} custom-call(s32[4]{0:T(128)} %shift_hbm.1, f32[81,2,2,128]{3,2,1,0:T(2,128)S(1)} %get-tuple-element.22.nest_ref, s32[4,128]{1,0:T(4,128)S(1)} %get-tuple-element.23.bidx_ref, s32[4,256]{1,0:T(4,128)S(1)} %get-tuple-element.24.dest_ref, f32[256,256]{1,0:T(8,128)S(1)} %get-tuple-element.25.mix_ref), custom_call_target="tpu_custom_call" | custom-call | bytes 67108864 | tf_op jit(solution)/shard_map/send/pallas_call | solution.py:571
  3.8 16.3 %all-to-all-start = ((f32[128,4,128]{2,1,0:T(4,128)}), f32[128,4,128]{2,1,0:T(4,128)S(1)}, u32[]{:S(2)}, u32[]{:S(2)}) async-start(f32[128,4,128]{2,1,0:T(4,128)} %bitcast.5), calls=%async_computation | async-start | bytes 524288 | tf_op jit(solution)/shard_map/all_to_all | solution.py:530
  20.2 0.7 collective-permute-start
  20.9 3.1 %collective-permute-start.1 = (bf16[992,128]{1,0:T(8,128)(2,1)S(1)}, bf16[992,128]{1,0:T(8,128)(2,1)S(1)}, u32[]{:S(2)}, u32[]{:S(2)}) collective-permute-start(bf16[992,128]{1,0:T(8,128)(2,1)S(1)} %get-tuple-element.28), channel_id=1, source_target_pairs={{0,1},{2,3},{4,5},{6,7},{8,9},{10,11},{12,13},{14,15},{16,17},{18,... | collective-permute-start | bytes 761864 | tf_op jit(solution)/shard_map/ppermute | solution.py:587
  23.9 0.0 collective-permute-done.second_ref
  23.9 7.6 %collective-permute-done.1.first_ref = bf16[992,128]{1,0:T(8,128)(2,1)S(1)} collective-permute-done((bf16[992,128]{1,0:T(8,128)(2,1)S(1)}, bf16[992,128]{1,0:T(8,128)(2,1)S(1)}, u32[]{:S(2)}, u32[]{:S(2)}) %collective-permute-start.1) | collective-permute-done | bytes 253984 | tf_op jit(solution)/shard_map/ppermute | solution.py:587
  31.6 0.0 copy-start.1
  31.6 6.6 %parent.1 = (bf16[4,256,1024]{2,1,0:T(8,128)(2,1)S(1)}, f32[3072,128]{1,0:T(8,128)}) custom-call(s32[1]{0:T(128)} %bitcast.1.tile_ref, f32[1296,128]{1,0:T(8,128)S(1)} %get-tuple-element.26.parent_ref, bf16[992,128]{1,0:T(8,128)(2,1)S(1)} %collective-permute-done.second_ref, bf16[992,128]{1,0:T(8,128)(2,1)S(1)} %collective-permute-done.1.first_ref, ...), custom_call_target="tpu_custom_call" | custom-call | flops 16777216 | bytes 4194304 | tf_op jit(solution)/shard_map/parent/pallas_call | solution.py:589
  38.2 0.0 all-to-all-done
  38.2 1.7 %gather.1 = bf16[1536,128]{1,0:T(8,128)(2,1)} custom-call(f32[512,128]{1,0:T(8,128)S(1)} %bitcast.22, bf16[4,256,1024]{2,1,0:T(8,128)(2,1)S(1)} %get-tuple-element.29.cells_ref), custom_call_target="tpu_custom_call" | custom-call | flops 536870912 | bytes 3145728 | tf_op jit(solution)/shard_map/gather/pallas_call | solution.py:613
  39.9 12.6 %all-to-all-start.1 = ((bf16[384,4,128]{2,1,0:T(4,128)(2,1)}), bf16[384,4,128]{2,1,0:T(4,128)(2,1)S(1)}, u32[]{:S(2)}, u32[]{:S(2)}) async-start(bf16[384,4,128]{2,1,0:T(4,128)(2,1)} %bitcast.7), calls=%async_computation.1 | async-start | bytes 786432 | tf_op jit(solution)/shard_map/all_to_all | solution.py:530
  52.5 0.0 copy-done.1
  52.5 0.1 reshape.56
  52.6 0.1 copy.14
  52.7 0.1 reshape.57.bperm_ref
  52.8 0.0 copy-start
  52.8 2.2 %plan.1 = (bf16[2,512,512]{2,1,0:T(8,128)(2,1)S(1)}, f32[512,128]{1,0:T(8,128)S(1)}) custom-call(s32[1]{0:T(128)} %bitcast.1.tile_ref, f32[512,128]{1,0:T(8,128)S(1)} %bitcast.23), custom_call_target="tpu_custom_call" | custom-call | flops 268435456 | bytes 3145728 | tf_op jit(solution)/shard_map/plan/pallas_call | solution.py:623
  55.0 10.9 %all-to-all-done.1 = bf16[384,4,128]{2,1,0:T(4,128)(2,1)S(1)} async-done(((bf16[384,4,128]{2,1,0:T(4,128)(2,1)}), bf16[384,4,128]{2,1,0:T(4,128)(2,1)S(1)}, u32[]{:S(2)}, u32[]{:S(2)}) %all-to-all-start.1) | async-done | bytes 393248 | tf_op jit(solution)/shard_map/all_to_all | solution.py:530
  65.9 1.2 %regroup.1 = bf16[1024,128]{1,0:T(8,128)(2,1)} custom-call(s32[4,128]{1,0:T(4,128)S(1)} %reshape.57.bperm_ref, bf16[1536,128]{1,0:T(8,128)(2,1)S(1)} %bitcast.18), custom_call_target="tpu_custom_call" | custom-call | flops 67108864 | bytes 1048576 | tf_op jit(solution)/shard_map/regroup/pallas_call | solution.py:634
  67.0 8.4 %all-to-all-start.2 = ((bf16[128,8,128]{2,1,0:T(8,128)(2,1)}), bf16[128,8,128]{2,1,0:T(8,128)(2,1)S(1)}, u32[]{:S(2)}, u32[]{:S(2)}) async-start(bf16[128,8,128]{2,1,0:T(8,128)(2,1)} %bitcast.9), calls=%async_computation.2 | async-start | bytes 524288 | tf_op jit(solution)/shard_map/all_to_all | solution.py:530
  75.4 3.3 %last_parent.1 = f32[162,8,128]{2,1,0:T(8,128)} custom-call(f32[3072,128]{1,0:T(8,128)} %get-tuple-element.33.ring_hbm, s32[8,128]{1,0:T(8,128)} %terrain_hbm.5), custom_call_target="tpu_custom_call" | custom-call | flops 4194304 | bytes 2097152 | tf_op jit(solution)/shard_map/last_parent/pallas_call | solution.py:644
  78.7 8.7 %all-to-all-done.2 = bf16[128,8,128]{2,1,0:T(8,128)(2,1)S(1)} async-done(((bf16[128,8,128]{2,1,0:T(8,128)(2,1)}), bf16[128,8,128]{2,1,0:T(8,128)(2,1)S(1)}, u32[]{:S(2)}, u32[]{:S(2)}) %all-to-all-start.2) | async-done | bytes 262176 | tf_op jit(solution)/shard_map/all_to_all | solution.py:530
  87.3 0.0 copy-done
  87.3 0.6 owner.1
  87.9 18.1 %all_to_all.20 = f32[128,4,128]{2,1,0:T(4,128)S(1)} all-to-all(f32[128,4,128]{2,1,0:T(4,128)S(1)} %bitcast.20), channel_id=1, replica_groups=mesh['member'=2,'tile'=128] {'tile'}, dimensions={0} | all-to-all | bytes 524288 | tf_op jit(solution)/shard_map/all_to_all | solution.py:530
  106.0 0.2 nest.1.own_ref
  106.2 5.1 %collective-permute-start.2 = (f32[324,128]{1,0:T(8,128)S(1)}, f32[324,128]{1,0:T(8,128)S(1)}, u32[]{:S(2)}, u32[]{:S(2)}) collective-permute-start(f32[324,128]{1,0:T(8,128)S(1)} %nest.1.own_ref), channel_id=1, source_target_pairs={{0,128},{128,0},{1,129},{129,1},{2,130},{130,2},{3,131},{131,3},{4... | collective-permute-start | bytes 497672 | tf_op jit(solution)/shard_map/ppermute | solution.py:676
  111.3 0.8 reshape.70
  112.1 0.3 collective-permute-done.2.other_ref
  112.4 0.7 stats.1
Async XLA Ops:
  3.8 34.4 %all-to-all-start = ((f32[128,4,128]{2,1,0:T(4,128)}), f32[128,4,128]{2,1,0:T(4,128)S(1)}, u32[]{:S(2)}, u32[]{:S(2)}) async-start(f32[128,4,128]{2,1,0:T(4,128)} %bitcast.5), calls=%async_computation | async-start | bytes 524288 | tf_op jit(solution)/shard_map/all_to_all | solution.py:530
  20.2 3.8 %collective-permute-start = (bf16[992,128]{1,0:T(8,128)(2,1)S(1)}, bf16[992,128]{1,0:T(8,128)(2,1)S(1)}, u32[]{:S(2)}, u32[]{:S(2)}) collective-permute-start(bf16[992,128]{1,0:T(8,128)(2,1)S(1)} %get-tuple-element.27), channel_id=1, source_target_pairs={{1,2},{3,4},{5,6},{7,8},{9,10},{11,12},{13,14},{15,16},{17,18},{19... | collective-permute-start | bytes 761864 | tf_op jit(solution)/shard_map/ppermute | solution.py:586
  20.9 10.7 %collective-permute-start.1 = (bf16[992,128]{1,0:T(8,128)(2,1)S(1)}, bf16[992,128]{1,0:T(8,128)(2,1)S(1)}, u32[]{:S(2)}, u32[]{:S(2)}) collective-permute-start(bf16[992,128]{1,0:T(8,128)(2,1)S(1)} %get-tuple-element.28), channel_id=1, source_target_pairs={{0,1},{2,3},{4,5},{6,7},{8,9},{10,11},{12,13},{14,15},{16,17},{18,... | collective-permute-start | bytes 761864 | tf_op jit(solution)/shard_map/ppermute | solution.py:587
  31.6 20.9 %copy-start.1 = (s32[4,128]{1,0:T(4,128)S(1)}, s32[4,128]{1,0:T(4,128)}, u32[]{:S(2)}) copy-start(s32[4,128]{1,0:T(4,128)} %bidx_hbm.1) | copy-start | bytes 6148
  39.9 26.0 %all-to-all-start.1 = ((bf16[384,4,128]{2,1,0:T(4,128)(2,1)}), bf16[384,4,128]{2,1,0:T(4,128)(2,1)S(1)}, u32[]{:S(2)}, u32[]{:S(2)}) async-start(bf16[384,4,128]{2,1,0:T(4,128)(2,1)} %bitcast.7), calls=%async_computation.1 | async-start | bytes 786432 | tf_op jit(solution)/shard_map/all_to_all | solution.py:530
  52.8 34.5 %copy-start = (bf16[2,256,384]{2,1,0:T(8,128)(2,1)S(1)}, bf16[2,256,384]{2,1,0:T(8,128)(2,1)}, u32[]{:S(2)}) copy-start(bf16[2,256,384]{2,1,0:T(8,128)(2,1)} %constant.9.clone.mix_ref) | copy-start | bytes 1179652
  67.0 20.3 %all-to-all-start.2 = ((bf16[128,8,128]{2,1,0:T(8,128)(2,1)}), bf16[128,8,128]{2,1,0:T(8,128)(2,1)S(1)}, u32[]{:S(2)}, u32[]{:S(2)}) async-start(bf16[128,8,128]{2,1,0:T(8,128)(2,1)} %bitcast.9), calls=%async_computation.2 | async-start | bytes 524288 | tf_op jit(solution)/shard_map/all_to_all | solution.py:530
  106.2 6.2 %collective-permute-start.2 = (f32[324,128]{1,0:T(8,128)S(1)}, f32[324,128]{1,0:T(8,128)S(1)}, u32[]{:S(2)}, u32[]{:S(2)}) collective-permute-start(f32[324,128]{1,0:T(8,128)S(1)} %nest.1.own_ref), channel_id=1, source_target_pairs={{0,128},{128,0},{1,129},{129,1},{2,130},{130,2},{3,131},{131,3},{4... | collective-permute-start | bytes 497672 | tf_op jit(solution)/shard_map/ppermute | solution.py:676

commit v8 on v7

--- a/solution.py
+++ b/solution.py
@@ -18,12 +18,13 @@
 LPAD = 96
 RING = 16
 BSTR = LPAD * RING
-SENT = 6
+SENT = 5
 FLAT = 2 * LEV * ROWS
-HALO_ROWS = 992
-DIST = ((0, 1), (2, 3), (4, None), (5, None))
+HALO_ROWS = 816
+DIST = ((0, 1), (2, None), (3, None), (4, None))
 SPLIT = 40
 PACK = 12
+EPACK = 6
 CUT = W - LEV
 L_TOP = 81
 L_REQ = 86
@@ -188,21 +189,26 @@
     copies[0].wait()
     lane = lax.broadcasted_iota(jnp.int32, (NT, W), 1)
     tile = lax.broadcasted_iota(jnp.int32, (NT, W), 0)
+    asked = jnp.logical_or(lane == L_REQ, lane == L_REQ + 1)
+    wanted = tile == L_REQ + jnp.bitwise_and(lane, 1)
     for s in range(STEPS):
         idx = bidx_ref[s : s + 1, :]
         owner = jnp.right_shift(idx, 10)
         row = jnp.bitwise_and(jnp.right_shift(idx, 7), ROWS - 1)
         col = jnp.bitwise_and(jnp.bitwise_and(idx, W - 1) + shift_ref[s], W - 1)
-        cell = (row * W + col + 1).astype(F32)
-        mine = tile == owner
-        picked = jnp.where(mine, jnp.broadcast_to(cell, (NT, W)), 0.0)
-        even = jnp.bitwise_and(lane, 1) == 0
-        first = jnp.sum(jnp.where(even, picked, 0.0), axis=1, keepdims=True) - 1.0
-        second = jnp.sum(jnp.where(even, 0.0, picked), axis=1, keepdims=True) - 1.0
+        mine = jnp.where(tile == owner, 1.0, 0.0).astype(BF16)
+        found = []
+        for value in (row + 1, col):
+            value = jnp.broadcast_to(value.astype(F32), (NT, W))
+            value = jnp.where(wanted, value, 0.0).astype(BF16)
+            found.append(
+                lax.dot_general(
+                    mine, value, (((1,), (1,)), ((), ())), preferred_element_type=F32
+                )
+            )
+        cell = (found[0] - 1.0) * W + found[1]
         rows = msg_ref[pl.ds(s, NT, stride=4), :]
-        rows = jnp.where(lane == L_REQ, first, rows)
-        rows = jnp.where(lane == L_REQ + 1, second, rows)
-        msg_ref[pl.ds(s, NT, stride=4), :] = rows
+        msg_ref[pl.ds(s, NT, stride=4), :] = jnp.where(asked, cell, rows)
 
 
 def ring_step(read, write, level_stride, coef, own_only=False):
@@ -374,6 +380,7 @@
     lane = lax.broadcasted_iota(jnp.int32, (2 * NT, W), 1)
     parity = jnp.bitwise_and(jnp.right_shift(lane, 5), 1)
     target = sub - parity * NT
+    found = {}
     for s in range(STEPS):
         owner = jnp.right_shift(bperm_ref[s : s + 1, :], 10)
         hot = jnp.where(target == owner, 1.0, 0.0).astype(BF16)
@@ -392,10 +399,20 @@
         )
         for b in range(2):
             for j in range(4):
-                start = (b * 64 + (s // 2) * 32) * 8 + (s % 2) * 4 + j
-                scr2_ref[pl.ds(start, 32, stride=8), :] = res[
+                found[b, s // 2, (s % 2) * 4 + j] = res[
                     j * 32 : (j + 1) * 32, b * W : (b + 1) * W
                 ]
+    lane = lax.broadcasted_iota(jnp.int32, (32, W), 1)
+    for b in range(2):
+        for half in range(2):
+            for r in range(EPACK):
+                value = found[b, half, r]
+                if r < 4:
+                    extra = found[b, half, EPACK + r // 2]
+                    turn = LEV if r % 2 == 0 else LEV - CUT
+                    value = jnp.where(lane < LEV, value, pltpu.roll(extra, turn, 1))
+                start = (b * 64 + half * 32) * EPACK + r
+                scr2_ref[pl.ds(start, 32, stride=EPACK), :] = value
     out_ref[...] = scr2_ref[...].astype(BF16)
 
 
@@ -478,11 +495,18 @@
 def owner_kernel(tile_ref, got_ref, hot_ref, base_ref, mix_ref, out_ref, scr_ref):
     late = jnp.bitwise_and(jnp.right_shift(tile_ref[0], 5), 1)
     scr_ref[...] = got_ref[...].astype(F32)
+    low = lax.broadcasted_iota(jnp.int32, (NT, W), 1) < CUT
+
+    def row(r):
+        if r < EPACK:
+            return scr_ref[pl.ds(r, NT, stride=EPACK), :]
+        first = pltpu.roll(row(2 * (r - EPACK)), W - LEV, 1)
+        second = pltpu.roll(row(2 * (r - EPACK) + 1), W - LEV + CUT, 1)
+        return jnp.where(low, first, second)
+
     moved = []
     for s in range(2):
-        edge = jnp.concatenate(
-            [scr_ref[pl.ds(s * 4 + j, NT, stride=8), :] for j in range(4)], axis=0
-        ).astype(BF16)
+        edge = jnp.concatenate([row(s * 4 + j) for j in range(4)], axis=0).astype(BF16)
         moved.append(jnp.dot(hot_ref[s], edge, preferred_element_type=F32).astype(BF16))
     total = jnp.dot(
         jnp.concatenate(moved, axis=1), mix_ref[late], preferred_element_type=F32
@@ -606,8 +630,8 @@
             pltpu.SemaphoreType.DMA((2,)),
         ],
         name="parent",
-        flops=1 << 24,
-        nbytes=4 << 20,
+        flops=1 << 33,
+        nbytes=1 << 27,
     )(tile, kept, from_gap, from_pair, in_hbm(terrain))
 
     values = call(
@@ -633,13 +657,13 @@
     bperm = boundary_index.reshape(STEPS, 32, 4).transpose(0, 2, 1).reshape(STEPS, NT)
     edges = call(
         regroup_kernel,
-        sds((8 * NT, W), BF16),
-        scratch=[pltpu.VMEM((PACK * NT, W), F32), pltpu.VMEM((8 * NT, W), F32)],
+        sds((EPACK * NT, W), BF16),
+        scratch=[pltpu.VMEM((PACK * NT, W), F32), pltpu.VMEM((EPACK * NT, W), F32)],
         name="regroup",
         flops=1 << 26,
         nbytes=1 << 20,
     )(bperm, second)
-    third = exchange(edges.reshape(NT, 8, W)).reshape(8 * NT, W)
+    third = exchange(edges.reshape(EPACK // 2 * NT, 2, W)).reshape(EPACK * NT, W)
 
     parent_out = call(
         last_parent_kernel,
@@ -659,7 +683,7 @@
         owner_kernel,
         sds((4 * NT, W), F32),
         in_specs=[SM, VM, VM, VM, VM],
-        scratch=[pltpu.VMEM((8 * NT, W), F32)],
+        scratch=[pltpu.VMEM((EPACK * NT, W), F32)],
         name="owner",
         flops=1 << 29,
         nbytes=3 << 20,

time: 113 us -> 106 us (0.938)
  starting transfers between devices: 46.2 us -> 41.6 us
  waiting for transfers between devices: 27.5 us -> 24.4 us
    ppermute x1, waiting for transfers between devices: 7.64 us -> 0.01 us  [on_device(): from_pair = lax.ppermute(down, 'tile', pairs)]
    all_to_all x3, starting transfers between devices: 37.3 us -> 30.8 us  [exchange(): return lax.all_to_all(x, 'tile', split_axis=0, concat_axis=0, tiled=True)]
    all_to_all x3, waiting for transfers between devices: 19.5 us -> 24.2 us  [exchange(): return lax.all_to_all(x, 'tile', split_axis=0, concat_axis=0, tiled=True)]
    ppermute x1, starting transfers between devices: 3.07 us -> 4.74 us  [on_device(): from_pair = lax.ppermute(down, 'tile', pairs)]
where the time goes in v8:
time: 106 us; the launch traced here: 105 us
  starting transfers between devices  41.6 us (39%)
  waiting for transfers between devices  24.4 us (23%)
  Pallas kernels  19.5 us (18%)
  blocking collectives  17.7 us (17%)
    all_to_all x3, starting transfers between devices, exchange(): return lax.all_to_all(x, 'tile', split_axis=0, concat_axis=0, tiled=True)  30.8 us
    all_to_all x3, waiting for transfers between devices, exchange(): return lax.all_to_all(x, 'tile', split_axis=0, concat_axis=0, tiled=True)  24.2 us
    all_to_all x1, blocking collectives, exchange(): return lax.all_to_all(x, 'tile', split_axis=0, concat_axis=0, tiled=True)  17.7 us
    pallas_call x1, Pallas kernels, on_device(): call(parent_kernel, (pltpu.VMEM((STEPS, 2 * W, ROWS * W), BF16), pltpu.HB...  6.61 us
    ppermute x1, starting transfers between devices, on_device(): other = lax.ppermute(nest_out, 'member', [(0, 1), (1, 0)])  5.4 us
    ppermute x1, starting transfers between devices, on_device(): from_pair = lax.ppermute(down, 'tile', pairs)  4.74 us
    pallas_call x1, Pallas kernels, on_device(): call(last_parent_kernel, sds((2 * LEV, ROWS, W), F32), in_specs=[HB, HB],...  3.26 us
    pallas_call x1, Pallas kernels, on_device(): call(plan_kernel, (sds((2, 4 * NT, 4 * NT), BF16), sds((4 * NT, W), F32))...  2.18 us
  transfers between devices with their start and end apart: 6, of which 4 were waited for; matrix products, arithmetic and copies ran while one was open for 1% of the time, Pallas kernels for 11%

profile of v8, /device:TPU:1, one launch (start us, length us, event | category | flops | bytes accessed | tf_op | source)
XLA Modules:
  0.0 105.1 jit_solution(14344250014312778377)
XLA Ops:
  0.6 1.4 %halo.1 = (f32[1296,128]{1,0:T(8,128)S(1)}, bf16[816,128]{1,0:T(8,128)(2,1)S(1)}, bf16[816,128]{1,0:T(8,128)(2,1)S(1)}, f32[81,2,2,128]{3,2,1,0:T(2,128)S(1)}, s...) custom-call(s32[1]{0:T(128)} %bitcast.1.tile_ref, f32[1296,128]{1,0:T(8,128)} %bitcast.24, ...), custom_call_target="tpu_custom_call" | custom-call | bytes 1048576 | tf_op jit(solution)/shard_map/halo/pallas_call | solution.py:565
  2.1 0.7 collective-permute-start
  2.7 4.7 %collective-permute-start.1 = (bf16[816,128]{1,0:T(8,128)(2,1)S(1)}, bf16[816,128]{1,0:T(8,128)(2,1)S(1)}, u32[]{:S(2)}, u32[]{:S(2)}) collective-permute-start(bf16[816,128]{1,0:T(8,128)(2,1)S(1)} %get-tuple-element.28), channel_id=1, source_target_pairs={{0,1},{2,3},{4,5},{6,7},{8,9},{10,11},{12,13},{14,15},{16,17},{18,... | collective-permute-start | bytes 626696 | tf_op jit(solution)/shard_map/ppermute | solution.py:611
  7.5 1.8 %send.1 = f32[512,128]{1,0:T(8,128)} custom-call(s32[4]{0:T(128)} %shift_hbm.1, f32[81,2,2,128]{3,2,1,0:T(2,128)S(1)} %get-tuple-element.22.nest_ref, s32[4,128]{1,0:T(4,128)S(1)} %get-tuple-element.23.bidx_ref, s32[4,256]{1,0:T(4,128)S(1)} %get-tuple-element.24.dest_ref, f32[256,256]{1,0:T(8,128)S(1)} %get-tuple-element.25.mix_ref), custom_call_target="tpu_custom_call" | custom-call | bytes 67108864 | tf_op jit(solution)/shard_map/send/pallas_call | solution.py:595
  9.3 14.3 %all-to-all-start = ((f32[128,4,128]{2,1,0:T(4,128)}), f32[128,4,128]{2,1,0:T(4,128)S(1)}, u32[]{:S(2)}, u32[]{:S(2)}) async-start(f32[128,4,128]{2,1,0:T(4,128)} %bitcast.5), calls=%async_computation | async-start | bytes 524288 | tf_op jit(solution)/shard_map/all_to_all | solution.py:554
  23.6 0.0 collective-permute-done.second_ref
  23.6 0.0 collective-permute-done.1.first_ref
  23.6 6.6 %parent.1 = (bf16[4,256,1024]{2,1,0:T(8,128)(2,1)S(1)}, f32[3072,128]{1,0:T(8,128)}) custom-call(s32[1]{0:T(128)} %bitcast.1.tile_ref, f32[1296,128]{1,0:T(8,128)S(1)} %get-tuple-element.26.parent_ref, bf16[816,128]{1,0:T(8,128)(2,1)S(1)} %collective-permute-done.second_ref, bf16[816,128]{1,0:T(8,128)(2,1)S(1)} %collective-permute-done.1.first_ref, ...), custom_call_target="tpu_custom_call" | custom-call | flops 8589934592 | bytes 134217728 | tf_op jit(solution)/shard_map/parent/pallas_call | solution.py:613
  30.2 0.0 copy-start.1
  30.2 5.3 %all-to-all-done = f32[128,4,128]{2,1,0:T(4,128)S(1)} async-done(((f32[128,4,128]{2,1,0:T(4,128)}), f32[128,4,128]{2,1,0:T(4,128)S(1)}, u32[]{:S(2)}, u32[]{:S(2)}) %all-to-all-start) | async-done | bytes 262176 | tf_op jit(solution)/shard_map/all_to_all | solution.py:554
  35.5 1.7 %gather.1 = bf16[1536,128]{1,0:T(8,128)(2,1)} custom-call(f32[512,128]{1,0:T(8,128)S(1)} %bitcast.21, bf16[4,256,1024]{2,1,0:T(8,128)(2,1)S(1)} %get-tuple-element.29.cells_ref), custom_call_target="tpu_custom_call" | custom-call | flops 536870912 | bytes 3145728 | tf_op jit(solution)/shard_map/gather/pallas_call | solution.py:637
  37.2 8.0 %all-to-all-start.1 = ((bf16[384,4,128]{2,1,0:T(4,128)(2,1)}), bf16[384,4,128]{2,1,0:T(4,128)(2,1)S(1)}, u32[]{:S(2)}, u32[]{:S(2)}) async-start(bf16[384,4,128]{2,1,0:T(4,128)(2,1)} %bitcast.7), calls=%async_computation.1 | async-start | bytes 786432 | tf_op jit(solution)/shard_map/all_to_all | solution.py:554
  45.2 0.0 copy-done.1
  45.2 0.1 reshape.56
  45.3 0.1 copy.14
  45.4 0.1 reshape.57.bperm_ref
  45.5 0.0 copy-start
  45.5 2.2 %plan.1 = (bf16[2,512,512]{2,1,0:T(8,128)(2,1)S(1)}, f32[512,128]{1,0:T(8,128)S(1)}) custom-call(s32[1]{0:T(128)} %bitcast.1.tile_ref, f32[512,128]{1,0:T(8,128)S(1)} %bitcast.22), custom_call_target="tpu_custom_call" | custom-call | flops 268435456 | bytes 3145728 | tf_op jit(solution)/shard_map/plan/pallas_call | solution.py:647
  47.7 10.8 %all-to-all-done.1 = bf16[384,4,128]{2,1,0:T(4,128)(2,1)S(1)} async-done(((bf16[384,4,128]{2,1,0:T(4,128)(2,1)}), bf16[384,4,128]{2,1,0:T(4,128)(2,1)S(1)}, u32[]{:S(2)}, u32[]{:S(2)}) %all-to-all-start.1) | async-done | bytes 393248 | tf_op jit(solution)/shard_map/all_to_all | solution.py:554
  58.4 1.2 %regroup.1 = bf16[768,128]{1,0:T(8,128)(2,1)} custom-call(s32[4,128]{1,0:T(4,128)S(1)} %reshape.57.bperm_ref, bf16[1536,128]{1,0:T(8,128)(2,1)S(1)} %bitcast.18), custom_call_target="tpu_custom_call" | custom-call | flops 67108864 | bytes 1048576 | tf_op jit(solution)/shard_map/regroup/pallas_call | solution.py:658
  59.6 8.5 %all-to-all-start.2 = ((bf16[384,2,128]{2,1,0:T(2,128)(2,1)}), bf16[384,2,128]{2,1,0:T(2,128)(2,1)S(1)}, u32[]{:S(2)}, u32[]{:S(2)}) async-start(bf16[384,2,128]{2,1,0:T(2,128)(2,1)} %bitcast.9), calls=%async_computation.2 | async-start | bytes 393216 | tf_op jit(solution)/shard_map/all_to_all | solution.py:554
  68.1 3.3 %last_parent.1 = f32[162,8,128]{2,1,0:T(8,128)} custom-call(f32[3072,128]{1,0:T(8,128)} %get-tuple-element.33.ring_hbm, s32[8,128]{1,0:T(8,128)} %terrain_hbm.5), custom_call_target="tpu_custom_call" | custom-call | flops 4194304 | bytes 2097152 | tf_op jit(solution)/shard_map/last_parent/pallas_call | solution.py:668
  71.3 8.1 %all-to-all-done.2 = bf16[384,2,128]{2,1,0:T(2,128)(2,1)S(1)} async-done(((bf16[384,2,128]{2,1,0:T(2,128)(2,1)}), bf16[384,2,128]{2,1,0:T(2,128)(2,1)S(1)}, u32[]{:S(2)}, u32[]{:S(2)}) %all-to-all-start.2) | async-done | bytes 196640 | tf_op jit(solution)/shard_map/all_to_all | solution.py:554
  79.5 0.0 copy-done
  79.5 0.6 owner.1
  80.1 17.7 %all_to_all.20 = f32[128,4,128]{2,1,0:T(4,128)S(1)} all-to-all(f32[128,4,128]{2,1,0:T(4,128)S(1)} %bitcast.19), channel_id=1, replica_groups=mesh['member'=2,'tile'=128] {'tile'}, dimensions={0} | all-to-all | bytes 524288 | tf_op jit(solution)/shard_map/all_to_all | solution.py:554
  97.8 0.2 nest.1.own_ref
  98.0 5.4 %collective-permute-start.2 = (f32[324,128]{1,0:T(8,128)S(1)}, f32[324,128]{1,0:T(8,128)S(1)}, u32[]{:S(2)}, u32[]{:S(2)}) collective-permute-start(f32[324,128]{1,0:T(8,128)S(1)} %nest.1.own_ref), channel_id=1, source_target_pairs={{0,128},{128,0},{1,129},{129,1},{2,130},{130,2},{3,131},{131,3},{4... | collective-permute-start | bytes 497672 | tf_op jit(solution)/shard_map/ppermute | solution.py:700
  103.4 0.8 reshape.70
  104.1 0.3 collective-permute-done.2.other_ref
  104.4 0.7 stats.1
Async XLA Ops:
  2.1 21.5 %collective-permute-start = (bf16[816,128]{1,0:T(8,128)(2,1)S(1)}, bf16[816,128]{1,0:T(8,128)(2,1)S(1)}, u32[]{:S(2)}, u32[]{:S(2)}) collective-permute-start(bf16[816,128]{1,0:T(8,128)(2,1)S(1)} %get-tuple-element.27), channel_id=1, source_target_pairs={{1,2},{3,4},{5,6},{7,8},{9,10},{11,12},{13,14},{15,16},{17,18},{19... | collective-permute-start | bytes 626696 | tf_op jit(solution)/shard_map/ppermute | solution.py:610
  2.7 20.9 %collective-permute-start.1 = (bf16[816,128]{1,0:T(8,128)(2,1)S(1)}, bf16[816,128]{1,0:T(8,128)(2,1)S(1)}, u32[]{:S(2)}, u32[]{:S(2)}) collective-permute-start(bf16[816,128]{1,0:T(8,128)(2,1)S(1)} %get-tuple-element.28), channel_id=1, source_target_pairs={{0,1},{2,3},{4,5},{6,7},{8,9},{10,11},{12,13},{14,15},{16,17},{18,... | collective-permute-start | bytes 626696 | tf_op jit(solution)/shard_map/ppermute | solution.py:611
  9.3 26.3 %all-to-all-start = ((f32[128,4,128]{2,1,0:T(4,128)}), f32[128,4,128]{2,1,0:T(4,128)S(1)}, u32[]{:S(2)}, u32[]{:S(2)}) async-start(f32[128,4,128]{2,1,0:T(4,128)} %bitcast.5), calls=%async_computation | async-start | bytes 524288 | tf_op jit(solution)/shard_map/all_to_all | solution.py:554
  30.2 14.9 %copy-start.1 = (s32[4,128]{1,0:T(4,128)S(1)}, s32[4,128]{1,0:T(4,128)}, u32[]{:S(2)}) copy-start(s32[4,128]{1,0:T(4,128)} %bidx_hbm.1) | copy-start | bytes 6148
  37.2 21.3 %all-to-all-start.1 = ((bf16[384,4,128]{2,1,0:T(4,128)(2,1)}), bf16[384,4,128]{2,1,0:T(4,128)(2,1)S(1)}, u32[]{:S(2)}, u32[]{:S(2)}) async-start(bf16[384,4,128]{2,1,0:T(4,128)(2,1)} %bitcast.7), calls=%async_computation.1 | async-start | bytes 786432 | tf_op jit(solution)/shard_map/all_to_all | solution.py:554
  45.5 34.0 %copy-start = (bf16[2,256,384]{2,1,0:T(8,128)(2,1)S(1)}, bf16[2,256,384]{2,1,0:T(8,128)(2,1)}, u32[]{:S(2)}) copy-start(bf16[2,256,384]{2,1,0:T(8,128)(2,1)} %constant.9.clone.mix_ref) | copy-start | bytes 1179652
  59.6 19.8 %all-to-all-start.2 = ((bf16[384,2,128]{2,1,0:T(2,128)(2,1)}), bf16[384,2,128]{2,1,0:T(2,128)(2,1)S(1)}, u32[]{:S(2)}, u32[]{:S(2)}) async-start(bf16[384,2,128]{2,1,0:T(2,128)(2,1)} %bitcast.9), calls=%async_computation.2 | async-start | bytes 393216 | tf_op jit(solution)/shard_map/all_to_all | solution.py:554
  98.0 6.4 %collective-permute-start.2 = (f32[324,128]{1,0:T(8,128)S(1)}, f32[324,128]{1,0:T(8,128)S(1)}, u32[]{:S(2)}, u32[]{:S(2)}) collective-permute-start(f32[324,128]{1,0:T(8,128)S(1)} %nest.1.own_ref), channel_id=1, source_target_pairs={{0,128},{128,0},{1,129},{129,1},{2,130},{130,2},{3,131},{131,3},{4... | collective-permute-start | bytes 497672 | tf_op jit(solution)/shard_map/ppermute | solution.py:700

commit v9 on v8

--- a/solution.py
+++ b/solution.py
@@ -18,10 +18,10 @@
 LPAD = 96
 RING = 16
 BSTR = LPAD * RING
-SENT = 5
+SENT = 6
 FLAT = 2 * LEV * ROWS
-HALO_ROWS = 816
-DIST = ((0, 1), (2, None), (3, None), (4, None))
+HALO_ROWS = 992
+DIST = ((0, 1), (2, 3), (4, None), (5, None))
 SPLIT = 40
 PACK = 12
 EPACK = 6
@@ -78,7 +78,8 @@
         for owner in range(2):
             for k in range(STEPS):
                 send[part, LEV + k, owner, L_DEST[owner] + part * STEPS + k] = 1.0
-    send = send.reshape(2 * W, 2 * W).astype(np.float32)
+    coarse, fine, _ = split3(send.reshape(2 * W, 2 * W))
+    send = np.concatenate([coarse, coarse, fine])
     mix = [
         padded_transpose(power[STEPS - k] * RELAX * keep ** (STEPS - 1 - k))
         for k in range(STEPS)
@@ -132,10 +133,14 @@
         [
             (parent_hbm, parent_ref),
             (terrain_hbm, terrain_ref),
-            (nest_hbm, nest_ref),
             (bidx_hbm, bidx_ref),
             (dest_hbm, dest_ref),
             (mix_hbm, mix_ref),
+        ]
+        + [
+            (nest_hbm.at[:, part, b, :], nest_ref.at[b * 2 + part])
+            for b in range(2)
+            for part in range(2)
         ],
         sems,
     )
@@ -172,15 +177,17 @@
         for part in range(2):
             top = part * W
             pad_ref[b, top + LEV - 1 : top + W, :] = zeros
-            pad_ref[b, top : top + LEV, :] = nest_ref[:, part, b, :]
+            pad_ref[b, top : top + LEV, :] = nest_ref[b * 2 + part]
             pad_ref[b, top + LEV : top + LEV + STEPS, :] = dest_ref[
                 :, part * W : (part + 1) * W
             ].astype(F32)
+        value = pad_ref[b]
+        coarse = value.astype(BF16)
+        fine = (value - coarse.astype(F32)).astype(BF16)
         res = lax.dot_general(
-            pad_ref[b],
+            jnp.concatenate([coarse, fine, coarse], axis=0),
             mix_ref[...],
             (((0,), (0,)), ((), ())),
-            precision=lax.Precision.HIGHEST,
             preferred_element_type=F32,
         )
         for owner in range(2):
@@ -523,27 +530,34 @@
         sum_ref[...] = (early + late).T
         early_ref[...] = early.T
         late_ref[...] = late.T
-        out_ref[pl.ds(b, LEV, stride=4), :] = sum_ref[:LEV, :]
-        inner = 2 + b
-        out_ref[pl.ds(inner, SPLIT, stride=4), :] = early_ref[L_INNER:, :]
-        out_ref[pl.ds(inner + 4 * SPLIT, SPLIT, stride=4), :] = late_ref[L_INNER:, :]
-        top = inner + 8 * SPLIT
-        out_ref[top : top + 1, :] = late_ref[L_TOP : L_TOP + 1, :]
-
-
-def stats_kernel(own_ref, other_ref, mean_ref, var_ref):
-    for half in range(2):
+        out_ref[2 * b] = sum_ref[:LEV, :]
+        inner = 2 * b + 1
+        out_ref[inner, :SPLIT, :] = early_ref[L_INNER:, :]
+        out_ref[inner, SPLIT : 2 * SPLIT, :] = late_ref[L_INNER:, :]
+        out_ref[inner, 2 * SPLIT :, :] = late_ref[L_TOP : L_TOP + 1, :]
+
+
+def stats_kernel(own_ref, other_ref, mean_ref, var_ref, nest_hbm, sems):
+    copies = start_all(
+        [
+            (own_ref.at[2 * b + part], nest_hbm.at[:, part, b, :])
+            for b in range(2)
+            for part in range(2)
+        ],
+        sems,
+    )
+    for part in range(2):
         a0, a1, b0, b1 = (
-            ref[pl.ds(half * 2 + b, LEV, stride=4), :]
-            for ref in (own_ref, other_ref)
-            for b in range(2)
+            ref[2 * b + part] for ref in (own_ref, other_ref) for b in range(2)
         )
-        lanes = slice(half * W, (half + 1) * W)
+        lanes = slice(part * W, (part + 1) * W)
         mean = ((a0 + a1) + (b0 + b1)) / 4.0
         mean_ref[:, lanes] = mean
         own = (a0 - mean) * (a0 - mean) + (a1 - mean) * (a1 - mean)
         other = (b0 - mean) * (b0 - mean) + (b1 - mean) * (b1 - mean)
         var_ref[:, lanes] = (own + other) / 4.0
+    for copy in copies:
+        copy.wait()
 
 
 def in_hbm(x):
@@ -568,10 +582,10 @@
             pltpu.VMEM((FLAT, W), F32),
             sds((HALO_ROWS, W), BF16),
             sds((HALO_ROWS, W), BF16),
-            pltpu.VMEM((LEV, 2, 2, W), F32),
+            pltpu.VMEM((4, LEV, W), F32),
             pltpu.VMEM((STEPS, NT), jnp.int32),
             pltpu.VMEM((STEPS, 2 * W), jnp.int32),
-            pltpu.VMEM((2 * W, 2 * W), F32),
+            pltpu.VMEM((6 * W, 2 * W), BF16),
         ),
         in_specs=[SM, HB, HB, HB, HB, HB, HB],
         scratch=[
@@ -579,7 +593,7 @@
             pltpu.VMEM((HALO_ROWS, W), F32),
             pltpu.VMEM((HALO_ROWS, W), F32),
             pltpu.VMEM((ROWS, W), F32),
-            pltpu.SemaphoreType.DMA((6,)),
+            pltpu.SemaphoreType.DMA((9,)),
         ],
         name="halo",
         nbytes=1 << 20,
@@ -690,21 +704,28 @@
     )(tile, third, hot, base, e_mix)
     fourth = exchange(columns.reshape(NT, 4, W)).reshape(4 * NT, W)
 
-    nest_out = call(
+    own = call(
         nest_kernel,
-        sds((4 * LEV, W), F32),
+        pltpu.VMEM((4, LEV, W), F32),
         scratch=[pltpu.VMEM((W, W), F32)] * 3,
         name="nest",
         nbytes=1 << 19,
     )(fourth)
-    other = lax.ppermute(nest_out, "member", [(0, 1), (1, 0)])
-    mean, variance = call(
+    other = lax.ppermute(own, "member", [(0, 1), (1, 0)])
+    mean, variance, nest_out = call(
         stats_kernel,
-        (sds((LEV, 2 * W), F32), sds((LEV, 2 * W), F32)),
+        (
+            sds((LEV, 2 * W), F32),
+            sds((LEV, 2 * W), F32),
+            pltpu.HBM((LEV, 2, 2, W), F32),
+        ),
+        in_specs=[VM, VM],
+        out_specs=(VM, VM, HB),
+        scratch=[pltpu.SemaphoreType.DMA((4,))],
         name="stats",
         nbytes=1 << 19,
-    )(nest_out, other)
-    nest_out = nest_out.reshape(LEV, 2, 2, W).transpose(2, 0, 1, 3)
+    )(own, other)
+    nest_out = nest_out.transpose(2, 0, 1, 3)
     nest_out = nest_out.reshape(nest_state.shape)
     return (parent_out.reshape(parent_state.shape), nest_out, mean, variance)
 

time: 106 us -> 106 us (level)
  transfers between devices with their start and end apart: 6 -> 6, of which waited for: 4 -> 4; matrix products, arithmetic and copies ran while one was open for 1% -> 0% of each run, Pallas kernels for 11% -> 11%
where the time goes in v9:
time: 106 us
  starting transfers between devices  41.6 us (39%)
  waiting for transfers between devices  25.2 us (24%)
  Pallas kernels  20.3 us (19%)
  blocking collectives  17.7 us (17%)
    all_to_all x3, starting transfers between devices, exchange(): return lax.all_to_all(x, 'tile', split_axis=0, concat_axis=0, tiled=True)  30.8 us
    all_to_all x3, waiting for transfers between devices, exchange(): return lax.all_to_all(x, 'tile', split_axis=0, concat_axis=0, tiled=True)  24.2 us
    all_to_all x1, blocking collectives, exchange(): return lax.all_to_all(x, 'tile', split_axis=0, concat_axis=0, tiled=True)  17.7 us
    pallas_call x1, Pallas kernels, on_device(): call(parent_kernel, (pltpu.VMEM((STEPS, 2 * W, ROWS * W), BF16), pltpu.HB...  6.62 us
    ppermute x1, starting transfers between devices, on_device(): other = lax.ppermute(own, 'member', [(0, 1), (1, 0)])  5.4 us
    ppermute x1, starting transfers between devices, on_device(): from_pair = lax.ppermute(down, 'tile', pairs)  4.74 us
    pallas_call x1, Pallas kernels, on_device(): call(last_parent_kernel, sds((2 * LEV, ROWS, W), F32), in_specs=[HB, HB],...  3.26 us
    pallas_call x1, Pallas kernels, on_device(): call(plan_kernel, (sds((2, 4 * NT, 4 * NT), BF16), sds((4 * NT, W), F32))...  2.18 us
  transfers between devices with their start and end apart: 6, of which 4 were waited for; matrix products, arithmetic and copies ran while one was open for 0% of the time, Pallas kernels for 11%

profile of v9, /device:TPU:1, one launch (start us, length us, event | category | flops | bytes accessed | tf_op | source)
XLA Modules:
  0.0 106.0 jit_solution(8088968497703560245)
XLA Ops:
  0.6 1.5 %halo.1 = (f32[1296,128]{1,0:T(8,128)S(1)}, bf16[992,128]{1,0:T(8,128)(2,1)S(1)}, bf16[992,128]{1,0:T(8,128)(2,1)S(1)}, f32[4,81,128]{2,1,0:T(8,128)S(1)}, s32[4...) custom-call(s32[1]{0:T(128)} %bitcast.1.tile_ref, f32[1296,128]{1,0:T(8,128)} %bitcast.24, ...), custom_call_target="tpu_custom_call" | custom-call | bytes 1048576 | tf_op jit(solution)/shard_map/halo/pallas_call | solution.py:579
  2.1 0.7 collective-permute-start
  2.8 4.7 %collective-permute-start.1 = (bf16[992,128]{1,0:T(8,128)(2,1)S(1)}, bf16[992,128]{1,0:T(8,128)(2,1)S(1)}, u32[]{:S(2)}, u32[]{:S(2)}) collective-permute-start(bf16[992,128]{1,0:T(8,128)(2,1)S(1)} %get-tuple-element.29), channel_id=1, source_target_pairs={{0,1},{2,3},{4,5},{6,7},{8,9},{10,11},{12,13},{14,15},{16,17},{18,... | collective-permute-start | bytes 761864 | tf_op jit(solution)/shard_map/ppermute | solution.py:625
  7.6 1.8 %send.1 = f32[512,128]{1,0:T(8,128)} custom-call(s32[4]{0:T(128)} %shift_hbm.1, f32[4,81,128]{2,1,0:T(8,128)S(1)} %get-tuple-element.23.nest_ref, s32[4,128]{1,0:T(4,128)S(1)} %get-tuple-element.24.bidx_ref, s32[4,256]{1,0:T(4,128)S(1)} %get-tuple-element.25.dest_ref, bf16[768,256]{1,0:T(8,128)(2,1)S(1)} %get-tuple-element.26.mix_ref), custom_call_target="tpu_custom_call" | custom-call | bytes 67108864 | tf_op jit(solution)/shard_map/send/pallas_call | solution.py:609
  9.4 14.3 %all-to-all-start = ((f32[128,4,128]{2,1,0:T(4,128)}), f32[128,4,128]{2,1,0:T(4,128)S(1)}, u32[]{:S(2)}, u32[]{:S(2)}) async-start(f32[128,4,128]{2,1,0:T(4,128)} %bitcast.5), calls=%async_computation | async-start | bytes 524288 | tf_op jit(solution)/shard_map/all_to_all | solution.py:568
  23.7 0.0 collective-permute-done.second_ref
  23.7 0.0 collective-permute-done.1.first_ref
  23.7 6.6 %parent.1 = (bf16[4,256,1024]{2,1,0:T(8,128)(2,1)S(1)}, f32[3072,128]{1,0:T(8,128)}) custom-call(s32[1]{0:T(128)} %bitcast.1.tile_ref, f32[1296,128]{1,0:T(8,128)S(1)} %get-tuple-element.27.parent_ref, bf16[992,128]{1,0:T(8,128)(2,1)S(1)} %collective-permute-done.second_ref, bf16[992,128]{1,0:T(8,128)(2,1)S(1)} %collective-permute-done.1.first_ref, ...), custom_call_target="tpu_custom_call" | custom-call | flops 8589934592 | bytes 134217728 | tf_op jit(solution)/shard_map/parent/pallas_call | solution.py:627
  30.3 0.0 copy-start.1
  30.4 5.3 %all-to-all-done = f32[128,4,128]{2,1,0:T(4,128)S(1)} async-done(((f32[128,4,128]{2,1,0:T(4,128)}), f32[128,4,128]{2,1,0:T(4,128)S(1)}, u32[]{:S(2)}, u32[]{:S(2)}) %all-to-all-start) | async-done | bytes 262176 | tf_op jit(solution)/shard_map/all_to_all | solution.py:568
  35.6 1.7 %gather.1 = bf16[1536,128]{1,0:T(8,128)(2,1)} custom-call(f32[512,128]{1,0:T(8,128)S(1)} %bitcast.21, bf16[4,256,1024]{2,1,0:T(8,128)(2,1)S(1)} %get-tuple-element.30.cells_ref), custom_call_target="tpu_custom_call" | custom-call | flops 536870912 | bytes 3145728 | tf_op jit(solution)/shard_map/gather/pallas_call | solution.py:651
  37.3 8.0 %all-to-all-start.1 = ((bf16[384,4,128]{2,1,0:T(4,128)(2,1)}), bf16[384,4,128]{2,1,0:T(4,128)(2,1)S(1)}, u32[]{:S(2)}, u32[]{:S(2)}) async-start(bf16[384,4,128]{2,1,0:T(4,128)(2,1)} %bitcast.7), calls=%async_computation.1 | async-start | bytes 786432 | tf_op jit(solution)/shard_map/all_to_all | solution.py:568
  45.3 0.0 copy-done.1
  45.3 0.1 reshape.53
  45.4 0.1 copy.13
  45.5 0.1 reshape.54.bperm_ref
  45.6 0.0 copy-start
  45.6 2.2 %plan.1 = (bf16[2,512,512]{2,1,0:T(8,128)(2,1)S(1)}, f32[512,128]{1,0:T(8,128)S(1)}) custom-call(s32[1]{0:T(128)} %bitcast.1.tile_ref, f32[512,128]{1,0:T(8,128)S(1)} %bitcast.22), custom_call_target="tpu_custom_call" | custom-call | flops 268435456 | bytes 3145728 | tf_op jit(solution)/shard_map/plan/pallas_call | solution.py:661
  47.8 10.8 %all-to-all-done.1 = bf16[384,4,128]{2,1,0:T(4,128)(2,1)S(1)} async-done(((bf16[384,4,128]{2,1,0:T(4,128)(2,1)}), bf16[384,4,128]{2,1,0:T(4,128)(2,1)S(1)}, u32[]{:S(2)}, u32[]{:S(2)}) %all-to-all-start.1) | async-done | bytes 393248 | tf_op jit(solution)/shard_map/all_to_all | solution.py:568
  58.6 1.2 %regroup.1 = bf16[768,128]{1,0:T(8,128)(2,1)} custom-call(s32[4,128]{1,0:T(4,128)S(1)} %reshape.54.bperm_ref, bf16[1536,128]{1,0:T(8,128)(2,1)S(1)} %bitcast.18), custom_call_target="tpu_custom_call" | custom-call | flops 67108864 | bytes 1048576 | tf_op jit(solution)/shard_map/regroup/pallas_call | solution.py:672
  59.7 8.5 %all-to-all-start.2 = ((bf16[384,2,128]{2,1,0:T(2,128)(2,1)}), bf16[384,2,128]{2,1,0:T(2,128)(2,1)S(1)}, u32[]{:S(2)}, u32[]{:S(2)}) async-start(bf16[384,2,128]{2,1,0:T(2,128)(2,1)} %bitcast.9), calls=%async_computation.2 | async-start | bytes 393216 | tf_op jit(solution)/shard_map/all_to_all | solution.py:568
  68.2 3.3 %last_parent.1 = f32[162,8,128]{2,1,0:T(8,128)} custom-call(f32[3072,128]{1,0:T(8,128)} %get-tuple-element.34.ring_hbm, s32[8,128]{1,0:T(8,128)} %terrain_hbm.5), custom_call_target="tpu_custom_call" | custom-call | flops 4194304 | bytes 2097152 | tf_op jit(solution)/shard_map/last_parent/pallas_call | solution.py:682
  71.5 8.1 %all-to-all-done.2 = bf16[384,2,128]{2,1,0:T(2,128)(2,1)S(1)} async-done(((bf16[384,2,128]{2,1,0:T(2,128)(2,1)}), bf16[384,2,128]{2,1,0:T(2,128)(2,1)S(1)}, u32[]{:S(2)}, u32[]{:S(2)}) %all-to-all-start.2) | async-done | bytes 196640 | tf_op jit(solution)/shard_map/all_to_all | solution.py:568
  79.6 0.0 copy-done
  79.6 0.6 owner.1
  80.2 17.7 %all_to_all.20 = f32[128,4,128]{2,1,0:T(4,128)S(1)} all-to-all(f32[128,4,128]{2,1,0:T(4,128)S(1)} %bitcast.19), channel_id=1, replica_groups=mesh['member'=2,'tile'=128] {'tile'}, dimensions={0} | all-to-all | bytes 524288 | tf_op jit(solution)/shard_map/all_to_all | solution.py:568
  97.9 0.2 nest.1.own_ref
  98.1 5.4 %collective-permute-start.2 = (f32[4,81,128]{2,1,0:T(8,128)S(1)}, f32[4,81,128]{2,1,0:T(8,128)S(1)}, u32[]{:S(2)}, u32[]{:S(2)}) collective-permute-start(f32[4,81,128]{2,1,0:T(8,128)S(1)} %nest.1.own_ref), channel_id=1, source_target_pairs={{0,128},{128,0},{1,129},{129,1},{2,130},{130,2},{3,131},{131,3},{4... | collective-permute-start | bytes 497672 | tf_op jit(solution)/shard_map/ppermute | solution.py:714
  103.5 1.0 collective-permute-done.2.other_ref
  104.5 1.4 %stats.1 = (f32[81,256]{1,0:T(8,128)}, f32[81,256]{1,0:T(8,128)}, f32[81,2,2,128]{3,2,1,0:T(2,128)}) custom-call(f32[4,81,128]{2,1,0:T(8,128)S(1)} %nest.1.own_ref, f32[4,81,128]{2,1,0:T(8,128)S(1)} %collective-permute-done.2.other_ref), custom_call_target="tpu_custom_call" | custom-call | bytes 524288 | tf_op jit(solution)/shard_map/stats/pallas_call | solution.py:715
Async XLA Ops:
  2.1 21.6 %collective-permute-start = (bf16[992,128]{1,0:T(8,128)(2,1)S(1)}, bf16[992,128]{1,0:T(8,128)(2,1)S(1)}, u32[]{:S(2)}, u32[]{:S(2)}) collective-permute-start(bf16[992,128]{1,0:T(8,128)(2,1)S(1)} %get-tuple-element.28), channel_id=1, source_target_pairs={{1,2},{3,4},{5,6},{7,8},{9,10},{11,12},{13,14},{15,16},{17,18},{19... | collective-permute-start | bytes 761864 | tf_op jit(solution)/shard_map/ppermute | solution.py:624
  2.8 20.9 %collective-permute-start.1 = (bf16[992,128]{1,0:T(8,128)(2,1)S(1)}, bf16[992,128]{1,0:T(8,128)(2,1)S(1)}, u32[]{:S(2)}, u32[]{:S(2)}) collective-permute-start(bf16[992,128]{1,0:T(8,128)(2,1)S(1)} %get-tuple-element.29), channel_id=1, source_target_pairs={{0,1},{2,3},{4,5},{6,7},{8,9},{10,11},{12,13},{14,15},{16,17},{18,... | collective-permute-start | bytes 761864 | tf_op jit(solution)/shard_map/ppermute | solution.py:625
  9.4 26.3 %all-to-all-start = ((f32[128,4,128]{2,1,0:T(4,128)}), f32[128,4,128]{2,1,0:T(4,128)S(1)}, u32[]{:S(2)}, u32[]{:S(2)}) async-start(f32[128,4,128]{2,1,0:T(4,128)} %bitcast.5), calls=%async_computation | async-start | bytes 524288 | tf_op jit(solution)/shard_map/all_to_all | solution.py:568
  30.3 14.9 %copy-start.1 = (s32[4,128]{1,0:T(4,128)S(1)}, s32[4,128]{1,0:T(4,128)}, u32[]{:S(2)}) copy-start(s32[4,128]{1,0:T(4,128)} %bidx_hbm.1) | copy-start | bytes 6148
  37.3 21.3 %all-to-all-start.1 = ((bf16[384,4,128]{2,1,0:T(4,128)(2,1)}), bf16[384,4,128]{2,1,0:T(4,128)(2,1)S(1)}, u32[]{:S(2)}, u32[]{:S(2)}) async-start(bf16[384,4,128]{2,1,0:T(4,128)(2,1)} %bitcast.7), calls=%async_computation.1 | async-start | bytes 786432 | tf_op jit(solution)/shard_map/all_to_all | solution.py:568
  45.6 34.0 %copy-start = (bf16[2,256,384]{2,1,0:T(8,128)(2,1)S(1)}, bf16[2,256,384]{2,1,0:T(8,128)(2,1)}, u32[]{:S(2)}) copy-start(bf16[2,256,384]{2,1,0:T(8,128)(2,1)} %constant.9.clone.mix_ref) | copy-start | bytes 1179652
  59.7 19.8 %all-to-all-start.2 = ((bf16[384,2,128]{2,1,0:T(2,128)(2,1)}), bf16[384,2,128]{2,1,0:T(2,128)(2,1)S(1)}, u32[]{:S(2)}, u32[]{:S(2)}) async-start(bf16[384,2,128]{2,1,0:T(2,128)(2,1)} %bitcast.9), calls=%async_computation.2 | async-start | bytes 393216 | tf_op jit(solution)/shard_map/all_to_all | solution.py:568
  98.1 6.4 %collective-permute-start.2 = (f32[4,81,128]{2,1,0:T(8,128)S(1)}, f32[4,81,128]{2,1,0:T(8,128)S(1)}, u32[]{:S(2)}, u32[]{:S(2)}) collective-permute-start(f32[4,81,128]{2,1,0:T(8,128)S(1)} %nest.1.own_ref), channel_id=1, source_target_pairs={{0,128},{128,0},{1,129},{129,1},{2,130},{130,2},{3,131},{131,3},{4... | collective-permute-start | bytes 497672 | tf_op jit(solution)/shard_map/ppermute | solution.py:714

commit v10 on v8

--- a/solution.py
+++ b/solution.py
@@ -18,10 +18,10 @@
 LPAD = 96
 RING = 16
 BSTR = LPAD * RING
-SENT = 5
+SENT = 6
 FLAT = 2 * LEV * ROWS
-HALO_ROWS = 816
-DIST = ((0, 1), (2, None), (3, None), (4, None))
+HALO_ROWS = 992
+DIST = ((0, 1), (2, 3), (4, None), (5, None))
 SPLIT = 40
 PACK = 12
 EPACK = 6
@@ -78,7 +78,8 @@
         for owner in range(2):
             for k in range(STEPS):
                 send[part, LEV + k, owner, L_DEST[owner] + part * STEPS + k] = 1.0
-    send = send.reshape(2 * W, 2 * W).astype(np.float32)
+    coarse, fine, _ = split3(send.reshape(2 * W, 2 * W))
+    send = np.concatenate([coarse, coarse, fine])
     mix = [
         padded_transpose(power[STEPS - k] * RELAX * keep ** (STEPS - 1 - k))
         for k in range(STEPS)
@@ -124,18 +125,23 @@
 
 
 def halo_kernel(
-    tile_ref, parent_hbm, terrain_hbm, nest_hbm, bidx_hbm, dest_hbm, mix_hbm,
-    parent_ref, first_ref, second_ref, nest_ref, bidx_ref, dest_ref, mix_ref,
-    terrain_ref, down_ref, up_ref, damp_ref, sems,
+    tile_ref, parent_hbm, terrain_hbm, nest_hbm, bidx_hbm, dest_hbm, mix_hbm, shift_hbm,
+    parent_ref, first_ref, second_ref, nest_ref, moved_ref, dest_ref, mix_ref,
+    terrain_ref, down_ref, up_ref, damp_ref, bidx_ref, shift_ref, sems,
 ):
     copies = start_all(
         [
             (parent_hbm, parent_ref),
             (terrain_hbm, terrain_ref),
-            (nest_hbm, nest_ref),
             (bidx_hbm, bidx_ref),
             (dest_hbm, dest_ref),
             (mix_hbm, mix_ref),
+            (shift_hbm, shift_ref),
+        ]
+        + [
+            (nest_hbm.at[:, part, b, :], nest_ref.at[b * 2 + part])
+            for b in range(2)
+            for part in range(2)
         ],
         sems,
     )
@@ -159,43 +165,44 @@
     second_ref[...] = jnp.where(even, up, down).astype(BF16)
     for copy in copies[2:]:
         copy.wait()
-
-
-def send_kernel(
-    shift_hbm, nest_ref, bidx_ref, dest_ref, mix_ref,
-    msg_ref,
-    shift_ref, pad_ref, sems,
-):
-    copies = start_all([(shift_hbm, shift_ref)], sems)
+    for s in range(STEPS):
+        idx = bidx_ref[s : s + 1, :]
+        col = jnp.bitwise_and(idx, W - 1)
+        moved = jnp.bitwise_and(col + shift_ref[s], W - 1)
+        moved_ref[s : s + 1, :] = idx - col + moved
+
+
+def send_kernel(nest_ref, moved_ref, dest_ref, mix_ref, msg_ref, pad_ref):
     zeros = jnp.zeros((W - LEV + 1, W), F32)
     for b in range(2):
         for part in range(2):
             top = part * W
             pad_ref[b, top + LEV - 1 : top + W, :] = zeros
-            pad_ref[b, top : top + LEV, :] = nest_ref[:, part, b, :]
+            pad_ref[b, top : top + LEV, :] = nest_ref[b * 2 + part]
             pad_ref[b, top + LEV : top + LEV + STEPS, :] = dest_ref[
                 :, part * W : (part + 1) * W
             ].astype(F32)
+        value = pad_ref[b]
+        coarse = value.astype(BF16)
+        fine = (value - coarse.astype(F32)).astype(BF16)
         res = lax.dot_general(
-            pad_ref[b],
+            jnp.concatenate([coarse, fine, coarse], axis=0),
             mix_ref[...],
             (((0,), (0,)), ((), ())),
-            precision=lax.Precision.HIGHEST,
             preferred_element_type=F32,
         )
         for owner in range(2):
             start = b * 2 * W + owner * W
             msg_ref[start : start + W, :] = res[:, owner * W : (owner + 1) * W]
-    copies[0].wait()
     lane = lax.broadcasted_iota(jnp.int32, (NT, W), 1)
     tile = lax.broadcasted_iota(jnp.int32, (NT, W), 0)
     asked = jnp.logical_or(lane == L_REQ, lane == L_REQ + 1)
     wanted = tile == L_REQ + jnp.bitwise_and(lane, 1)
     for s in range(STEPS):
-        idx = bidx_ref[s : s + 1, :]
+        idx = moved_ref[s : s + 1, :]
         owner = jnp.right_shift(idx, 10)
         row = jnp.bitwise_and(jnp.right_shift(idx, 7), ROWS - 1)
-        col = jnp.bitwise_and(jnp.bitwise_and(idx, W - 1) + shift_ref[s], W - 1)
+        col = jnp.bitwise_and(idx, W - 1)
         mine = jnp.where(tile == owner, 1.0, 0.0).astype(BF16)
         found = []
         for value in (row + 1, col):
@@ -562,24 +569,26 @@
     parent = parent_state.reshape(FLAT, W)
 
     nest = nest_state.reshape(2, LEV, 2, W).transpose(1, 2, 0, 3)
-    kept, down, up, nest, bidx, dest, q_mix = call(
+    kept, down, up, nest, moved, dest, q_mix = call(
         halo_kernel,
         (
             pltpu.VMEM((FLAT, W), F32),
             sds((HALO_ROWS, W), BF16),
             sds((HALO_ROWS, W), BF16),
-            pltpu.VMEM((LEV, 2, 2, W), F32),
+            pltpu.VMEM((4, LEV, W), F32),
             pltpu.VMEM((STEPS, NT), jnp.int32),
             pltpu.VMEM((STEPS, 2 * W), jnp.int32),
-            pltpu.VMEM((2 * W, 2 * W), F32),
+            pltpu.VMEM((6 * W, 2 * W), BF16),
         ),
-        in_specs=[SM, HB, HB, HB, HB, HB, HB],
+        in_specs=[SM, HB, HB, HB, HB, HB, HB, HB],
         scratch=[
             pltpu.VMEM((ROWS, W), jnp.int32),
             pltpu.VMEM((HALO_ROWS, W), F32),
             pltpu.VMEM((HALO_ROWS, W), F32),
             pltpu.VMEM((ROWS, W), F32),
-            pltpu.SemaphoreType.DMA((6,)),
+            pltpu.VMEM((STEPS, NT), jnp.int32),
+            pltpu.SMEM((STEPS,), jnp.int32),
+            pltpu.SemaphoreType.DMA((10,)),
         ],
         name="halo",
         nbytes=1 << 20,
@@ -591,19 +600,15 @@
         in_hbm(boundary_index),
         in_hbm(reloc_dest),
         in_hbm(q_mix),
+        in_hbm(shift_x),
     )
     message = call(
         send_kernel,
         sds((4 * NT, W), F32),
-        in_specs=[HB, VM, VM, VM, VM],
-        scratch=[
-            pltpu.SMEM((STEPS,), jnp.int32),
-            pltpu.VMEM((2, 2 * W, W), F32),
-            pltpu.SemaphoreType.DMA((1,)),
-        ],
+        scratch=[pltpu.VMEM((2, 2 * W, W), F32)],
         name="send",
         nbytes=64 << 20,
-    )(in_hbm(shift_x), nest, bidx, dest, q_mix)
+    )(nest, moved, dest, q_mix)
     pairs = [(i, i + 1) for i in range(0, NT, 2)] + [(i + 1, i) for i in range(0, NT, 2)]
     gaps = [(i, i + 1) for i in range(1, NT - 1, 2)]
     gaps = gaps + [(i + 1, i) for i in range(1, NT - 1, 2)]

time: 106 us -> 105 us (level)
  transfers between devices with their start and end apart: 6 -> 6, of which waited for: 4 -> 4; matrix products, arithmetic and copies ran while one was open for 1% -> 1% of each run, Pallas kernels for 11% -> 12%
where the time goes in v10:
time: 105 us
  starting transfers between devices  41.6 us (40%)
  waiting for transfers between devices  24.4 us (23%)
  Pallas kernels  19 us (18%)
  blocking collectives  17.7 us (17%)
  local copies, waits for them, and re-layouts  1.05 us (1%)
    all_to_all x3, starting transfers between devices, exchange(): return lax.all_to_all(x, 'tile', split_axis=0, concat_axis=0, tiled=True)  30.8 us
    all_to_all x3, waiting for transfers between devices, exchange(): return lax.all_to_all(x, 'tile', split_axis=0, concat_axis=0, tiled=True)  24.2 us
    all_to_all x1, blocking collectives, exchange(): return lax.all_to_all(x, 'tile', split_axis=0, concat_axis=0, tiled=True)  17.7 us
    pallas_call x1, Pallas kernels, on_device(): call(parent_kernel, (pltpu.VMEM((STEPS, 2 * W, ROWS * W), BF16), pltpu.HB...  6.62 us
    ppermute x1, starting transfers between devices, on_device(): other = lax.ppermute(nest_out, 'member', [(0, 1), (1, 0)])  5.4 us
    ppermute x1, starting transfers between devices, on_device(): from_pair = lax.ppermute(down, 'tile', pairs)  4.74 us
    pallas_call x1, Pallas kernels, on_device(): call(last_parent_kernel, sds((2 * LEV, ROWS, W), F32), in_specs=[HB, HB],...  3.26 us
    pallas_call x1, Pallas kernels, on_device(): call(plan_kernel, (sds((2, 4 * NT, 4 * NT), BF16), sds((4 * NT, W), F32))...  2.18 us
  transfers between devices with their start and end apart: 6, of which 4 were waited for; matrix products, arithmetic and copies ran while one was open for 1% of the time, Pallas kernels for 12%

profile of v10, /device:TPU:1, one launch (start us, length us, event | category | flops | bytes accessed | tf_op | source)
XLA Modules:
  0.0 104.5 jit_solution(10201785910199179646)
XLA Ops:
  0.6 1.5 %halo.1 = (f32[1296,128]{1,0:T(8,128)S(1)}, bf16[992,128]{1,0:T(8,128)(2,1)S(1)}, bf16[992,128]{1,0:T(8,128)(2,1)S(1)}, f32[4,81,128]{2,1,0:T(8,128)S(1)}, s32[4...) custom-call(s32[1]{0:T(128)} %bitcast.1.tile_ref, f32[1296,128]{1,0:T(8,128)} %bitcast.24, ...), custom_call_target="tpu_custom_call" | custom-call | bytes 1048576 | tf_op jit(solution)/shard_map/halo/pallas_call | solution.py:572
  2.2 0.7 collective-permute-start
  2.8 4.7 %collective-permute-start.1 = (bf16[992,128]{1,0:T(8,128)(2,1)S(1)}, bf16[992,128]{1,0:T(8,128)(2,1)S(1)}, u32[]{:S(2)}, u32[]{:S(2)}) collective-permute-start(bf16[992,128]{1,0:T(8,128)(2,1)S(1)} %get-tuple-element.28), channel_id=1, source_target_pairs={{0,1},{2,3},{4,5},{6,7},{8,9},{10,11},{12,13},{14,15},{16,17},{18,... | collective-permute-start | bytes 761864 | tf_op jit(solution)/shard_map/ppermute | solution.py:616
  7.6 1.1 %send.1 = f32[512,128]{1,0:T(8,128)} custom-call(f32[4,81,128]{2,1,0:T(8,128)S(1)} %get-tuple-element.22.nest_ref, s32[4,128]{1,0:T(4,128)S(1)} %get-tuple-element.23.moved_ref, s32[4,256]{1,0:T(4,128)S(1)} %get-tuple-element.24.dest_ref, bf16[768,256]{1,0:T(8,128)(2,1)S(1)} %get-tuple-element.25.mix_ref), custom_call_target="tpu_custom_call" | custom-call | bytes 67108864 | tf_op jit(solution)/shard_map/send/pallas_call | solution.py:605
  8.7 14.3 %all-to-all-start = ((f32[128,4,128]{2,1,0:T(4,128)}), f32[128,4,128]{2,1,0:T(4,128)S(1)}, u32[]{:S(2)}, u32[]{:S(2)}) async-start(f32[128,4,128]{2,1,0:T(4,128)} %bitcast.5), calls=%async_computation | async-start | bytes 524288 | tf_op jit(solution)/shard_map/all_to_all | solution.py:561
  23.0 0.0 collective-permute-done.second_ref
  23.0 0.0 collective-permute-done.1.first_ref
  23.0 6.6 %parent.1 = (bf16[4,256,1024]{2,1,0:T(8,128)(2,1)S(1)}, f32[3072,128]{1,0:T(8,128)}) custom-call(s32[1]{0:T(128)} %bitcast.1.tile_ref, f32[1296,128]{1,0:T(8,128)S(1)} %get-tuple-element.26.parent_ref, bf16[992,128]{1,0:T(8,128)(2,1)S(1)} %collective-permute-done.second_ref, bf16[992,128]{1,0:T(8,128)(2,1)S(1)} %collective-permute-done.1.first_ref, ...), custom_call_target="tpu_custom_call" | custom-call | flops 8589934592 | bytes 134217728 | tf_op jit(solution)/shard_map/parent/pallas_call | solution.py:618
  29.7 0.0 copy-start.1
  29.7 5.3 %all-to-all-done = f32[128,4,128]{2,1,0:T(4,128)S(1)} async-done(((f32[128,4,128]{2,1,0:T(4,128)}), f32[128,4,128]{2,1,0:T(4,128)S(1)}, u32[]{:S(2)}, u32[]{:S(2)}) %all-to-all-start) | async-done | bytes 262176 | tf_op jit(solution)/shard_map/all_to_all | solution.py:561
  34.9 1.7 %gather.1 = bf16[1536,128]{1,0:T(8,128)(2,1)} custom-call(f32[512,128]{1,0:T(8,128)S(1)} %bitcast.21, bf16[4,256,1024]{2,1,0:T(8,128)(2,1)S(1)} %get-tuple-element.29.cells_ref), custom_call_target="tpu_custom_call" | custom-call | flops 536870912 | bytes 3145728 | tf_op jit(solution)/shard_map/gather/pallas_call | solution.py:642
  36.6 8.0 %all-to-all-start.1 = ((bf16[384,4,128]{2,1,0:T(4,128)(2,1)}), bf16[384,4,128]{2,1,0:T(4,128)(2,1)S(1)}, u32[]{:S(2)}, u32[]{:S(2)}) async-start(bf16[384,4,128]{2,1,0:T(4,128)(2,1)} %bitcast.7), calls=%async_computation.1 | async-start | bytes 786432 | tf_op jit(solution)/shard_map/all_to_all | solution.py:561
  44.6 0.0 copy-done.1
  44.6 0.1 reshape.56
  44.7 0.1 copy.14
  44.8 0.1 reshape.57.bperm_ref
  44.9 0.0 copy-start
  44.9 2.2 %plan.1 = (bf16[2,512,512]{2,1,0:T(8,128)(2,1)S(1)}, f32[512,128]{1,0:T(8,128)S(1)}) custom-call(s32[1]{0:T(128)} %bitcast.1.tile_ref, f32[512,128]{1,0:T(8,128)S(1)} %bitcast.22), custom_call_target="tpu_custom_call" | custom-call | flops 268435456 | bytes 3145728 | tf_op jit(solution)/shard_map/plan/pallas_call | solution.py:652
  47.1 10.8 %all-to-all-done.1 = bf16[384,4,128]{2,1,0:T(4,128)(2,1)S(1)} async-done(((bf16[384,4,128]{2,1,0:T(4,128)(2,1)}), bf16[384,4,128]{2,1,0:T(4,128)(2,1)S(1)}, u32[]{:S(2)}, u32[]{:S(2)}) %all-to-all-start.1) | async-done | bytes 393248 | tf_op jit(solution)/shard_map/all_to_all | solution.py:561
  57.9 1.2 %regroup.1 = bf16[768,128]{1,0:T(8,128)(2,1)} custom-call(s32[4,128]{1,0:T(4,128)S(1)} %reshape.57.bperm_ref, bf16[1536,128]{1,0:T(8,128)(2,1)S(1)} %bitcast.18), custom_call_target="tpu_custom_call" | custom-call | flops 67108864 | bytes 1048576 | tf_op jit(solution)/shard_map/regroup/pallas_call | solution.py:663
  59.0 8.5 %all-to-all-start.2 = ((bf16[384,2,128]{2,1,0:T(2,128)(2,1)}), bf16[384,2,128]{2,1,0:T(2,128)(2,1)S(1)}, u32[]{:S(2)}, u32[]{:S(2)}) async-start(bf16[384,2,128]{2,1,0:T(2,128)(2,1)} %bitcast.9), calls=%async_computation.2 | async-start | bytes 393216 | tf_op jit(solution)/shard_map/all_to_all | solution.py:561
  67.5 3.3 %last_parent.1 = f32[162,8,128]{2,1,0:T(8,128)} custom-call(f32[3072,128]{1,0:T(8,128)} %get-tuple-element.33.ring_hbm, s32[8,128]{1,0:T(8,128)} %terrain_hbm.5), custom_call_target="tpu_custom_call" | custom-call | flops 4194304 | bytes 2097152 | tf_op jit(solution)/shard_map/last_parent/pallas_call | solution.py:673
  70.8 8.1 %all-to-all-done.2 = bf16[384,2,128]{2,1,0:T(2,128)(2,1)S(1)} async-done(((bf16[384,2,128]{2,1,0:T(2,128)(2,1)}), bf16[384,2,128]{2,1,0:T(2,128)(2,1)S(1)}, u32[]{:S(2)}, u32[]{:S(2)}) %all-to-all-start.2) | async-done | bytes 196640 | tf_op jit(solution)/shard_map/all_to_all | solution.py:561
  78.9 0.0 copy-done
  78.9 0.6 owner.1
  79.5 17.7 %all_to_all.20 = f32[128,4,128]{2,1,0:T(4,128)S(1)} all-to-all(f32[128,4,128]{2,1,0:T(4,128)S(1)} %bitcast.19), channel_id=1, replica_groups=mesh['member'=2,'tile'=128] {'tile'}, dimensions={0} | all-to-all | bytes 524288 | tf_op jit(solution)/shard_map/all_to_all | solution.py:561
  97.2 0.2 nest.1.own_ref
  97.4 5.4 %collective-permute-start.2 = (f32[324,128]{1,0:T(8,128)S(1)}, f32[324,128]{1,0:T(8,128)S(1)}, u32[]{:S(2)}, u32[]{:S(2)}) collective-permute-start(f32[324,128]{1,0:T(8,128)S(1)} %nest.1.own_ref), channel_id=1, source_target_pairs={{0,128},{128,0},{1,129},{129,1},{2,130},{130,2},{3,131},{131,3},{4... | collective-permute-start | bytes 497672 | tf_op jit(solution)/shard_map/ppermute | solution.py:705
  102.8 0.8 reshape.70
  103.5 0.3 collective-permute-done.2.other_ref
  103.8 0.7 stats.1
Async XLA Ops:
  2.2 20.9 %collective-permute-start = (bf16[992,128]{1,0:T(8,128)(2,1)S(1)}, bf16[992,128]{1,0:T(8,128)(2,1)S(1)}, u32[]{:S(2)}, u32[]{:S(2)}) collective-permute-start(bf16[992,128]{1,0:T(8,128)(2,1)S(1)} %get-tuple-element.27), channel_id=1, source_target_pairs={{1,2},{3,4},{5,6},{7,8},{9,10},{11,12},{13,14},{15,16},{17,18},{19... | collective-permute-start | bytes 761864 | tf_op jit(solution)/shard_map/ppermute | solution.py:615
  2.8 20.2 %collective-permute-start.1 = (bf16[992,128]{1,0:T(8,128)(2,1)S(1)}, bf16[992,128]{1,0:T(8,128)(2,1)S(1)}, u32[]{:S(2)}, u32[]{:S(2)}) collective-permute-start(bf16[992,128]{1,0:T(8,128)(2,1)S(1)} %get-tuple-element.28), channel_id=1, source_target_pairs={{0,1},{2,3},{4,5},{6,7},{8,9},{10,11},{12,13},{14,15},{16,17},{18,... | collective-permute-start | bytes 761864 | tf_op jit(solution)/shard_map/ppermute | solution.py:616
  8.7 26.2 %all-to-all-start = ((f32[128,4,128]{2,1,0:T(4,128)}), f32[128,4,128]{2,1,0:T(4,128)S(1)}, u32[]{:S(2)}, u32[]{:S(2)}) async-start(f32[128,4,128]{2,1,0:T(4,128)} %bitcast.5), calls=%async_computation | async-start | bytes 524288 | tf_op jit(solution)/shard_map/all_to_all | solution.py:561
  29.7 14.9 %copy-start.1 = (s32[4,128]{1,0:T(4,128)S(1)}, s32[4,128]{1,0:T(4,128)}, u32[]{:S(2)}) copy-start(s32[4,128]{1,0:T(4,128)} %bidx_hbm.1) | copy-start | bytes 6148
  36.6 21.3 %all-to-all-start.1 = ((bf16[384,4,128]{2,1,0:T(4,128)(2,1)}), bf16[384,4,128]{2,1,0:T(4,128)(2,1)S(1)}, u32[]{:S(2)}, u32[]{:S(2)}) async-start(bf16[384,4,128]{2,1,0:T(4,128)(2,1)} %bitcast.7), calls=%async_computation.1 | async-start | bytes 786432 | tf_op jit(solution)/shard_map/all_to_all | solution.py:561
  44.9 34.0 %copy-start = (bf16[2,256,384]{2,1,0:T(8,128)(2,1)S(1)}, bf16[2,256,384]{2,1,0:T(8,128)(2,1)}, u32[]{:S(2)}) copy-start(bf16[2,256,384]{2,1,0:T(8,128)(2,1)} %constant.9.clone.mix_ref) | copy-start | bytes 1179652
  59.0 19.8 %all-to-all-start.2 = ((bf16[384,2,128]{2,1,0:T(2,128)(2,1)}), bf16[384,2,128]{2,1,0:T(2,128)(2,1)S(1)}, u32[]{:S(2)}, u32[]{:S(2)}) async-start(bf16[384,2,128]{2,1,0:T(2,128)(2,1)} %bitcast.9), calls=%async_computation.2 | async-start | bytes 393216 | tf_op jit(solution)/shard_map/all_to_all | solution.py:561
  97.4 6.4 %collective-permute-start.2 = (f32[324,128]{1,0:T(8,128)S(1)}, f32[324,128]{1,0:T(8,128)S(1)}, u32[]{:S(2)}, u32[]{:S(2)}) collective-permute-start(f32[324,128]{1,0:T(8,128)S(1)} %nest.1.own_ref), channel_id=1, source_target_pairs={{0,128},{128,0},{1,129},{129,1},{2,130},{130,2},{3,131},{131,3},{4... | collective-permute-start | bytes 497672 | tf_op jit(solution)/shard_map/ppermute | solution.py:705

commit v11 on v10

--- a/solution.py
+++ b/solution.py
@@ -129,10 +129,12 @@
     parent_ref, first_ref, second_ref, nest_ref, moved_ref, dest_ref, mix_ref,
     terrain_ref, down_ref, up_ref, damp_ref, bidx_ref, shift_ref, sems,
 ):
+    half = FLAT // 2
     copies = start_all(
         [
-            (parent_hbm, parent_ref),
             (terrain_hbm, terrain_ref),
+            (parent_hbm.at[pl.ds(0, half)], parent_ref.at[pl.ds(0, half)]),
+            (parent_hbm.at[pl.ds(half, half)], parent_ref.at[pl.ds(half, half)]),
             (bidx_hbm, bidx_ref),
             (dest_hbm, dest_ref),
             (mix_hbm, mix_ref),
@@ -145,25 +147,32 @@
         ],
         sems,
     )
-    for copy in copies[:2]:
-        copy.wait()
+
+    def put(ref, distance, base, count, value):
+        coarse, fine = DIST[distance]
+        ref[pl.ds(base + coarse, count, stride=SENT), :] = value
+        if fine is not None:
+            rest = value - value.astype(BF16).astype(F32)
+            ref[pl.ds(base + fine, count, stride=SENT), :] = rest
+
+    sides = ((down_ref, (7, 6, 5, 4)), (up_ref, (0, 1, 2, 3)))
+    copies[0].wait()
     damp_ref[...] = DRAG * terrain_ref[...].astype(F32) / 3000.0
-    for ref, rows in ((down_ref, (7, 6, 5, 4)), (up_ref, (0, 1, 2, 3))):
+    for ref, rows in sides:
         ref[HALO_ROWS - 24 :, :] = jnp.zeros((24, W), F32)
-        for row, (coarse, fine) in zip(rows, DIST):
-            for count, base, value in (
-                (2 * LEV, 0, parent_ref[pl.ds(row, 2 * LEV, stride=ROWS), :]),
-                (1, 2 * LEV * SENT, damp_ref[row : row + 1, :]),
-            ):
-                ref[pl.ds(base + coarse, count, stride=SENT), :] = value
-                if fine is not None:
-                    rest = value - value.astype(BF16).astype(F32)
-                    ref[pl.ds(base + fine, count, stride=SENT), :] = rest
+        for distance, row in enumerate(rows):
+            put(ref, distance, 2 * LEV * SENT, 1, damp_ref[row : row + 1, :])
+    for member in range(2):
+        copies[1 + member].wait()
+        for ref, rows in sides:
+            for distance, row in enumerate(rows):
+                value = parent_ref[pl.ds(member * half + row, LEV, stride=ROWS), :]
+                put(ref, distance, member * LEV * SENT, LEV, value)
     even = jnp.bitwise_and(tile_ref[0], 1) == 0
     down, up = down_ref[...], up_ref[...]
     first_ref[...] = jnp.where(even, down, up).astype(BF16)
     second_ref[...] = jnp.where(even, up, down).astype(BF16)
-    for copy in copies[2:]:
+    for copy in copies[3:]:
         copy.wait()
     for s in range(STEPS):
         idx = bidx_ref[s : s + 1, :]
@@ -254,7 +263,7 @@
 
 
 def parent_kernel(
-    tile_ref, parent_ref, second_ref, first_ref, terrain_hbm,
+    tile_ref, parent_ref, first_ref, second_ref, terrain_hbm,
     cells_ref, ring_hbm,
     next_ref, prev_ref, halo_ref, damp_ref, a_ref, b_ref, ring_ref, terrain_ref, sems,
 ):
@@ -588,7 +597,7 @@
             pltpu.VMEM((ROWS, W), F32),
             pltpu.VMEM((STEPS, NT), jnp.int32),
             pltpu.SMEM((STEPS,), jnp.int32),
-            pltpu.SemaphoreType.DMA((10,)),
+            pltpu.SemaphoreType.DMA((11,)),
         ],
         name="halo",
         nbytes=1 << 20,
@@ -612,8 +621,8 @@
     pairs = [(i, i + 1) for i in range(0, NT, 2)] + [(i + 1, i) for i in range(0, NT, 2)]
     gaps = [(i, i + 1) for i in range(1, NT - 1, 2)]
     gaps = gaps + [(i + 1, i) for i in range(1, NT - 1, 2)]
+    from_pair = lax.ppermute(down, "tile", pairs)
     from_gap = lax.ppermute(up, "tile", gaps)
-    from_pair = lax.ppermute(down, "tile", pairs)
     first = exchange(message.reshape(NT, 4, W)).reshape(4 * NT, W)
     cells, ring = call(
         parent_kernel,
@@ -637,7 +646,7 @@
         name="parent",
         flops=1 << 33,
         nbytes=1 << 27,
-    )(tile, kept, from_gap, from_pair, in_hbm(terrain))
+    )(tile, kept, from_pair, from_gap, in_hbm(terrain))
 
     values = call(
         gather_kernel,

time: 105 us -> 105 us (level)
    all_to_all x3, starting transfers between devices: 30.8 us -> 33.4 us  [exchange(): return lax.all_to_all(x, 'tile', split_axis=0, concat_axis=0, tiled=True)]
    ppermute x1, starting transfers between devices: 4.74 us -> 2.21 us  [on_device(): from_pair = lax.ppermute(down, 'tile', pairs)]
where the time goes in v11:
time: 105 us
  starting transfers between devices  41.7 us (40%)
  waiting for transfers between devices  24.4 us (23%)
  Pallas kernels  18.9 us (18%)
  blocking collectives  17.7 us (17%)
  local copies, waits for them, and re-layouts  1.05 us (1%)
    all_to_all x3, starting transfers between devices, exchange(): return lax.all_to_all(x, 'tile', split_axis=0, concat_axis=0, tiled=True)  33.4 us
    all_to_all x3, waiting for transfers between devices, exchange(): return lax.all_to_all(x, 'tile', split_axis=0, concat_axis=0, tiled=True)  24.1 us
    all_to_all x1, blocking collectives, exchange(): return lax.all_to_all(x, 'tile', split_axis=0, concat_axis=0, tiled=True)  17.7 us
    pallas_call x1, Pallas kernels, on_device(): call(parent_kernel, (pltpu.VMEM((STEPS, 2 * W, ROWS * W), BF16), pltpu.HB...  6.62 us
    ppermute x1, starting transfers between devices, on_device(): other = lax.ppermute(nest_out, 'member', [(0, 1), (1, 0)])  5.39 us
    pallas_call x1, Pallas kernels, on_device(): call(last_parent_kernel, sds((2 * LEV, ROWS, W), F32), in_specs=[HB, HB],...  3.26 us
    ppermute x1, starting transfers between devices, on_device(): from_pair = lax.ppermute(down, 'tile', pairs)  2.21 us
    pallas_call x1, Pallas kernels, on_device(): call(plan_kernel, (sds((2, 4 * NT, 4 * NT), BF16), sds((4 * NT, W), F32))...  2.18 us
  transfers between devices with their start and end apart: 6, of which 4 were waited for; matrix products, arithmetic and copies ran while one was open for 1% of the time, Pallas kernels for 12%

profile of v11, /device:TPU:1, one launch (start us, length us, event | category | flops | bytes accessed | tf_op | source)
XLA Modules:
  0.0 104.6 jit_solution(9687611797768389395)
XLA Ops:
  0.6 1.4 %halo.1 = (f32[1296,128]{1,0:T(8,128)S(1)}, bf16[992,128]{1,0:T(8,128)(2,1)S(1)}, bf16[992,128]{1,0:T(8,128)(2,1)S(1)}, f32[4,81,128]{2,1,0:T(8,128)S(1)}, s32[4...) custom-call(s32[1]{0:T(128)} %bitcast.1.tile_ref, f32[1296,128]{1,0:T(8,128)} %bitcast.24, ...), custom_call_target="tpu_custom_call" | custom-call | bytes 1048576 | tf_op jit(solution)/shard_map/halo/pallas_call | solution.py:581
  2.1 2.2 %collective-permute-start = (bf16[992,128]{1,0:T(8,128)(2,1)S(1)}, bf16[992,128]{1,0:T(8,128)(2,1)S(1)}, u32[]{:S(2)}, u32[]{:S(2)}) collective-permute-start(bf16[992,128]{1,0:T(8,128)(2,1)S(1)} %get-tuple-element.27), channel_id=1, source_target_pairs={{0,1},{2,3},{4,5},{6,7},{8,9},{10,11},{12,13},{14,15},{16,17},{18,... | collective-permute-start | bytes 761864 | tf_op jit(solution)/shard_map/ppermute | solution.py:624
  4.3 0.7 collective-permute-start.1
  5.0 1.1 %send.1 = f32[512,128]{1,0:T(8,128)} custom-call(f32[4,81,128]{2,1,0:T(8,128)S(1)} %get-tuple-element.22.nest_ref, s32[4,128]{1,0:T(4,128)S(1)} %get-tuple-element.23.moved_ref, s32[4,256]{1,0:T(4,128)S(1)} %get-tuple-element.24.dest_ref, bf16[768,256]{1,0:T(8,128)(2,1)S(1)} %get-tuple-element.25.mix_ref), custom_call_target="tpu_custom_call" | custom-call | bytes 67108864 | tf_op jit(solution)/shard_map/send/pallas_call | solution.py:614
  6.1 17.0 %all-to-all-start = ((f32[128,4,128]{2,1,0:T(4,128)}), f32[128,4,128]{2,1,0:T(4,128)S(1)}, u32[]{:S(2)}, u32[]{:S(2)}) async-start(f32[128,4,128]{2,1,0:T(4,128)} %bitcast.5), calls=%async_computation | async-start | bytes 524288 | tf_op jit(solution)/shard_map/all_to_all | solution.py:570
  23.0 0.0 collective-permute-done.first_ref
  23.0 0.0 collective-permute-done.1.second_ref
  23.1 6.6 %parent.1 = (bf16[4,256,1024]{2,1,0:T(8,128)(2,1)S(1)}, f32[3072,128]{1,0:T(8,128)}) custom-call(s32[1]{0:T(128)} %bitcast.1.tile_ref, f32[1296,128]{1,0:T(8,128)S(1)} %get-tuple-element.26.parent_ref, bf16[992,128]{1,0:T(8,128)(2,1)S(1)} %collective-permute-done.first_ref, bf16[992,128]{1,0:T(8,128)(2,1)S(1)} %collective-permute-done.1.second_ref, ...), custom_call_target="tpu_custom_call" | custom-call | flops 8589934592 | bytes 134217728 | tf_op jit(solution)/shard_map/parent/pallas_call | solution.py:627
  29.7 0.0 copy-start.1
  29.7 5.3 %all-to-all-done = f32[128,4,128]{2,1,0:T(4,128)S(1)} async-done(((f32[128,4,128]{2,1,0:T(4,128)}), f32[128,4,128]{2,1,0:T(4,128)S(1)}, u32[]{:S(2)}, u32[]{:S(2)}) %all-to-all-start) | async-done | bytes 262176 | tf_op jit(solution)/shard_map/all_to_all | solution.py:570
  35.0 1.7 %gather.1 = bf16[1536,128]{1,0:T(8,128)(2,1)} custom-call(f32[512,128]{1,0:T(8,128)S(1)} %bitcast.21, bf16[4,256,1024]{2,1,0:T(8,128)(2,1)S(1)} %get-tuple-element.29.cells_ref), custom_call_target="tpu_custom_call" | custom-call | flops 536870912 | bytes 3145728 | tf_op jit(solution)/shard_map/gather/pallas_call | solution.py:651
  36.6 8.0 %all-to-all-start.1 = ((bf16[384,4,128]{2,1,0:T(4,128)(2,1)}), bf16[384,4,128]{2,1,0:T(4,128)(2,1)S(1)}, u32[]{:S(2)}, u32[]{:S(2)}) async-start(bf16[384,4,128]{2,1,0:T(4,128)(2,1)} %bitcast.7), calls=%async_computation.1 | async-start | bytes 786432 | tf_op jit(solution)/shard_map/all_to_all | solution.py:570
  44.6 0.0 copy-done.1
  44.6 0.1 reshape.56
  44.7 0.1 copy.14
  44.8 0.1 reshape.57.bperm_ref
  44.9 0.0 copy-start
  44.9 2.2 %plan.1 = (bf16[2,512,512]{2,1,0:T(8,128)(2,1)S(1)}, f32[512,128]{1,0:T(8,128)S(1)}) custom-call(s32[1]{0:T(128)} %bitcast.1.tile_ref, f32[512,128]{1,0:T(8,128)S(1)} %bitcast.22), custom_call_target="tpu_custom_call" | custom-call | flops 268435456 | bytes 3145728 | tf_op jit(solution)/shard_map/plan/pallas_call | solution.py:661
  47.1 10.8 %all-to-all-done.1 = bf16[384,4,128]{2,1,0:T(4,128)(2,1)S(1)} async-done(((bf16[384,4,128]{2,1,0:T(4,128)(2,1)}), bf16[384,4,128]{2,1,0:T(4,128)(2,1)S(1)}, u32[]{:S(2)}, u32[]{:S(2)}) %all-to-all-start.1) | async-done | bytes 393248 | tf_op jit(solution)/shard_map/all_to_all | solution.py:570
  57.9 1.2 %regroup.1 = bf16[768,128]{1,0:T(8,128)(2,1)} custom-call(s32[4,128]{1,0:T(4,128)S(1)} %reshape.57.bperm_ref, bf16[1536,128]{1,0:T(8,128)(2,1)S(1)} %bitcast.18), custom_call_target="tpu_custom_call" | custom-call | flops 67108864 | bytes 1048576 | tf_op jit(solution)/shard_map/regroup/pallas_call | solution.py:672
  59.1 8.5 %all-to-all-start.2 = ((bf16[384,2,128]{2,1,0:T(2,128)(2,1)}), bf16[384,2,128]{2,1,0:T(2,128)(2,1)S(1)}, u32[]{:S(2)}, u32[]{:S(2)}) async-start(bf16[384,2,128]{2,1,0:T(2,128)(2,1)} %bitcast.9), calls=%async_computation.2 | async-start | bytes 393216 | tf_op jit(solution)/shard_map/all_to_all | solution.py:570
  67.5 3.3 %last_parent.1 = f32[162,8,128]{2,1,0:T(8,128)} custom-call(f32[3072,128]{1,0:T(8,128)} %get-tuple-element.33.ring_hbm, s32[8,128]{1,0:T(8,128)} %terrain_hbm.5), custom_call_target="tpu_custom_call" | custom-call | flops 4194304 | bytes 2097152 | tf_op jit(solution)/shard_map/last_parent/pallas_call | solution.py:682
  70.8 8.1 %all-to-all-done.2 = bf16[384,2,128]{2,1,0:T(2,128)(2,1)S(1)} async-done(((bf16[384,2,128]{2,1,0:T(2,128)(2,1)}), bf16[384,2,128]{2,1,0:T(2,128)(2,1)S(1)}, u32[]{:S(2)}, u32[]{:S(2)}) %all-to-all-start.2) | async-done | bytes 196640 | tf_op jit(solution)/shard_map/all_to_all | solution.py:570
  78.9 0.0 copy-done
  78.9 0.6 owner.1
  79.5 17.7 %all_to_all.20 = f32[128,4,128]{2,1,0:T(4,128)S(1)} all-to-all(f32[128,4,128]{2,1,0:T(4,128)S(1)} %bitcast.19), channel_id=1, replica_groups=mesh['member'=2,'tile'=128] {'tile'}, dimensions={0} | all-to-all | bytes 524288 | tf_op jit(solution)/shard_map/all_to_all | solution.py:570
  97.3 0.2 nest.1.own_ref
  97.4 5.4 %collective-permute-start.2 = (f32[324,128]{1,0:T(8,128)S(1)}, f32[324,128]{1,0:T(8,128)S(1)}, u32[]{:S(2)}, u32[]{:S(2)}) collective-permute-start(f32[324,128]{1,0:T(8,128)S(1)} %nest.1.own_ref), channel_id=1, source_target_pairs={{0,128},{128,0},{1,129},{129,1},{2,130},{130,2},{3,131},{131,3},{4... | collective-permute-start | bytes 497672 | tf_op jit(solution)/shard_map/ppermute | solution.py:714
  102.8 0.8 reshape.70
  103.6 0.3 collective-permute-done.2.other_ref
  103.8 0.7 stats.1
Async XLA Ops:
  2.1 21.0 %collective-permute-start = (bf16[992,128]{1,0:T(8,128)(2,1)S(1)}, bf16[992,128]{1,0:T(8,128)(2,1)S(1)}, u32[]{:S(2)}, u32[]{:S(2)}) collective-permute-start(bf16[992,128]{1,0:T(8,128)(2,1)S(1)} %get-tuple-element.27), channel_id=1, source_target_pairs={{0,1},{2,3},{4,5},{6,7},{8,9},{10,11},{12,13},{14,15},{16,17},{18,... | collective-permute-start | bytes 761864 | tf_op jit(solution)/shard_map/ppermute | solution.py:624
  4.3 18.8 %collective-permute-start.1 = (bf16[992,128]{1,0:T(8,128)(2,1)S(1)}, bf16[992,128]{1,0:T(8,128)(2,1)S(1)}, u32[]{:S(2)}, u32[]{:S(2)}) collective-permute-start(bf16[992,128]{1,0:T(8,128)(2,1)S(1)} %get-tuple-element.28), channel_id=1, source_target_pairs={{1,2},{3,4},{5,6},{7,8},{9,10},{11,12},{13,14},{15,16},{17,18},{19... | collective-permute-start | bytes 761864 | tf_op jit(solution)/shard_map/ppermute | solution.py:625
  6.1 28.9 %all-to-all-start = ((f32[128,4,128]{2,1,0:T(4,128)}), f32[128,4,128]{2,1,0:T(4,128)S(1)}, u32[]{:S(2)}, u32[]{:S(2)}) async-start(f32[128,4,128]{2,1,0:T(4,128)} %bitcast.5), calls=%async_computation | async-start | bytes 524288 | tf_op jit(solution)/shard_map/all_to_all | solution.py:570
  29.7 14.9 %copy-start.1 = (s32[4,128]{1,0:T(4,128)S(1)}, s32[4,128]{1,0:T(4,128)}, u32[]{:S(2)}) copy-start(s32[4,128]{1,0:T(4,128)} %bidx_hbm.1) | copy-start | bytes 6148
  36.6 21.3 %all-to-all-start.1 = ((bf16[384,4,128]{2,1,0:T(4,128)(2,1)}), bf16[384,4,128]{2,1,0:T(4,128)(2,1)S(1)}, u32[]{:S(2)}, u32[]{:S(2)}) async-start(bf16[384,4,128]{2,1,0:T(4,128)(2,1)} %bitcast.7), calls=%async_computation.1 | async-start | bytes 786432 | tf_op jit(solution)/shard_map/all_to_all | solution.py:570
  44.9 34.0 %copy-start = (bf16[2,256,384]{2,1,0:T(8,128)(2,1)S(1)}, bf16[2,256,384]{2,1,0:T(8,128)(2,1)}, u32[]{:S(2)}) copy-start(bf16[2,256,384]{2,1,0:T(8,128)(2,1)} %constant.9.clone.mix_ref) | copy-start | bytes 1179652
  59.1 19.8 %all-to-all-start.2 = ((bf16[384,2,128]{2,1,0:T(2,128)(2,1)}), bf16[384,2,128]{2,1,0:T(2,128)(2,1)S(1)}, u32[]{:S(2)}, u32[]{:S(2)}) async-start(bf16[384,2,128]{2,1,0:T(2,128)(2,1)} %bitcast.9), calls=%async_computation.2 | async-start | bytes 393216 | tf_op jit(solution)/shard_map/all_to_all | solution.py:570
  97.4 6.4 %collective-permute-start.2 = (f32[324,128]{1,0:T(8,128)S(1)}, f32[324,128]{1,0:T(8,128)S(1)}, u32[]{:S(2)}, u32[]{:S(2)}) collective-permute-start(f32[324,128]{1,0:T(8,128)S(1)} %nest.1.own_ref), channel_id=1, source_target_pairs={{0,128},{128,0},{1,129},{129,1},{2,130},{130,2},{3,131},{131,3},{4... | collective-permute-start | bytes 497672 | tf_op jit(solution)/shard_map/ppermute | solution.py:714

commit v12 on v10

--- a/solution.py
+++ b/solution.py
@@ -372,7 +372,7 @@
     out_ref[...] = scr_ref[...].astype(BF16)
 
 
-def regroup_kernel(bperm_ref, got_ref, out_ref, scr_ref, scr2_ref):
+def regroup_kernel(select_ref, got_ref, out_ref, scr_ref, scr2_ref):
     scr_ref[...] = got_ref[...].astype(F32)
     low = lax.broadcasted_iota(jnp.int32, (NT, W), 1) < CUT
 
@@ -383,14 +383,8 @@
         second = pltpu.roll(row(2 * (r - PACK) + 1), W - LEV + CUT, 1)
         return jnp.where(low, first, second)
 
-    sub = lax.broadcasted_iota(jnp.int32, (2 * NT, W), 0)
-    lane = lax.broadcasted_iota(jnp.int32, (2 * NT, W), 1)
-    parity = jnp.bitwise_and(jnp.right_shift(lane, 5), 1)
-    target = sub - parity * NT
     found = {}
     for s in range(STEPS):
-        owner = jnp.right_shift(bperm_ref[s : s + 1, :], 10)
-        hot = jnp.where(target == owner, 1.0, 0.0).astype(BF16)
         values = jnp.concatenate(
             [
                 jnp.concatenate(
@@ -401,9 +395,7 @@
             ],
             axis=0,
         ).astype(BF16)
-        res = lax.dot_general(
-            hot, values, (((0,), (0,)), ((), ())), preferred_element_type=F32
-        )
+        res = jnp.dot(select_ref[s], values, preferred_element_type=F32)
         for b in range(2):
             for j in range(4):
                 found[b, s // 2, (s % 2) * 4 + j] = res[
@@ -423,7 +415,14 @@
     out_ref[...] = scr2_ref[...].astype(BF16)
 
 
-def plan_kernel(tile_ref, got_ref, hot_ref, base_ref):
+def plan_kernel(tile_ref, got_ref, bperm_ref, hot_ref, base_ref, select_ref):
+    sub = lax.broadcasted_iota(jnp.int32, (2 * NT, W), 0)
+    lane = lax.broadcasted_iota(jnp.int32, (2 * NT, W), 1)
+    parity = jnp.bitwise_and(jnp.right_shift(lane, 5), 1)
+    target = sub - parity * NT
+    for s in range(STEPS):
+        owner = jnp.right_shift(bperm_ref[s : s + 1, :], 10)
+        select_ref[s] = jnp.where(target == owner, 1.0, 0.0).T.astype(BF16)
     late = jnp.bitwise_and(jnp.right_shift(tile_ref[0], 5), 1) == 1
     n = 4 * NT
     turned = [got_ref[pl.ds(j, NT, stride=4), :].T for j in range(4)]
@@ -649,17 +648,21 @@
     )(first, cells)
     second = exchange(values.reshape(PACK // 4 * NT, 4, W)).reshape(PACK * NT, W)
 
-    hot, base = call(
+    bperm = boundary_index.reshape(STEPS, 32, 4).transpose(0, 2, 1).reshape(STEPS, NT)
+    hot, base, select = call(
         plan_kernel,
-        (sds((2, 4 * NT, 4 * NT), BF16), sds((4 * NT, W), F32)),
-        in_specs=[SM, VM],
+        (
+            sds((2, 4 * NT, 4 * NT), BF16),
+            sds((4 * NT, W), F32),
+            pltpu.VMEM((STEPS, W, 2 * NT), BF16),
+        ),
+        in_specs=[SM, VM, VM],
         name="plan",
         flops=1 << 28,
         nbytes=3 << 20,
-    )(tile, first)
-
-    second, hot, base = lax.optimization_barrier((second, hot, base))
-    bperm = boundary_index.reshape(STEPS, 32, 4).transpose(0, 2, 1).reshape(STEPS, NT)
+    )(tile, first, bperm)
+
+    second, hot, base, select = lax.optimization_barrier((second, hot, base, select))
     edges = call(
         regroup_kernel,
         sds((EPACK * NT, W), BF16),
@@ -667,7 +670,7 @@
         name="regroup",
         flops=1 << 26,
         nbytes=1 << 20,
-    )(bperm, second)
+    )(select, second)
     third = exchange(edges.reshape(EPACK // 2 * NT, 2, W)).reshape(EPACK * NT, W)
 
     parent_out = call(

time: 105 us -> 105 us (level)
  no operation moved by 1% of the time
where the time goes in v12:
time: 105 us; the launch traced here: 104 us
  starting transfers between devices  41.6 us (40%)
  waiting for transfers between devices  24.4 us (23%)
  Pallas kernels  18.9 us (18%)
  blocking collectives  17.7 us (17%)
  local copies, waits for them, and re-layouts  1.05 us (1%)
    all_to_all x3, starting transfers between devices, exchange(): return lax.all_to_all(x, 'tile', split_axis=0, concat_axis=0, tiled=True)  30.8 us
    all_to_all x3, waiting for transfers between devices, exchange(): return lax.all_to_all(x, 'tile', split_axis=0, concat_axis=0, tiled=True)  24.2 us
    all_to_all x1, blocking collectives, exchange(): return lax.all_to_all(x, 'tile', split_axis=0, concat_axis=0, tiled=True)  17.7 us
    pallas_call x1, Pallas kernels, on_device(): call(parent_kernel, (pltpu.VMEM((STEPS, 2 * W, ROWS * W), BF16), pltpu.HB...  6.62 us
    ppermute x1, starting transfers between devices, on_device(): other = lax.ppermute(nest_out, 'member', [(0, 1), (1, 0)])  5.4 us
    ppermute x1, starting transfers between devices, on_device(): from_pair = lax.ppermute(down, 'tile', pairs)  4.74 us
    pallas_call x1, Pallas kernels, on_device(): call(last_parent_kernel, sds((2 * LEV, ROWS, W), F32), in_specs=[HB, HB],...  3.26 us
    pallas_call x1, Pallas kernels, on_device(): call(plan_kernel, (sds((2, 4 * NT, 4 * NT), BF16), sds((4 * NT, W), F32),...  2.18 us
  transfers between devices with their start and end apart: 6, of which 4 were waited for; matrix products, arithmetic and copies ran while one was open for 1% of the time, Pallas kernels for 12%

profile of v12, /device:TPU:1, one launch (start us, length us, event | category | flops | bytes accessed | tf_op | source)
XLA Modules:
  0.0 104.5 jit_solution(9217855218059114503)
XLA Ops:
  0.6 1.5 %halo.1 = (f32[1296,128]{1,0:T(8,128)S(1)}, bf16[992,128]{1,0:T(8,128)(2,1)S(1)}, bf16[992,128]{1,0:T(8,128)(2,1)S(1)}, f32[4,81,128]{2,1,0:T(8,128)S(1)}, s32[4...) custom-call(s32[1]{0:T(128)} %bitcast.tile_ref, f32[1296,128]{1,0:T(8,128)} %bitcast.24, ...), custom_call_target="tpu_custom_call" | custom-call | bytes 1048576 | tf_op jit(solution)/shard_map/halo/pallas_call | solution.py:571
  2.2 0.7 collective-permute-start
  2.8 4.7 %collective-permute-start.1 = (bf16[992,128]{1,0:T(8,128)(2,1)S(1)}, bf16[992,128]{1,0:T(8,128)(2,1)S(1)}, u32[]{:S(2)}, u32[]{:S(2)}) collective-permute-start(bf16[992,128]{1,0:T(8,128)(2,1)S(1)} %get-tuple-element.30), channel_id=1, source_target_pairs={{0,1},{2,3},{4,5},{6,7},{8,9},{10,11},{12,13},{14,15},{16,17},{18,... | collective-permute-start | bytes 761864 | tf_op jit(solution)/shard_map/ppermute | solution.py:615
  7.6 1.1 %send.1 = f32[512,128]{1,0:T(8,128)} custom-call(f32[4,81,128]{2,1,0:T(8,128)S(1)} %get-tuple-element.24.nest_ref, s32[4,128]{1,0:T(4,128)S(1)} %get-tuple-element.25.moved_ref, s32[4,256]{1,0:T(4,128)S(1)} %get-tuple-element.26.dest_ref, bf16[768,256]{1,0:T(8,128)(2,1)S(1)} %get-tuple-element.27.mix_ref), custom_call_target="tpu_custom_call" | custom-call | bytes 67108864 | tf_op jit(solution)/shard_map/send/pallas_call | solution.py:604
  8.7 14.3 %all-to-all-start = ((f32[128,4,128]{2,1,0:T(4,128)}), f32[128,4,128]{2,1,0:T(4,128)S(1)}, u32[]{:S(2)}, u32[]{:S(2)}) async-start(f32[128,4,128]{2,1,0:T(4,128)} %bitcast.4), calls=%async_computation | async-start | bytes 524288 | tf_op jit(solution)/shard_map/all_to_all | solution.py:560
  23.0 0.0 collective-permute-done.second_ref
  23.0 0.0 collective-permute-done.1.first_ref
  23.0 6.6 %parent.1 = (bf16[4,256,1024]{2,1,0:T(8,128)(2,1)S(1)}, f32[3072,128]{1,0:T(8,128)}) custom-call(s32[1]{0:T(128)} %bitcast.tile_ref, f32[1296,128]{1,0:T(8,128)S(1)} %get-tuple-element.28.parent_ref, bf16[992,128]{1,0:T(8,128)(2,1)S(1)} %collective-permute-done.second_ref, bf16[992,128]{1,0:T(8,128)(2,1)S(1)} %collective-permute-done.1.first_ref, ...), custom_call_target="tpu_custom_call" | custom-call | flops 8589934592 | bytes 134217728 | tf_op jit(solution)/shard_map/parent/pallas_call | solution.py:617
  29.7 0.0 copy-start.1
  29.7 5.3 %all-to-all-done = f32[128,4,128]{2,1,0:T(4,128)S(1)} async-done(((f32[128,4,128]{2,1,0:T(4,128)}), f32[128,4,128]{2,1,0:T(4,128)S(1)}, u32[]{:S(2)}, u32[]{:S(2)}) %all-to-all-start) | async-done | bytes 262176 | tf_op jit(solution)/shard_map/all_to_all | solution.py:560
  34.9 1.7 %gather.1 = bf16[1536,128]{1,0:T(8,128)(2,1)} custom-call(f32[512,128]{1,0:T(8,128)S(1)} %bitcast.21, bf16[4,256,1024]{2,1,0:T(8,128)(2,1)S(1)} %get-tuple-element.31.cells_ref), custom_call_target="tpu_custom_call" | custom-call | flops 536870912 | bytes 3145728 | tf_op jit(solution)/shard_map/gather/pallas_call | solution.py:641
  36.6 8.0 %all-to-all-start.1 = ((bf16[384,4,128]{2,1,0:T(4,128)(2,1)}), bf16[384,4,128]{2,1,0:T(4,128)(2,1)S(1)}, u32[]{:S(2)}, u32[]{:S(2)}) async-start(bf16[384,4,128]{2,1,0:T(4,128)(2,1)} %bitcast.6), calls=%async_computation.1 | async-start | bytes 786432 | tf_op jit(solution)/shard_map/all_to_all | solution.py:560
  44.6 0.0 copy-done.1
  44.6 0.1 reshape.63
  44.7 0.1 copy.14
  44.8 0.1 reshape.64.bperm_ref
  44.9 0.0 copy-start
  44.9 2.2 %plan.1 = (bf16[2,512,512]{2,1,0:T(8,128)(2,1)S(1)}, f32[512,128]{1,0:T(8,128)S(1)}, bf16[4,128,256]{2,1,0:T(8,128)(2,1)S(1)}) custom-call(s32[1]{0:T(128)} %bitcast.tile_ref, f32[512,128]{1,0:T(8,128)S(1)} %bitcast.22, s32[4,128]{1,0:T(4,128)S(1)} %reshape.64.bperm_ref), custom_call_target="tpu_custom_call" | custom-call | flops 268435456 | bytes 3145728 | tf_op jit(solution)/shard_map/plan/pallas_call | solution.py:652
  47.1 10.8 %all-to-all-done.1 = bf16[384,4,128]{2,1,0:T(4,128)(2,1)S(1)} async-done(((bf16[384,4,128]{2,1,0:T(4,128)(2,1)}), bf16[384,4,128]{2,1,0:T(4,128)(2,1)S(1)}, u32[]{:S(2)}, u32[]{:S(2)}) %all-to-all-start.1) | async-done | bytes 393248 | tf_op jit(solution)/shard_map/all_to_all | solution.py:560
  57.9 1.1 %regroup.1 = bf16[768,128]{1,0:T(8,128)(2,1)} custom-call(bf16[4,128,256]{2,1,0:T(8,128)(2,1)S(1)} %get-tuple-element.35.select_ref, bf16[1536,128]{1,0:T(8,128)(2,1)S(1)} %bitcast.18), custom_call_target="tpu_custom_call" | custom-call | flops 67108864 | bytes 1048576 | tf_op jit(solution)/shard_map/regroup/pallas_call | solution.py:666
  59.0 8.5 %all-to-all-start.2 = ((bf16[384,2,128]{2,1,0:T(2,128)(2,1)}), bf16[384,2,128]{2,1,0:T(2,128)(2,1)S(1)}, u32[]{:S(2)}, u32[]{:S(2)}) async-start(bf16[384,2,128]{2,1,0:T(2,128)(2,1)} %bitcast.9), calls=%async_computation.2 | async-start | bytes 393216 | tf_op jit(solution)/shard_map/all_to_all | solution.py:560
  67.4 3.3 %last_parent.1 = f32[162,8,128]{2,1,0:T(8,128)} custom-call(f32[3072,128]{1,0:T(8,128)} %get-tuple-element.37.ring_hbm, s32[8,128]{1,0:T(8,128)} %terrain_hbm.5), custom_call_target="tpu_custom_call" | custom-call | flops 4194304 | bytes 2097152 | tf_op jit(solution)/shard_map/last_parent/pallas_call | solution.py:676
  70.7 8.1 %all-to-all-done.2 = bf16[384,2,128]{2,1,0:T(2,128)(2,1)S(1)} async-done(((bf16[384,2,128]{2,1,0:T(2,128)(2,1)}), bf16[384,2,128]{2,1,0:T(2,128)(2,1)S(1)}, u32[]{:S(2)}, u32[]{:S(2)}) %all-to-all-start.2) | async-done | bytes 196640 | tf_op jit(solution)/shard_map/all_to_all | solution.py:560
  78.8 0.0 copy-done
  78.8 0.6 owner.1
  79.4 17.7 %all_to_all.20 = f32[128,4,128]{2,1,0:T(4,128)S(1)} all-to-all(f32[128,4,128]{2,1,0:T(4,128)S(1)} %bitcast.19), channel_id=1, replica_groups=mesh['member'=2,'tile'=128] {'tile'}, dimensions={0} | all-to-all | bytes 524288 | tf_op jit(solution)/shard_map/all_to_all | solution.py:560
  97.2 0.2 nest.1.own_ref
  97.3 5.4 %collective-permute-start.2 = (f32[324,128]{1,0:T(8,128)S(1)}, f32[324,128]{1,0:T(8,128)S(1)}, u32[]{:S(2)}, u32[]{:S(2)}) collective-permute-start(f32[324,128]{1,0:T(8,128)S(1)} %nest.1.own_ref), channel_id=1, source_target_pairs={{0,128},{128,0},{1,129},{129,1},{2,130},{130,2},{3,131},{131,3},{4... | collective-permute-start | bytes 497672 | tf_op jit(solution)/shard_map/ppermute | solution.py:708
  102.7 0.8 reshape.70
  103.5 0.3 collective-permute-done.2.other_ref
  103.8 0.7 stats.1
Async XLA Ops:
  2.2 20.9 %collective-permute-start = (bf16[992,128]{1,0:T(8,128)(2,1)S(1)}, bf16[992,128]{1,0:T(8,128)(2,1)S(1)}, u32[]{:S(2)}, u32[]{:S(2)}) collective-permute-start(bf16[992,128]{1,0:T(8,128)(2,1)S(1)} %get-tuple-element.29), channel_id=1, source_target_pairs={{1,2},{3,4},{5,6},{7,8},{9,10},{11,12},{13,14},{15,16},{17,18},{19... | collective-permute-start | bytes 761864 | tf_op jit(solution)/shard_map/ppermute | solution.py:614
  2.8 20.2 %collective-permute-start.1 = (bf16[992,128]{1,0:T(8,128)(2,1)S(1)}, bf16[992,128]{1,0:T(8,128)(2,1)S(1)}, u32[]{:S(2)}, u32[]{:S(2)}) collective-permute-start(bf16[992,128]{1,0:T(8,128)(2,1)S(1)} %get-tuple-element.30), channel_id=1, source_target_pairs={{0,1},{2,3},{4,5},{6,7},{8,9},{10,11},{12,13},{14,15},{16,17},{18,... | collective-permute-start | bytes 761864 | tf_op jit(solution)/shard_map/ppermute | solution.py:615
  8.7 26.2 %all-to-all-start = ((f32[128,4,128]{2,1,0:T(4,128)}), f32[128,4,128]{2,1,0:T(4,128)S(1)}, u32[]{:S(2)}, u32[]{:S(2)}) async-start(f32[128,4,128]{2,1,0:T(4,128)} %bitcast.4), calls=%async_computation | async-start | bytes 524288 | tf_op jit(solution)/shard_map/all_to_all | solution.py:560
  29.7 14.9 %copy-start.1 = (s32[4,128]{1,0:T(4,128)S(1)}, s32[4,128]{1,0:T(4,128)}, u32[]{:S(2)}) copy-start(s32[4,128]{1,0:T(4,128)} %bidx_hbm.1) | copy-start | bytes 6148
  36.6 21.3 %all-to-all-start.1 = ((bf16[384,4,128]{2,1,0:T(4,128)(2,1)}), bf16[384,4,128]{2,1,0:T(4,128)(2,1)S(1)}, u32[]{:S(2)}, u32[]{:S(2)}) async-start(bf16[384,4,128]{2,1,0:T(4,128)(2,1)} %bitcast.6), calls=%async_computation.1 | async-start | bytes 786432 | tf_op jit(solution)/shard_map/all_to_all | solution.py:560
  44.9 33.9 %copy-start = (bf16[2,256,384]{2,1,0:T(8,128)(2,1)S(1)}, bf16[2,256,384]{2,1,0:T(8,128)(2,1)}, u32[]{:S(2)}) copy-start(bf16[2,256,384]{2,1,0:T(8,128)(2,1)} %constant.9.clone.mix_ref) | copy-start | bytes 1179652
  59.0 19.8 %all-to-all-start.2 = ((bf16[384,2,128]{2,1,0:T(2,128)(2,1)}), bf16[384,2,128]{2,1,0:T(2,128)(2,1)S(1)}, u32[]{:S(2)}, u32[]{:S(2)}) async-start(bf16[384,2,128]{2,1,0:T(2,128)(2,1)} %bitcast.9), calls=%async_computation.2 | async-start | bytes 393216 | tf_op jit(solution)/shard_map/all_to_all | solution.py:560
  97.3 6.4 %collective-permute-start.2 = (f32[324,128]{1,0:T(8,128)S(1)}, f32[324,128]{1,0:T(8,128)S(1)}, u32[]{:S(2)}, u32[]{:S(2)}) collective-permute-start(f32[324,128]{1,0:T(8,128)S(1)} %nest.1.own_ref), channel_id=1, source_target_pairs={{0,128},{128,0},{1,129},{129,1},{2,130},{130,2},{3,131},{131,3},{4... | collective-permute-start | bytes 497672 | tf_op jit(solution)/shard_map/ppermute | solution.py:708
